TPU v7x, 32 devices: a whole 2x2x4 slice. The times are simulated.
32 devices in a mesh: dp: 8 (over z, x), seq: 4 (over y, core).
Axes of the slice: x: 2, y: 2, z: 4, core: 2. Of those that a mesh axis runs over, the one named last changes fastest.
Arguments:
- hidden: bfloat16 [16384, 2048], P(('dp', 'seq')), may hold values from -6 to 6
- grad_out: bfloat16 [16384, 2048], P(('dp', 'seq')), may hold values from -6 to 6
- doc_lengths: int32 [8, 4], P('dp'), may hold values from 1 to 1024, 2048 in all within a row
- resets: int32 [8, 4], P('dp'), may hold values 0 or 1
- width_index: int32 [8], P('dp'), may hold values from 0 to 3
- owner_counts: int32 [32], replicated, may hold values from 24 to 40, as said below
- w_in: float32 [2560, 8512], P(('dp', 'seq')), may hold values from -0.125 to 0.125
- m_in: float32 [2560, 8512], P(('dp', 'seq')), may hold values from -0.0029296875 to 0.0029296875
- v_in: float32 [2560, 8512], P(('dp', 'seq')), may hold values from 3.872789e-08 to 1.5491156e-07
- w_out: float32 [2560, 4096], P(('dp', 'seq')), may hold values from -0.125 to 0.125
- m_out: float32 [2560, 4096], P(('dp', 'seq')), may hold values from -0.0029296875 to 0.0029296875
- v_out: float32 [2560, 4096], P(('dp', 'seq')), may hold values from 3.872789e-08 to 1.5491156e-07
- small_params: float32 [28096], replicated, may hold values from -12 to 1.5, as said below
- small_m: float32 [28096], replicated
- small_v: float32 [28096], replicated, as said below
Outputs:
- output: bfloat16 [16384, 2048], P(('dp', 'seq'))
- input_grad: float32 [16384, 2048], P(('dp', 'seq'))
- w_in_new: float32 [2560, 8512], P(('dp', 'seq'))
- m_in_new: float32 [2560, 8512], P(('dp', 'seq'))
- v_in_new: float32 [2560, 8512], P(('dp', 'seq'))
- w_out_new: float32 [2560, 4096], P(('dp', 'seq'))
- m_out_new: float32 [2560, 4096], P(('dp', 'seq'))
- v_out_new: float32 [2560, 4096], P(('dp', 'seq'))
- small_new: float32 [28096], replicated
- small_m_new: float32 [28096], replicated
- small_v_new: float32 [28096], replicated
- w_in_grad: float32 [2560, 8512], P(('dp', 'seq'))
- w_out_grad: float32 [2560, 4096], P(('dp', 'seq'))
- small_grad: float32 [28096], replicated
- norm: float32 [1], replicated
Inputs may be any that keep to these rules, and one draw needn't show every extreme that they name: `doc_lengths`: each row lists the 4 documents of one sequence in order and sums to 2048. `resets`: the entry of a sequence's first document has no effect. `width_index`: a sequence of width index w uses the first 64 * (w + 1) // 4 heads. `owner_counts`: the counts sum to 1024; owners hold consecutive blocks in device order; the first block of device d lies between d * 32 and d * 32 + 40 - 1024 / 32. `small_params`: gains and skip gains are positive. `small_v`: every entry is positive.
All inputs are finite; a program needn't handle non-finite values. No bound on the sum of `resets` on one device may be relied on, other than what follows from the above.
Results may differ from a plain program's by a relative error of at most 0.0093.
Values may be sent and summed in bfloat16 or wider, within the bound.
No kernel may reach another device: no remote copies, remote signals or barrier semaphores. Data moves between devices by JAX's collectives and lax.ppermute only.
A program may use at most 400 MiB of HBM per device.

v0:
```python
from functools import partial

import jax
import jax.numpy as jnp
from jax import lax
from jax.sharding import PartitionSpec as P

D = 2048
E = 4096
H = 64
P_SIZE = 64
N = 128
K = 4
BLK = 256
RB = 2
CW = 4352


highest = lax.Precision.HIGHEST
norm_eps = 1e-05
adam_eps = 1e-08
weight_decay = 0.1
rate_matrix = 0.02
rate_vector = 0.15
bias_fix = 1.0 - 0.5**3


def shifted(block, axis, distance):
    devices = range(lax.axis_size(axis))
    route = [(i - distance, i) for i in devices if i - distance in devices]
    return lax.ppermute(block, axis, route)


def entering(value, axis, join, neutral, backward):
    count, mine = (lax.axis_size(axis), lax.axis_index(axis))
    pieces = jax.tree.map(lambda part: lax.all_gather(part, axis), value)
    if backward:
        pieces = jax.tree.map(lambda part: part[::-1], pieces)
        mine = count - 1 - mine
    running = jax.tree.map(
        lambda part, zero: jnp.full_like(part, 0) + jnp.asarray(zero, part.dtype), value, neutral
    )

    def turn(position, running):
        longer = join(running, jax.tree.map(lambda part: part[position], pieces))
        return jax.tree.map(lambda new, old: jnp.where(position < mine, new, old), longer, running)

    return lax.fori_loop(0, count - 1, turn, running)


def unpack(small):
    offset = 0
    pieces = []
    for length in (D, K * CW, CW, H, H, H, E):
        pieces.append(lax.slice_in_dim(small, offset, offset + length))
        offset = offset + length
    return (
        pieces[0],
        pieces[1].reshape(K, CW),
        pieces[2],
        pieces[3],
        pieces[4],
        pieces[5],
        pieces[6],
    )


def block_state(inputs, keys, steps, logs, resets):
    length = inputs.shape[0]
    totals = jnp.cumsum(logs, axis=0)
    segment = jnp.cumsum(resets)
    last_same = (segment == segment[-1]).astype(jnp.float32)
    tail = jnp.exp(totals[-1][None, :] - totals) * last_same[:, None] * steps
    weighted = (tail[:, :, None] * inputs).reshape(length, H * P_SIZE)
    fresh = jnp.dot(weighted.T, keys, precision=highest).reshape(H, P_SIZE, N)
    carry_on = jnp.exp(totals[-1]) * (segment[-1] == 0).astype(jnp.float32)
    return (carry_on, fresh)


def block_output(inputs, keys, queries, steps, logs, resets, state_in):
    length = inputs.shape[0]
    totals = jnp.cumsum(logs, axis=0)
    segment = jnp.cumsum(resets)
    order = jnp.arange(length)
    allowed = (segment[:, None] == segment[None, :]) & (order[:, None] >= order[None, :])
    center = 0.5 * totals[-1][None, :]
    rise = jnp.exp(totals - center)
    fall = jnp.exp(center - totals) * steps
    scores = jnp.where(allowed, jnp.dot(queries, keys.T, precision=highest), 0.0)
    weighted = (fall[:, :, None] * inputs).reshape(length, H * P_SIZE)
    result = (
        jnp.dot(scores, weighted, precision=highest).reshape(length, H, P_SIZE) * rise[:, :, None]
    )
    enter = jnp.exp(totals) * (segment == 0).astype(jnp.float32)[:, None]
    return result + enter[:, :, None] * jnp.einsum(
        "hpn,tn->thp", state_in, queries, precision=highest
    )


def split_blocks(array, count):
    return array.reshape((count, array.shape[0] // count) + array.shape[1:])


def local_transform(inputs, keys, steps, logs, resets):
    count = inputs.shape[0] // BLK

    def advance(carry, block):
        carry_on, fresh = block_state(*block)
        return ((carry[0] * carry_on, carry_on[:, None, None] * carry[1] + fresh), None)

    begin = (jnp.ones((H,), jnp.float32), jnp.zeros((H, P_SIZE, N), jnp.float32))
    blocks = tuple((split_blocks(array, count) for array in (inputs, keys, steps, logs, resets)))
    final, unused = lax.scan(jax.checkpoint(advance), begin, blocks)
    return final


def local_outputs(inputs, keys, queries, steps, logs, resets, state_in):
    count = inputs.shape[0] // BLK

    def advance(state, block):
        block_inputs, block_keys, block_queries, block_steps, block_logs, block_resets = block
        result = block_output(
            block_inputs, block_keys, block_queries, block_steps, block_logs, block_resets, state
        )
        carry_on, fresh = block_state(
            block_inputs, block_keys, block_steps, block_logs, block_resets
        )
        return (carry_on[:, None, None] * state + fresh, result)

    blocks = tuple(
        (split_blocks(array, count) for array in (inputs, keys, queries, steps, logs, resets))
    )
    final, results = lax.scan(jax.checkpoint(advance), state_in, blocks)
    return results.reshape(inputs.shape)


def combine(earlier, later):
    return (earlier[0] * later[0], later[0][:, None, None] * earlier[1] + later[1])


def reset_flags(lengths_row, flags_row, positions):
    starts = jnp.cumsum(lengths_row) - lengths_row
    later = jnp.arange(lengths_row.shape[0]) >= 1
    hits = (positions[:, None] == starts[None, :]) & (flags_row[None, :] == 1) & later[None, :]
    return jnp.any(hits, axis=1).astype(jnp.float32)


def width_mask(width):
    heads_on = H * (width + 1) // 4
    channel_mask = (jnp.arange(E) // P_SIZE < heads_on).astype(jnp.float32)
    return (channel_mask, (heads_on * P_SIZE).astype(jnp.float32))


def owner_tables(counts, slot):
    devices = counts.shape[0]
    ends = jnp.cumsum(counts)
    offsets = ends - counts
    within = jnp.arange(slot)
    source = offsets[:, None] * RB + within[None, :]
    alive = within[None, :] < counts[:, None] * RB
    source = jnp.where(alive, source, 0)
    rows = jnp.arange(D)
    blocks = rows // RB
    owner = jnp.sum((ends[None, :] <= blocks[:, None]).astype(jnp.int32), axis=1)
    match = jnp.arange(devices)[None, :] == owner[:, None]
    first_row = jnp.sum(jnp.where(match, offsets[None, :] * RB, 0), axis=1)
    place = owner * slot + rows - first_row
    return (source, alive, place)


def natural_order(gathered, place):
    return (jnp.take(gathered[0], place, axis=0), jnp.take(gathered[1], place, axis=0))


def owner_columns(values, order_source, order_alive):
    picked = jnp.take(values, order_source, axis=1)
    return jnp.where(order_alive[None, :], picked, jnp.zeros((), values.dtype))


def term_pair(normed_cols, grad_cols, grad_proj, mixed_low):
    part_in = jnp.einsum("tr,tc->rc", normed_cols, grad_proj, preferred_element_type=jnp.float32)
    part_out = jnp.einsum("tr,te->re", grad_cols, mixed_low, preferred_element_type=jnp.float32)
    return (part_in, part_out)


def adamw(weight, first, second, grad, rate, correction):
    first_new = 0.5 * first + 0.5 * grad
    second_new = 0.5 * second + 0.5 * grad * grad
    update = first_new / correction / (jnp.sqrt(second_new / correction) + adam_eps)
    return (weight - rate * (update + weight_decay * weight), first_new, second_new)


def norm_front(hidden_full, small):
    gain_in = unpack(small)[0]
    scale = lax.rsqrt(jnp.mean(hidden_full * hidden_full, axis=1, keepdims=True) + norm_eps)
    return hidden_full * scale * gain_in[None, :]


def mix_front(conv_in, dt_raw, rim, small):
    gain_in, conv_weight, conv_bias, dt_bias, decay_log, skip_gain, gain_out = unpack(small)
    length = conv_in.shape[0]
    padded = jnp.concatenate([rim, conv_in], axis=0)
    mixed = conv_bias[None, :] + sum(
        (conv_weight[tap][None, :] * padded[tap : tap + length] for tap in range(K))
    )
    steps = jax.nn.softplus(dt_raw + dt_bias[None, :])
    logs = -jnp.exp(decay_log)[None, :] * steps
    return (jax.nn.silu(mixed), steps, logs)


def mix_back(
    inputs, keys, queries, steps, logs, state_in, gate_raw, small, resets, channel_mask, active
):
    gain_in, conv_weight, conv_bias, dt_bias, decay_log, skip_gain, gain_out = unpack(small)
    length = inputs.shape[0]
    heads_in = inputs.reshape(length, H, P_SIZE)
    result = local_outputs(heads_in, keys, queries, steps, logs, resets, state_in)
    result = result + skip_gain[None, :, None] * heads_in
    gated = result.reshape(length, E) * jax.nn.silu(gate_raw) * channel_mask[None, :]
    square = jnp.sum(gated * gated, axis=1, keepdims=True) / active
    return gated * lax.rsqrt(square + norm_eps) * gain_out[None, :]


def local(
    hidden,
    grad_out,
    doc_lengths,
    resets,
    width_index,
    owner_counts,
    w_in,
    m_in,
    v_in,
    w_out,
    m_out,
    v_out,
    small_params,
    small_m,
    small_v,
):
    tokens = hidden.shape[0]
    slot = w_in.shape[0]
    width_in = w_in.shape[1]
    width_out = w_out.shape[1]
    seq_count = lax.axis_size("seq")
    data_count = lax.axis_size("dp")
    positions = lax.axis_index("seq") * tokens + jnp.arange(tokens)
    flags = reset_flags(doc_lengths[0], resets[0], positions)
    channel_mask, active = width_mask(width_index[0])
    source, alive, place = owner_tables(owner_counts, slot)
    hidden_full = hidden.astype(jnp.float32)
    normed, norm_pull = jax.vjp(norm_front, hidden_full, small_params)
    normed_low = normed.astype(jnp.bfloat16)
    in_low = w_in.astype(jnp.bfloat16)
    out_low = w_out.astype(jnp.bfloat16)
    in_rows, out_rows = natural_order(
        (
            lax.all_gather(in_low, ("dp", "seq"), axis=0, tiled=True),
            lax.all_gather(out_low, ("dp", "seq"), axis=0, tiled=True),
        ),
        place,
    )
    projected = jnp.dot(normed_low, in_rows, preferred_element_type=jnp.float32).astype(
        jnp.bfloat16
    )
    gate_raw = projected[:, :E].astype(jnp.float32)
    conv_in = projected[:, E : E + CW]
    dt_raw = projected[:, E + CW :].astype(jnp.float32)
    rim = shifted(conv_in[tokens - (K - 1) :], "seq", 1)
    front, front_pull = jax.vjp(
        mix_front, conv_in.astype(jnp.float32), dt_raw, rim.astype(jnp.float32), small_params
    )
    activated, steps, logs = front
    rounded = lax.optimization_barrier(activated.astype(jnp.bfloat16)).astype(jnp.float32)
    inputs = rounded[:, :E] * channel_mask[None, :]
    keys = rounded[:, E : E + N]
    queries = rounded[:, E + N :]
    transform, state_pull = jax.vjp(
        partial(local_transform, resets=flags), inputs.reshape(tokens, H, P_SIZE), keys, steps, logs
    )
    carry_on, fresh = transform
    neutral = (jnp.ones((H,), jnp.float32), jnp.zeros((H, P_SIZE, N), jnp.float32))
    entered = entering((carry_on, fresh), "seq", combine, neutral, False)[1]
    back_mix = partial(mix_back, resets=flags, channel_mask=channel_mask, active=active)
    mixed, back_pull = jax.vjp(
        back_mix, inputs, keys, queries, steps, logs, entered, gate_raw, small_params
    )
    mixed_low = mixed.astype(jnp.bfloat16)
    branch = jnp.einsum("te,de->td", mixed_low, out_rows, preferred_element_type=jnp.float32)
    output = (hidden_full + branch).astype(jnp.bfloat16)
    in_back, out_back = natural_order(
        (
            lax.all_gather(in_low, ("dp", "seq"), axis=0, tiled=True),
            lax.all_gather(out_low, ("dp", "seq"), axis=0, tiled=True),
        ),
        place,
    )
    mixed_grad = jnp.dot(grad_out, out_back, preferred_element_type=jnp.float32)
    grads_back = back_pull(mixed_grad)
    (
        grad_inputs,
        grad_keys,
        grad_queries,
        grad_steps,
        grad_logs,
        grad_entered,
        grad_gate,
        small_back,
    ) = grads_back
    carried = entering((carry_on, grad_entered), "seq", combine, neutral, True)[1]
    grad_carry = jnp.sum(carried * entered, axis=(1, 2))
    heads_back, keys_back, steps_back, logs_back = state_pull((grad_carry, carried))
    grad_front = jnp.concatenate(
        [
            (grad_inputs + heads_back.reshape(tokens, E)) * channel_mask[None, :],
            grad_keys + keys_back,
            grad_queries,
        ],
        axis=1,
    )
    grad_conv, grad_dt, grad_rim, small_front = front_pull(
        (grad_front, grad_steps + steps_back, grad_logs + logs_back)
    )
    pushed = shifted(grad_rim, "seq", -1)
    grad_conv = jnp.concatenate(
        [grad_conv[: tokens - (K - 1)], grad_conv[tokens - (K - 1) :] + pushed], axis=0
    )
    grad_proj = jnp.concatenate([grad_gate, grad_conv, grad_dt], axis=1).astype(jnp.bfloat16)
    grad_normed = jnp.einsum("tc,dc->td", grad_proj, in_back, preferred_element_type=jnp.float32)
    hidden_back, small_norm = norm_pull(grad_normed)
    input_grad = grad_out.astype(jnp.float32) + hidden_back
    order_source = source.reshape(data_count, seq_count, slot).transpose(1, 0, 2).reshape(-1)
    order_alive = alive.reshape(data_count, seq_count, slot).transpose(1, 0, 2).reshape(-1)
    part_in, part_out = term_pair(
        owner_columns(normed_low, order_source, order_alive),
        owner_columns(grad_out, order_source, order_alive),
        grad_proj,
        mixed_low,
    )
    got_in, got_out = (
        lax.all_to_all(
            part_in.reshape(seq_count, data_count * slot, width_in),
            "seq",
            split_axis=0,
            concat_axis=0,
            tiled=True,
        ),
        lax.all_to_all(
            part_out.reshape(seq_count, data_count * slot, width_out),
            "seq",
            split_axis=0,
            concat_axis=0,
            tiled=True,
        ),
    )
    fin_in, fin_out = (
        lax.all_to_all(
            jnp.sum(got_in, axis=0).reshape(data_count, slot, width_in),
            "dp",
            split_axis=0,
            concat_axis=0,
            tiled=True,
        ),
        lax.all_to_all(
            jnp.sum(got_out, axis=0).reshape(data_count, slot, width_out),
            "dp",
            split_axis=0,
            concat_axis=0,
            tiled=True,
        ),
    )
    owned_in = jnp.sum(fin_in, axis=0)
    owned_out = jnp.sum(fin_out, axis=0)
    small_grad = small_back + small_front + small_norm
    big_square = jnp.sum(owned_in * owned_in) + jnp.sum(owned_out * owned_out)
    small_total, square_total = lax.psum((small_grad, big_square), ("dp", "seq"))
    norm = jnp.sqrt(square_total + jnp.sum(small_total * small_total))
    clip = 1.0 / jnp.maximum(norm, 1.0)
    correction = jnp.float32(bias_fix)
    w_in_new, m_in_new, v_in_new = adamw(w_in, m_in, v_in, owned_in * clip, rate_matrix, correction)
    w_out_new, m_out_new, v_out_new = adamw(
        w_out, m_out, v_out, owned_out * clip, rate_matrix, correction
    )
    small_new, small_m_new, small_v_new = adamw(
        small_params, small_m, small_v, small_total * clip, rate_vector, correction
    )
    return (
        output,
        input_grad,
        w_in_new,
        m_in_new,
        v_in_new,
        w_out_new,
        m_out_new,
        v_out_new,
        small_new,
        small_m_new,
        small_v_new,
        owned_in,
        owned_out,
        small_total,
        norm.reshape(1),
    )


def solution(mesh):
    in_specs = (
        P(("dp", "seq"), None),
        P(("dp", "seq"), None),
        P("dp", None),
        P("dp", None),
        P("dp"),
        P(),
        P(("dp", "seq"), None),
        P(("dp", "seq"), None),
        P(("dp", "seq"), None),
        P(("dp", "seq"), None),
        P(("dp", "seq"), None),
        P(("dp", "seq"), None),
        P(),
        P(),
        P(),
    )
    out_specs = (
        P(("dp", "seq"), None),
        P(("dp", "seq"), None),
        P(("dp", "seq"), None),
        P(("dp", "seq"), None),
        P(("dp", "seq"), None),
        P(("dp", "seq"), None),
        P(("dp", "seq"), None),
        P(("dp", "seq"), None),
        P(),
        P(),
        P(),
        P(("dp", "seq"), None),
        P(("dp", "seq"), None),
        P(),
        P(),
    )
    return jax.shard_map(local, mesh=mesh, in_specs=in_specs, out_specs=out_specs, check_vma=False)
```

profile of v0, /device:TPU:0, one launch (start us, length us, event | category | flops | bytes accessed | tf_op | source)
XLA Modules:
  0.0 3331.8 jit_solution(4697044882503385446)
XLA Ops:
  17.3 240.9 %all-gather.8.cloned.1.call-done = bf16[2560,8512]{1,0:T(8,128)(2,1)} async-done(((bf16[80,8512]{1,0:T(8,128)(2,1)}), bf16[2560,8512]{1,0:T(8,128)(2,1)}) %all-gather.8.cloned.1.call-update) | async-done | bytes 43581456 | tf_op jit(solution)/shard_map/all_gather | solution.py:258
  258.1 112.1 %gather_fusion = bf16[2048,8512]{1,0:T(8,128)(2,1)} fusion(bf16[2560,8512]{1,0:T(8,128)(2,1)} %all-gather.8.cloned.1.call-done, s32[2048]{0:T(1024)S(1)} %broadcast_clamp_fusion), kind=kCustom, calls=%fused_computation.clone | custom fusion | bytes 69738496 | tf_op jit(solution)/shard_map/jit(_take)/gather | solution.py:172
  370.2 26.5 fusion.92
  409.7 16.5 multiply_convert_fusion
  436.8 14.2 reshape.1090
  451.0 14.1 copy.475
  468.9 29.3 while.112
  503.0 41.0 %gather_fusion.1 = bf16[2048,4096]{1,0:T(8,128)(2,1)} fusion(bf16[2560,4096]{1,0:T(8,128)(2,1)} %all-gather.10.cloned.1.call-done, s32[2048]{0:T(1024)S(1)} %broadcast_clamp_fusion), kind=kCustom, calls=%fused_computation.1.clone | custom fusion | bytes 33562624 | tf_op jit(solution)/shard_map/jit(_take)/gather | solution.py:172
  544.2 7.2 all-reduce.20
  556.2 6.3 while.113
  572.4 44.6 %while.111 = (s32[]{:T(128)}, f32[64,64,128]{2,1,0:T(8,128)S(1)}, f32[2,256,64,64]{1,3,2,0:T(8,128)}, f32[2,64,64,128]{3,2,1,0:T(8,128)}, f32[2,256,64]{1,2,0:T(...) while((s32[]{:T(128)}, f32[64,64,128]{2,1,0:T(8,128)S(1)}, ...), condition=%wide.region_19.21_spmd.clone, body=%wide.region_14.20_spmd.clone.sunk | while | flops 6551930368 | bytes 113268552 | solution.py:133
  617.0 16.3 copy.507
  633.3 14.8 reshape.1086
  648.1 11.6 multiply_reduce_fusion.15
  659.7 17.7 fusion.104
  677.5 16.9 multiply_reduce_fusion.13
  694.4 14.2 reshape.1087
  708.6 14.2 copy.486
  730.0 203.3 %while.114 = (s32[]{:T(128)}, f32[64,64,128]{2,1,0:T(8,128)}, f32[2,256,64,64]{1,3,2,0:T(8,128)}, f32[2,256,128]{2,1,0:T(8,128)}, f32[2,256,128]{2,1,0:T(8,128)}...) while((s32[]{:T(128)}, f32[64,64,128]{2,1,0:T(8,128)}, ...), condition=%wide.region_39.42_spmd.clone, body=%wide.region_22.41_spmd.clone.sunk | while | flops 18047713280 | bytes 225222176 | solution.py:133
  774.1 6.9 multiply_reduce_fusion.33
  783.9 9.3 fusion.303
  797.3 7.2 bitcast_dynamic-update-slice_fusion.17
  804.6 6.7 fusion.300
  811.3 7.1 fusion.301
  873.5 6.9 multiply_reduce_fusion.33
  883.3 9.3 fusion.303
  896.5 7.1 bitcast_dynamic-update-slice_fusion.17
  903.6 6.7 fusion.300
  910.4 7.1 fusion.301
  937.5 8.2 gather_fusion.3
  945.7 23.5 fusion.117
  969.3 11.5 all-to-all-start.2
  983.3 10.2 gather_fusion.2
  998.3 16.3 copy.510
  1014.6 14.7 reshape.1088
  1029.3 8.3 rev.7
  1037.6 6.3 while.115
  1050.5 76.1 %while.110 = (s32[]{:T(128)}, f32[64]{0:T(128)S(1)}, f32[64,64,128]{2,1,0:T(8,128)S(1)}, f32[2,256,64,64]{1,3,2,0:T(8,128)}, f32[2,256,128]{2,1,0:T(8,128)S(1)},...) while((s32[]{:T(128)}, f32[64]{0:T(128)S(1)}, ...), condition=%wide.region_53.56_spmd, body=%wide.region_43.55_spmd.sunk | while | flops 3231450368 | bytes 71530168 | solution.py:113
  1064.5 7.0 multiply_reduce_fusion.29
  1071.8 6.7 fusion.259
  1102.2 7.1 multiply_reduce_fusion.29
  1109.5 6.7 fusion.259
  1126.9 16.3 copy.511
  1143.2 14.8 reshape.1089
  1158.1 13.9 add_multiply_fusion
  1174.4 15.1 multiply_reduce_fusion.11
  1189.5 11.4 broadcast_multiply_fusion.1
  1203.4 12.5 pad_add_fusion.2
  1224.8 37.6 %fusion.118 = f32[2560,8512]{0,1:T(8,128)} fusion(bf16[512,64]{1,0:T(8,128)(2,1)S(1)} %get-tuple-element.1714, bf16[3,4352]{1,0:T(4,128)(2,1)S(1)} %fusion.136, bf16[509,4352]{1,0:T(8,128)(2,1)} %slice.446, bf16[512,4096]{1,0:T(8,128)(2,1)} %get-tuple-element.1748, bf16[512,2560]{0,1:T(8,128)(2,1)} %bitcast_select_fusion.7), kind=kOutput, calls=%fused_computation.274 | convolution fusion | flops 22348562432 | bytes 98500608 | tf_op jit(solution)/shard_map/tr,tc->rc/dot_general | solution.py:181
  1262.4 57.0 %copy.597 = f32[1064,4,8,640]{3,2,0,1:T(8,128)} copy(f32[1064,4,8,640]{3,2,1,0:T(8,128)} %bitcast.161) | data formatting | bytes 174325760 | tf_op jit(solution)/shard_map/reshape | solution.py:342
  1319.4 120.1 %all-to-all-done.2 = f32[4,640,4096]{2,1,0:T(8,128)} async-done(((f32[4,640,4096]{2,1,0:T(8,128)}), f32[4,640,4096]{2,1,0:T(8,128)}, u32[]{:S(2)}, u32[]{:S(2)}) %all-to-all-start.2) | async-done | bytes 41943072 | tf_op jit(solution)/shard_map/all_to_all | solution.py:348
  1439.5 97.4 %all-to-all-start = ((f32[4,640,8512]{1,2,0:T(8,128)}), f32[4,640,8512]{1,2,0:T(8,128)}, u32[]{:S(2)}, u32[]{:S(2)}) async-start(f32[4,640,8512]{1,2,0:T(8,128)} %bitcast.412), calls=%async_computation | async-start | bytes 174325760 | tf_op jit(solution)/shard_map/all_to_all | solution.py:341
  1536.8 19.2 reduce_sum.486
  1556.0 918.1 %all-to-all-done = f32[4,640,8512]{1,2,0:T(8,128)} async-done(((f32[4,640,8512]{1,2,0:T(8,128)}), f32[4,640,8512]{1,2,0:T(8,128)}, u32[]{:S(2)}, u32[]{:S(2)}) %all-to-all-start) | async-done | bytes 87162912 | tf_op jit(solution)/shard_map/all_to_all | solution.py:341
  2479.6 35.3 %reduce_sum.483 = f32[640,8512]{0,1:T(8,128)} reduce(f32[4,640,8512]{1,2,0:T(8,128)} %all-to-all-done, f32[]{:T(128)} %constant.367.clone.1), dimensions={0}, to_apply=%region_55.59 | reduce | flops 16343040 | bytes 108953600 | tf_op jit(solution)/shard_map/reduce_sum | solution.py:358
  2514.9 23.1 copy.503
  2537.9 168.1 %all-to-all-done.3 = f32[8,80,4096]{2,1,0:T(8,128)} async-done(((f32[8,80,4096]{2,1,0:T(8,128)}), f32[8,80,4096]{2,1,0:T(8,128)}, u32[]{:S(2)}, u32[]{:S(2)}) %all-to-all-start.3) | async-done | bytes 10485792 | tf_op jit(solution)/shard_map/all_to_all | solution.py:364
  2712.8 16.5 fusion.113
  2729.6 10.2 pad_maximum_fusion.4.clone.5
  2739.9 27.5 fusion.110
  2780.2 404.7 %all-to-all-done.1 = f32[8,80,8512]{2,1,0:T(8,128)} async-done(((f32[8,80,8512]{2,1,0:T(8,128)}), f32[8,80,8512]{2,1,0:T(8,128)}, u32[]{:S(2)}, u32[]{:S(2)}) %all-to-all-start.1) | async-done | bytes 21790752 | tf_op jit(solution)/shard_map/all_to_all | solution.py:357
  3184.9 8.2 reduce_sum.484
  3195.9 71.0 %all-reduce.23.cloned.1.call-done = f32[28096]{0:T(1024)} async-done(((f32[28096]{0:T(1024)}), f32[28096]{0:T(1024)}) %all-reduce.23.cloned.1.call-update) | async-done | bytes 112400 | tf_op jit(solution)/shard_map/psum | solution.py:376
  3268.4 41.2 %psum.14 = f32[]{:T(128)} all-reduce(f32[]{:T(128)S(6)} %add.402), channel_id=1, replica_groups=mesh['dp'=8,'seq'=4] {'dp','seq'}, use_global_device_ids=true, to_apply=%region_61.65 | all-reduce | flops 1 | bytes 8 | tf_op jit(solution)/shard_map/psum | solution.py:376
  (703 shorter events, 385.4 us)
Async XLA Ops:
  7.2 250.9 %all-gather.8.cloned.1.call-start = ((), (), s32[]{:S(2)}) async-start(), calls=%async_computation.4 | async-start | bytes 45281280 | tf_op jit(solution)/shard_map/all_gather | solution.py:258
  10.5 492.5 %all-gather.10.cloned.1.call-start = ((), (), s32[]{:S(2)}) async-start(), calls=%async_computation.5 | async-start | bytes 21626880 | tf_op jit(solution)/shard_map/all_gather | solution.py:259
  11.5 544.7 %all-gather.12.cloned.1.call-start = ((), (), s32[]{:S(2)}) async-start(), calls=%async_computation.7 | async-start | bytes 10485760 | tf_op jit(solution)/shard_map/all_gather | solution.py:36
  13.1 357.0 %copy-start.68 = (f32[2048]{0:T(1024)}, f32[2048]{0:T(1024)S(1)}, u32[]{:S(2)}) copy-start(f32[2048]{0:T(1024)S(1)} %slice.304) | copy-start | bytes 24580
  13.4 415.5 %copy-start.44 = (f32[4096]{0:T(1024)}, f32[4096]{0:T(1024)S(1)}, u32[]{:S(2)}) copy-start(f32[4096]{0:T(1024)S(1)} %fusion.141) | copy-start | bytes 49156
  14.7 355.5 %copy-start.78 = (f32[512]{0:T(512)}, f32[512]{0:T(512)S(1)}, u32[]{:S(2)}) copy-start(f32[512]{0:T(512)S(1)} %fusion.145) | copy-start | bytes 6148
  15.3 390.7 %copy-start.91 = (f32[64]{0:T(128)}, f32[64]{0:T(128)S(1)}, u32[]{:S(2)}) copy-start(f32[64]{0:T(128)S(1)} %get-tuple-element.1759) | copy-start | bytes 772
  15.3 390.7 %copy-start.93 = (f32[64]{0:T(128)}, f32[64]{0:T(128)S(1)}, u32[]{:S(2)}) copy-start(f32[64]{0:T(128)S(1)} %get-tuple-element.1760) | copy-start | bytes 772
  15.3 354.9 %copy-start.98 = (pred[2048]{0:T(1024)(128)(4,1)}, pred[2048]{0:T(1024)(128)(4,1)S(1)}, u32[]{:S(2)}) copy-start(pred[2048]{0:T(1024)(128)(4,1)S(1)} %compare_and_fusion.1) | copy-start | bytes 6148
  15.4 394.3 %copy-start.50 = (f32[4352]{0:T(1024)}, f32[4352]{0:T(1024)S(1)}, u32[]{:S(2)}) copy-start(f32[4352]{0:T(1024)S(1)} %get-tuple-element.1762) | copy-start | bytes 52228
  15.4 394.3 %copy-start.52 = (f32[4352]{0:T(1024)}, f32[4352]{0:T(1024)S(1)}, u32[]{:S(2)}) copy-start(f32[4352]{0:T(1024)S(1)} %get-tuple-element.1763) | copy-start | bytes 52228
  15.4 394.3 %copy-start.54 = (f32[4352]{0:T(1024)}, f32[4352]{0:T(1024)S(1)}, u32[]{:S(2)}) copy-start(f32[4352]{0:T(1024)S(1)} %get-tuple-element.1764) | copy-start | bytes 52228
  15.4 394.3 %copy-start.56 = (f32[4352]{0:T(1024)}, f32[4352]{0:T(1024)S(1)}, u32[]{:S(2)}) copy-start(f32[4352]{0:T(1024)S(1)} %get-tuple-element.1765) | copy-start | bytes 52228
  17.3 352.9 %copy-start.24 = (bf16[512,2048]{1,0:T(8,128)(2,1)S(1)}, bf16[512,2048]{1,0:T(8,128)(2,1)}, u32[]{:S(2)}) copy-start(bf16[512,2048]{1,0:T(8,128)(2,1)} %fusion.109) | copy-start | bytes 6291460
  397.7 12.0 collective-permute-start
  409.7 16.5 copy-start.37
  468.9 32.1 copy-start.97
  468.9 32.8 copy-start.106
  499.5 529.8 %all-gather.14.cloned.1.call-start = ((), (), s32[]{:S(2)}) async-start(), calls=%async_computation.8 | async-start | bytes 10485760 | tf_op jit(solution)/shard_map/all_gather | solution.py:36
  617.0 16.3 copy-start.22
  633.3 14.8 copy-start.45
  633.3 14.8 copy-start.47
  659.7 17.8 copy-start.86
  659.7 17.8 slice-start
  659.7 17.8 slice-start.1
  659.7 17.8 slice-start.2
  969.3 470.2 %all-to-all-start.2 = ((f32[4,640,4096]{2,1,0:T(8,128)}), f32[4,640,4096]{2,1,0:T(8,128)}, u32[]{:S(2)}, u32[]{:S(2)}) async-start(f32[4,640,4096]{2,1,0:T(8,128)} %bitcast.675), calls=%async_computation.2 | async-start | bytes 83886080 | tf_op jit(solution)/shard_map/all_to_all | solution.py:348
  1050.5 76.1 %copy-start.41 = (f32[2,256,64]{1,2,0:T(8,128)S(1)}, f32[2,256,64]{1,2,0:T(8,128)}, u32[]{:S(2)}) copy-start(f32[2,256,64]{1,2,0:T(8,128)} %get-tuple-element.966) | copy-start | bytes 393220
  1050.9 13.6 copy-start.74
  1088.7 13.5 copy-start.74
  1143.2 14.8 copy-start.34
  1143.2 14.8 copy-start.46
  1143.2 14.9 copy-start.48
  1158.0 14.0 slice-start.3
  1158.0 14.0 slice-start.6
  1158.0 14.6 slice-start.4
  1158.0 14.9 slice-start.5
  1158.0 16.2 slice-start.7
  1158.1 16.2 slice-start.8
  1158.1 16.3 copy-start.31
  1158.1 16.2 copy-start.38
  1174.3 15.1 copy-start.51
  1174.3 15.1 copy-start.53
  1174.3 15.1 copy-start.55
  1174.3 15.1 copy-start.57
  1202.0 21.2 collective-permute-start.1
  1224.8 37.6 %copy-start.58 = (bf16[3,4352]{1,0:T(4,128)(2,1)}, bf16[3,4352]{1,0:T(4,128)(2,1)S(1)}, u32[]{:S(2)}) copy-start(bf16[3,4352]{1,0:T(4,128)(2,1)S(1)} %fusion.136) | copy-start | bytes 78340
  1439.5 1034.6 %all-to-all-start = ((f32[4,640,8512]{1,2,0:T(8,128)}), f32[4,640,8512]{1,2,0:T(8,128)}, u32[]{:S(2)}, u32[]{:S(2)}) async-start(f32[4,640,8512]{1,2,0:T(8,128)} %bitcast.412), calls=%async_computation | async-start | bytes 174325760 | tf_op jit(solution)/shard_map/all_to_all | solution.py:341
  2474.1 232.0 %all-to-all-start.3 = ((f32[8,80,4096]{2,1,0:T(8,128)}), f32[8,80,4096]{2,1,0:T(8,128)}, u32[]{:S(2)}, u32[]{:S(2)}) async-start(f32[8,80,4096]{2,1,0:T(8,128)} %bitcast.676), calls=%async_computation.3 | async-start | bytes 20971520 | tf_op jit(solution)/shard_map/all_to_all | solution.py:364
  2706.1 478.8 %all-to-all-start.1 = ((f32[8,80,8512]{2,1,0:T(8,128)}), f32[8,80,8512]{2,1,0:T(8,128)}, u32[]{:S(2)}, u32[]{:S(2)}) async-start(f32[8,80,8512]{2,1,0:T(8,128)} %bitcast.671), calls=%async_computation.1 | async-start | bytes 43909120 | tf_op jit(solution)/shard_map/all_to_all | solution.py:357
  2712.4 554.5 %all-reduce.23.cloned.1.call-start = ((), (), s32[]{:S(2)}) async-start(), calls=%async_computation.6 | async-start | bytes 229376 | tf_op jit(solution)/shard_map/psum | solution.py:376
  2712.7 16.6 copy-start.67
  2712.7 16.6 copy-start.66
  2712.7 16.7 copy-start.65
  2712.7 16.7 copy-start.64
  2712.7 16.8 copy-start.43
  2712.7 16.8 copy-start.103
  2712.8 16.9 copy-start.40
  2712.8 16.9 copy-start.59
  2739.9 27.5 copy-start.63
  2739.9 27.5 copy-start.82
  2739.9 27.5 copy-start.96
  2739.9 28.3 copy-start.81
  3193.1 123.2 %copy-start.13 = (f32[80,8512]{1,0:T(8,128)}, f32[80,8512]{1,0:T(8,128)S(1)}, u32[]{:S(2)}) copy-start(f32[80,8512]{1,0:T(8,128)S(1)} %reduce_sum.484) | copy-start | bytes 8171524
  (89 other events, 495.5 us)
Sparse Core Ops, SparseCore 0:
  11.5 246.5 all-gather.7
  261.5 131.9 all-gather.9
  499.6 56.5 all-gather.11
  933.4 64.3 all-gather.13
  2768.3 498.5 all-reduce.22
where the time goes:
time: 3350 us; the launch traced here: 3330 us
  waiting for transfers between devices  1930 us (58%)
  local copies, waits for them, and re-layouts  549 us (16%)
  other arithmetic  330 us (10%)
  matrix products  318 us (9%)
  starting transfers between devices  124 us (4%)
  blocking collectives  48.4 us (1%)
    all_to_all x1, waiting for transfers between devices, local(): lax.all_to_all(part_in.reshape(seq_count, data_count * slot, width_in), '...  918 us
    all_to_all x1, waiting for transfers between devices, local(): lax.all_to_all(jnp.sum(got_in, axis=0).reshape(data_count, slot, width_in...  405 us
    all_gather x1, waiting for transfers between devices, local(): lax.all_gather(in_low, ('dp', 'seq'), axis=0, tiled=True)  241 us
    all_to_all x1, waiting for transfers between devices, local(): lax.all_to_all(jnp.sum(got_out, axis=0).reshape(data_count, slot, width_o...  168 us
    all_to_all x1, waiting for transfers between devices, local(): lax.all_to_all(part_out.reshape(seq_count, data_count * slot, width_out),...  120 us
    gather x1, local copies, waits for them, and re-layouts, natural_order(): jnp.take(gathered[0], place, axis=0)  112 us
    all_to_all x1, starting transfers between devices, local(): lax.all_to_all(part_in.reshape(seq_count, data_count * slot, width_in), '...  97.4 us
    psum x1, waiting for transfers between devices, local(): lax.psum((small_grad, big_square), ('dp', 'seq'))  71 us
  transfers between devices with their start and end apart: 11, of which 7 were waited for; matrix products, arithmetic and copies ran while one was open for 24% of the time, Pallas kernels for 0%

commit v1 on v0

v1 whole, which is shorter than its diff:
```python
import jax
import jax.numpy as jnp
from jax import lax
from jax.experimental import pallas as pl
from jax.experimental.pallas import tpu as pltpu
from jax.sharding import PartitionSpec as P

D = 2048
E = 4096
H = 64
P_SIZE = 64
N = 128
K = 4
RB = 2
CW = 4352
PAIRS = E // 128

f32 = jnp.float32
bf16 = jnp.bfloat16
norm_eps = 1e-05
adam_eps = 1e-08
weight_decay = 0.1
rate_matrix = 0.02
rate_vector = 0.15
bias_fix = 1.0 - 0.5**3
OWNERS = ("dp", "seq")


def unpack(small):
    offset = 0
    pieces = []
    for length in (D, K * CW, CW, H, H, H, E):
        pieces.append(lax.slice_in_dim(small, offset, offset + length))
        offset = offset + length
    pieces[1] = pieces[1].reshape(K, CW)
    return pieces


def reset_flags(lengths_row, flags_row, positions):
    starts = jnp.cumsum(lengths_row) - lengths_row
    later = jnp.arange(lengths_row.shape[0]) >= 1
    hits = (positions[:, None] == starts[None, :]) & (flags_row[None, :] == 1) & later[None, :]
    return jnp.any(hits, axis=1).astype(f32)


def width_mask(width):
    heads_on = H * (width + 1) // 4
    channel_mask = (jnp.arange(E) // P_SIZE < heads_on).astype(f32)
    return (channel_mask, (heads_on * P_SIZE).astype(f32))


def adamw(weight, first, second, grad, rate, correction):
    first_new = 0.5 * first + 0.5 * grad
    second_new = 0.5 * second + 0.5 * grad * grad
    update = first_new / correction / (jnp.sqrt(second_new / correction) + adam_eps)
    return (weight - rate * (update + weight_decay * weight), first_new, second_new)


def even_rows(weights, count, lead, base):
    halo = weights.shape[0] - base
    devices = lax.axis_size("dp") * lax.axis_size("seq")
    last = lax.dynamic_slice_in_dim(weights, count - halo, halo, 0).astype(bf16)
    before = lax.ppermute(last, OWNERS, [(i, i + 1) for i in range(devices - 1)])
    joined = jnp.concatenate([before.astype(f32), weights], axis=0)
    return lax.dynamic_slice_in_dim(joined, halo - lead, base, 0).astype(bf16)


def owned_rows(block, count, lead, slot):
    halo = slot - block.shape[0]
    devices = lax.axis_size("dp") * lax.axis_size("seq")
    after = lax.ppermute(block[:halo], OWNERS, [(i + 1, i) for i in range(devices - 1)])
    joined = jnp.concatenate([block, after, jnp.zeros_like(after)], axis=0).astype(f32)
    picked = lax.dynamic_slice_in_dim(joined, lead, slot, 0)
    return jnp.where(jnp.arange(slot)[:, None] < count, picked, 0.0)


def exchange(value, bit, devices):
    return lax.ppermute(value, OWNERS, [(i, i ^ (1 << bit)) for i in range(devices)])


def sum_all(value, devices):
    for bit in range(devices.bit_length() - 1):
        value = value + exchange(value, bit, devices)
    return value


def split_rows(left, mine, base):
    order = jnp.arange(D)
    within = order % (D // 2)
    lowest = jnp.where(order < D // 2, 1 - mine % 2, mine % 2)
    source = (2 * (within // base) + lowest) * base + within % base
    pick = (jnp.arange(D)[:, None] == source[None, :]).astype(bf16)
    return jnp.dot(left, pick, preferred_element_type=f32).astype(bf16)


def orders_of(devices, gather):
    rest = list(range(3, devices.bit_length() - 1))
    orders = [[1, 2] + rest, [2, 1] + rest, rest[:2] + [1, 2] + rest[2:]]
    return [order[::-1] for order in orders] if gather else orders


class Reduce:
    def __init__(self, left, right, mine, base, devices, cuts):
        bits = devices.bit_length() - 1
        self.mine, self.devices, self.step = mine, devices, 0
        self.orders = orders_of(devices, False)
        self.axes = [list(range(bits - 1, 0, -1)) for _ in self.orders]
        pieces = [right[:, begin:end] for begin, end in zip((0,) + cuts, cuts + (right.shape[1],))]

        def product(features, piece):
            return lax.dot_general(features, piece, (((0,), (0,)), ((), ())), preferred_element_type=f32)

        sent = [exchange(product(left[:, : D // 2], piece).astype(bf16), 0, devices) for piece in pieces]
        self.values = [
            (product(left[:, D // 2 :], piece) + got.astype(f32))
            .astype(bf16)
            .reshape([2] * (bits - 1) + [base, piece.shape[1]])
            for piece, got in zip(pieces, sent)
        ]

    def advance(self):
        for piece, (order, axes) in enumerate(zip(self.orders, self.axes)):
            bit, value = order[self.step], self.values[piece]
            axis, own = axes.index(bit), (self.mine >> bit) & 1
            sent = lax.dynamic_index_in_dim(value, 1 - own, axis, keepdims=False).astype(bf16)
            kept = lax.dynamic_index_in_dim(value, own, axis, keepdims=False).astype(f32)
            value = kept + exchange(sent, bit, self.devices).astype(f32)
            self.values[piece] = value.astype(bf16) if self.step == 0 else value
            axes.remove(bit)
        self.step += 1

    def result(self):
        while self.step < len(self.orders[0]):
            self.advance()
        return jnp.concatenate(self.values, axis=1)


class Gather:
    def __init__(self, block, mine, devices, cuts):
        base, columns = block.shape
        half = columns // 2
        low = mine % 2
        other = lax.dynamic_slice_in_dim(block, (1 - low) * half, half, 1)
        own = lax.dynamic_slice_in_dim(block, low * half, half, 1)
        got = exchange(other, 0, devices)
        both = jnp.concatenate([jnp.where(low == 0, own, got), jnp.where(low == 0, got, own)], axis=0)
        self.mine, self.devices, self.step = mine, devices, 0
        self.orders = orders_of(devices, True)
        self.bits = [[] for _ in self.orders]
        self.values = [both[:, begin:end] for begin, end in zip((0,) + cuts, cuts + (half,))]

    def advance(self):
        for piece, (order, bits) in enumerate(zip(self.orders, self.bits)):
            bit, value = order[self.step], self.values[piece]
            own = (self.mine >> bit) & 1
            got = exchange(value, bit, self.devices)
            bits.append(bit)
            bits.sort(reverse=True)
            axis = bits.index(bit)
            self.values[piece] = jnp.stack(
                [jnp.where(own == 0, value, got), jnp.where(own == 0, got, value)], axis=axis
            )
        self.step += 1

    def result(self):
        while self.step < len(self.orders[0]):
            self.advance()
        return jnp.concatenate([value.reshape(D, value.shape[-1]) for value in self.values], axis=1)


def tie(value, *works):
    value, states = lax.optimization_barrier((value, [work.values for work in works]))
    for work, state in zip(works, states):
        work.values = state
    return value


def dot(a, b):
    return lax.dot_general(a, b, (((1,), (0,)), ((), ())), preferred_element_type=f32)


def dot_t(a, b):
    return lax.dot_general(a, b, (((1,), (1,)), ((), ())), preferred_element_type=f32)


def first_head(shape):
    return lax.broadcasted_iota(jnp.int32, shape, 1) < P_SIZE


def spread(columns, kind, left):
    return jnp.where(left, columns[:, kind : kind + 1], columns[:, 4 + kind : 5 + kind])


def note_heads(ref, value, first, left):
    lane = lax.broadcasted_iota(jnp.int32, ref.shape, 1) - first - 2 * pl.program_id(0)
    low = jnp.sum(jnp.where(left, value, 0.0), axis=1, keepdims=True)
    high = jnp.sum(jnp.where(left, 0.0, value), axis=1, keepdims=True)
    ref[...] += jnp.where(lane == 0, low, jnp.where(lane == 1, high, 0.0))


def sigmoid(v):
    return 1.0 / (1.0 + jnp.exp(-v))


def forward_kernel(
    x_ref, z_ref, cols_ref, rows_ref, g_ref, q_ref, state_ref, mask_ref, skip_ref, y_ref, gy_ref, ss_ref
):
    length = x_ref.shape[0]
    step = min(256, length)
    left = first_head(x_ref.shape)
    cols = cols_ref[0]
    x = x_ref[...].astype(f32) * mask_ref[...]
    xb = x.astype(bf16)
    inter = dot(q_ref[...], state_ref[...].astype(bf16)) * spread(cols, 3, left)
    parts = []
    for t in range(0, length, step):
        width = t + step
        outs = []
        for h in range(2):
            fall = jnp.minimum(cols[t:width, 4 * h : 4 * h + 1] - rows_ref[0, 2 * h : 2 * h + 1, :width], 0.0)
            mixing = g_ref[t:width, :width] * jnp.exp(fall) * rows_ref[0, 2 * h + 1 : 2 * h + 2, :width]
            outs.append(dot(mixing.astype(bf16), xb[:width]))
        parts.append(jnp.where(left[t:width], outs[0], outs[1]))
    y = jnp.concatenate(parts, axis=0) + inter + skip_ref[...] * x
    z = z_ref[...].astype(f32)
    gy = y * (z * sigmoid(z)) * mask_ref[...]
    y_ref[...] = y
    gy_ref[...] = gy

    @pl.when(pl.program_id(0) == 0)
    def _():
        ss_ref[...] = jnp.zeros_like(ss_ref)

    ss_ref[...] += gy * gy


def backward_kernel(
    do_ref, other_ref, own_ref, y_ref, z_ref, x_ref, cols_ref, rows_ref, gt_ref, qt_ref, state_ref, tok_ref, mask_ref, skip_ref,
    gain_ref, dz_ref, dx_ref, ds_ref, dgt_ref, dq_ref, heads_ref, vec_ref,
):
    length = x_ref.shape[0]
    step = min(256, length)
    left = first_head(x_ref.shape)
    cols = cols_ref[0]
    mask, skip, gain = mask_ref[...], skip_ref[...], gain_ref[...]
    r, pull = tok_ref[:, 0:1], tok_ref[:, 1:2]
    x = x_ref[...].astype(f32) * mask
    y = y_ref[...]
    z = z_ref[...].astype(f32)
    sig = sigmoid(z)
    gate = z * sig * mask
    gy = y * gate
    do = jnp.where(own_ref[...] > 0.5, do_ref[...], other_ref[...])
    dgy = r * do * gain - gy * pull
    dy = dgy * gate
    dz_ref[...] = (dgy * y * mask * sig * (1.0 + z * (1.0 - sig))).astype(bf16)
    vec_ref[0:1, :] = jnp.sum(do * gy * r, axis=0, keepdims=True)
    vec_ref[1:2, :] = jnp.sum(dy * x, axis=0, keepdims=True)
    vec_ref[2:8, :] = jnp.zeros((6, 128), f32)
    dyb = dy.astype(bf16)
    entering = (dy * spread(cols, 3, left)).astype(bf16)
    stateb = state_ref[...].astype(bf16)
    ds_ref[...] = dot(qt_ref[...], entering)

    @pl.when(pl.program_id(0) == 0)
    def _():
        dgt_ref[...] = jnp.zeros_like(dgt_ref)
        dq_ref[...] = jnp.zeros_like(dq_ref)
        heads_ref[...] = jnp.zeros_like(heads_ref)

    dq_ref[...] += dot_t(entering, stateb)
    xh = [jnp.where(left, x, 0.0).astype(bf16), jnp.where(left, 0.0, x).astype(bf16)]
    parts = []
    for s in range(0, length, step):
        outs = []
        total = None
        for h in range(2):
            here = cols[s : s + step]
            decay = jnp.exp(jnp.minimum(rows_ref[0, 2 * h : 2 * h + 1, s:] - here[:, 4 * h : 4 * h + 1], 0.0))
            outs.append(dot((gt_ref[s : s + step, s:] * decay).astype(bf16), dyb[s:]))
            part = dot_t(xh[h][s : s + step], dyb[s:]) * decay * here[:, 4 * h + 1 : 4 * h + 2]
            total = part if total is None else total + part
        dgt_ref[s : s + step, s:] += total
        parts.append(jnp.where(left[s : s + step], outs[0], outs[1]))
    u = jnp.concatenate(parts, axis=0)
    dx_ref[...] = spread(cols, 1, left) * u + skip * dy
    row = dy * (y - skip * x)
    xu = x * u
    note_heads(heads_ref, row, 0, left)
    note_heads(heads_ref, xu, H, left)


def conv_back(dact, in_ref, rim_ref, taps_ref, pad_ref, dc_ref, out_ref, vec_ref, edge_ref):
    length = in_ref.shape[0]
    pad_ref[0:8, :] = rim_ref[...].astype(f32)
    pad_ref[8 : 8 + length, :] = in_ref[...].astype(f32)
    c = taps_ref[4:5, :]
    for k in range(K):
        c = c + taps_ref[k : k + 1, :] * pad_ref[5 + k : 5 + k + length, :]
    sig = sigmoid(c)
    dc = dact * sig * (1.0 + c * (1.0 - sig))
    dc_ref[0:8, :] = jnp.zeros((8, 128), f32)
    dc_ref[8 : 8 + length, :] = dc
    dc_ref[8 + length : 16 + length, :] = jnp.zeros((8, 128), f32)
    for k in range(K):
        vec_ref[k : k + 1, :] = jnp.sum(dc * pad_ref[5 + k : 5 + k + length, :], axis=0, keepdims=True)
    vec_ref[4:5, :] = jnp.sum(dc, axis=0, keepdims=True)
    vec_ref[5:8, :] = jnp.zeros((3, 128), f32)
    grad = jnp.zeros((length + 8, 128), f32)
    for k in range(K):
        grad = grad + taps_ref[k : k + 1, :] * dc_ref[3 - k : 3 - k + length + 8, :]
    out_ref[...] = grad[8:].astype(bf16)
    edge_ref[0:8, :] = grad[:8]
    edge_ref[8:16, :] = grad[length:]


def inner_kernel(
    dx_ref, x_ref, cols_ref, k_ref, later_ref, mask_ref, in_ref, rim_ref, taps_ref, out_ref, vec_ref, edge_ref,
    heads_ref, dk_ref, pad_ref, dc_ref,
):
    left = first_head(x_ref.shape)
    cols = cols_ref[0]
    mask = mask_ref[...]
    x = x_ref[...].astype(f32) * mask
    later = later_ref[...].astype(bf16)
    tail, steps = spread(cols, 2, left), spread(cols, 1, left)
    u = dot(k_ref[...], later) * tail
    xu = x * u

    @pl.when(pl.program_id(0) == 0)
    def _():
        dk_ref[...] = jnp.zeros_like(dk_ref)
        heads_ref[...] = jnp.zeros_like(heads_ref)

    note_heads(heads_ref, xu, 0, left)

    dk_ref[...] += dot_t((x * tail * steps).astype(bf16), later)
    dact = (dx_ref[...] + steps * u) * mask
    conv_back(dact, in_ref, rim_ref, taps_ref, pad_ref, dc_ref, out_ref, vec_ref, edge_ref)


def outer_kernel(dact_ref, in_ref, rim_ref, taps_ref, out_ref, vec_ref, edge_ref, pad_ref, dc_ref):
    conv_back(dact_ref[...], in_ref, rim_ref, taps_ref, pad_ref, dc_ref, out_ref, vec_ref, edge_ref)


def lanes(rows, shift=0):
    return pl.BlockSpec((rows, 128), lambda i: (0, i + shift))


def turns(rows):
    return pl.BlockSpec((rows, 128), lambda i: (0, i % (PAIRS // 2)))


def whole(rows, width):
    return pl.BlockSpec((rows, width), lambda i: (0, 0))


def planes(rows, width):
    return pl.BlockSpec((1, rows, width), lambda i: (i, 0, 0))


def run(kernel, steps, ins, outs, shapes, scratch=()):
    return pl.pallas_call(
        kernel,
        grid=(steps,),
        in_specs=ins,
        out_specs=outs,
        out_shape=[jax.ShapeDtypeStruct(*shape) for shape in shapes],
        scratch_shapes=list(scratch),
        compiler_params=pltpu.CompilerParams(vmem_limit_bytes=48 * 1024 * 1024),
    )


def hand_on(fresh, carry, backward):
    count = lax.axis_size("seq")
    entered = jnp.zeros_like(fresh)
    for i in range(count - 1):
        leaving = (fresh + carry * entered).astype(bf16)
        route = [(count - 1 - i, count - 2 - i)] if backward else [(i, i + 1)]
        entered = entered + lax.ppermute(leaving, "seq", route).astype(f32)
    return entered


def local(
    hidden,
    grad_out,
    doc_lengths,
    resets,
    width_index,
    owner_counts,
    w_in,
    m_in,
    v_in,
    w_out,
    m_out,
    v_out,
    small_params,
    small_m,
    small_v,
):
    T = hidden.shape[0]
    slot = w_in.shape[0]
    seq_count = lax.axis_size("seq")
    devices = lax.axis_size("dp") * seq_count
    base = D // devices
    mine = lax.axis_index("dp") * seq_count + lax.axis_index("seq")
    gain_in, conv_weight, conv_bias, dt_bias, decay_log, skip_gain, gain_out = unpack(small_params)
    channel_mask, active = width_mask(width_index[0])
    before = jnp.arange(devices) < mine
    lead = jnp.sum(jnp.where(before, owner_counts, 0)) * RB - mine * base
    count = owner_counts[mine] * RB

    even_in = even_rows(w_in, count, lead, base)
    even_out = even_rows(w_out, count, lead, base)
    weights_x = lax.all_gather(even_in[:, E:], OWNERS, axis=0, tiled=True)
    weights_z = lax.all_gather(even_in[:, :E], OWNERS, axis=0, tiled=True)
    gather = Gather(even_out, mine, devices, (896, 1792))
    gather.advance()
    gather.advance()
    gather.advance()
    weights_x = tie(weights_x, gather)
    gather.advance()

    hidden_full = hidden.astype(f32)
    scale = lax.rsqrt(jnp.mean(hidden_full * hidden_full, axis=1, keepdims=True) + norm_eps)
    normed = (hidden_full * scale * gain_in[None, :]).astype(bf16)
    proj_x = jnp.dot(normed, weights_x, preferred_element_type=f32).astype(bf16)
    conv_in = proj_x[:, :CW]
    raw = proj_x[:, CW:].astype(f32) + dt_bias[None, :]
    route = [(i, i + 1) for i in range(seq_count - 1)]
    rim = lax.ppermute(conv_in[T - (K - 1) :], "seq", route)
    padded = jnp.concatenate([rim, conv_in], axis=0).astype(f32)
    mixed = conv_bias[None, :] + sum(
        (conv_weight[tap][None, :] * padded[tap : tap + T] for tap in range(K))
    )
    act = (mixed * sigmoid(mixed)).astype(bf16)
    keys, queries = act[:, E : E + N], act[:, E + N :]

    positions = lax.axis_index("seq") * T + jnp.arange(T)
    flags = reset_flags(doc_lengths[0], resets[0], positions)
    steps = jax.nn.softplus(raw)
    rate = jnp.exp(decay_log)[None, :]
    order = jnp.arange(T)
    lower = (order[:, None] >= order[None, :]).astype(f32)
    sums = jnp.dot(
        lower,
        jnp.concatenate([-rate * steps, jnp.broadcast_to(flags[:, None], (T, H))], axis=1),
        precision=lax.Precision.HIGHEST,
    )
    total, segment = sums[:, :H], jnp.round(sums[:, H])
    enter = jnp.exp(total) * (segment == 0)[:, None]
    tail = jnp.exp(total[-1:] - total) * (segment == segment[-1])[:, None]
    carry = jnp.repeat(enter[-1], P_SIZE)[None, :]
    cols = jnp.stack([total, steps, tail, enter], axis=2).reshape(T, PAIRS, 8).transpose(1, 0, 2)
    rows = jnp.stack([total.T, steps.T], axis=1).reshape(PAIRS, 4, T)
    allowed = (segment[:, None] == segment[None, :]) & (order[:, None] >= order[None, :])
    scores = jnp.where(allowed, jnp.einsum("tn,sn->ts", queries, keys, preferred_element_type=f32), 0.0)
    mask_row, skip_row = channel_mask[None, :], jnp.repeat(skip_gain, P_SIZE)[None, :]
    gain_row = gain_out[None, :]

    heads_of = (jnp.arange(E)[None, :] // P_SIZE == jnp.arange(H)[:, None]).astype(bf16)
    weight = jnp.dot((tail * steps).astype(bf16), heads_of, preferred_element_type=f32)
    handed = (act[:, :E].astype(f32) * mask_row * weight).astype(bf16)
    fresh = jnp.dot(keys.T, handed, preferred_element_type=f32)
    entered = hand_on(fresh, carry, False)
    weights_z = tie(weights_z, gather)
    half_out = gather.result()
    other_out = exchange(half_out, 0, devices)
    gate_raw = jnp.dot(normed, weights_z, preferred_element_type=f32).astype(bf16)
    y, gated, squares = run(
        forward_kernel,
        PAIRS,
        [lanes(T), lanes(T), planes(T, 8), planes(4, T), whole(T, T), whole(T, N), lanes(N), lanes(1), lanes(1)],
        [lanes(T), lanes(T), whole(T, 128)],
        [((T, E), f32), ((T, E), f32), ((T, 128), f32)],
    )(act, gate_raw, cols, rows, scores, queries, entered, mask_row, skip_row)
    root = lax.rsqrt(jnp.sum(squares, axis=1, keepdims=True) / active + norm_eps)
    mixed_low = (gated * root * gain_row).astype(bf16)
    half = E // 2
    own_at, other_at = (mine % 2) * half, (1 - mine % 2) * half

    def halves(array):
        return [lax.dynamic_slice_in_dim(array, at, half, 1) for at in (own_at, other_at)]

    out = Reduce(split_rows(grad_out, mine, base), mixed_low, mine, base, devices, (1664, 3328))
    grad_own = jnp.dot(grad_out, half_out, preferred_element_type=f32)
    grad_other = jnp.dot(grad_out, other_out, preferred_element_type=f32)
    grad_own, grad_other = tie((grad_own, grad_other), out)
    out.advance()
    gain_own, gain_other = halves(gain_row)
    gated_own, gated_other = halves(gated)
    along_own = jnp.sum(grad_own * gain_own * gated_own, axis=1, keepdims=True)
    along_other = jnp.sum(grad_other * gain_other * gated_other, axis=1, keepdims=True)
    pull = root**3 * (along_own + along_other) / active
    own_row = (jnp.arange(E)[None, :] // half == mine % 2).astype(f32)
    tok = jnp.concatenate([root, pull, jnp.zeros((T, 6), f32)], axis=1)
    grad_gate, grad_x, grad_entered, grad_scores, grad_queries, heads_a, vec_a = run(
        backward_kernel,
        PAIRS,
        [
            turns(T), turns(T), lanes(1), lanes(T), lanes(T), lanes(T), planes(T, 8), planes(4, T), whole(T, T),
            whole(N, T), lanes(N),
            whole(T, 8), lanes(1), lanes(1), lanes(1),
        ],
        [lanes(T), lanes(T), lanes(N), whole(T, T), whole(T, N), whole(T, 128), lanes(8)],
        [
            ((T, E), bf16), ((T, E), f32), ((N, E), f32), ((T, T), f32), ((T, N), f32), ((T, 128), f32),
            ((8, E), f32),
        ],
    )(grad_own, grad_other, own_row, y, gate_raw, act, cols, rows, scores.T, queries.T, entered, tok, mask_row, skip_row, gain_row)
    grad_gate, grad_entered = tie((grad_gate, grad_entered), out)
    features = split_rows(normed, mine, base)
    work_z = Reduce(features, grad_gate, mine, base, devices, (1664, 3328))
    out.advance()
    du = jnp.einsum("tc,dc->td", grad_gate, weights_z, preferred_element_type=f32)
    later = hand_on(grad_entered, carry, True)
    later, du = tie((later, du), out, work_z)
    out.advance()
    work_z.advance()
    rim8 = jnp.concatenate([jnp.zeros((8 - (K - 1), CW), bf16), rim], axis=0)
    taps = jnp.concatenate([conv_weight, conv_bias[None, :], jnp.zeros((3, CW), f32)], axis=0)
    scratch = (pltpu.VMEM((T + 16, 128), f32), pltpu.VMEM((T + 16, 128), f32))
    inner, vec_b, edge_b, heads_b, grad_keys = run(
        inner_kernel,
        PAIRS,
        [lanes(T), lanes(T), planes(T, 8), whole(T, N), lanes(N), lanes(1), lanes(T), lanes(8), lanes(8)],
        [lanes(T), lanes(8), lanes(16), whole(T, 128), whole(T, N)],
        [((T, E), bf16), ((8, E), f32), ((16, E), f32), ((T, 128), f32), ((T, N), f32)],
        scratch,
    )(grad_x, act, cols, keys, later, mask_row, proj_x, rim8, taps)
    inner, grad_keys = tie((inner, grad_keys), out, work_z)
    out.advance()
    work_z.advance()
    pairs_t = jnp.where(allowed.T, grad_scores, 0.0).astype(bf16)
    grad_keys = grad_keys + jnp.dot(pairs_t, queries, preferred_element_type=f32)
    grad_queries = grad_queries + jnp.einsum("st,sn->tn", pairs_t, keys, preferred_element_type=f32)
    outer, vec_c, edge_c = run(
        outer_kernel,
        2,
        [lanes(T), lanes(T, PAIRS), lanes(8, PAIRS), lanes(8, PAIRS)],
        [lanes(T), lanes(8), lanes(16)],
        [((T, 2 * N), bf16), ((8, 2 * N), f32), ((16, 2 * N), f32)],
        scratch,
    )(jnp.concatenate([grad_keys, grad_queries], axis=1), proj_x, rim8, taps)
    edges = jnp.concatenate([edge_b, edge_c], axis=1)
    pushed = lax.ppermute(edges[8 - (K - 1) : 8], "seq", [(i + 1, i) for i in range(seq_count - 1)])
    ends = (edges[8:] + jnp.concatenate([jnp.zeros((8 - (K - 1), CW), f32), pushed], axis=0)).astype(bf16)

    along = heads_a[:, H:] + heads_b[:, :H]
    leaving = carry * entered + fresh
    crossing = jnp.sum((later * leaving).reshape(N, H, P_SIZE), axis=(0, 2))
    upper = (order[:, None] <= order[None, :]).astype(f32)
    grad_logs = crossing[None, :] + jnp.dot(
        upper, heads_a[:, :H] - steps * along, precision=lax.Precision.HIGHEST
    )
    grad_raw = (along - rate * grad_logs) * jax.nn.sigmoid(raw)
    conv_vec = jnp.concatenate([vec_b, vec_c], axis=1)
    grad_proj = jnp.concatenate([inner, outer, grad_raw.astype(bf16)], axis=1)
    grad_proj = lax.dynamic_update_slice(grad_proj, ends, (T - 8, 0))
    grad_proj = tie(grad_proj, out, work_z)
    work_x = Reduce(features, grad_proj, mine, base, devices, (1792, 3584))
    work_z.advance()

    du = du + jnp.einsum("tc,dc->td", grad_proj, weights_x, preferred_element_type=f32)
    du, last_low = tie((du, mixed_low), work_x, work_z)
    work_x.advance()
    work_z.advance()
    mixed_own, mixed_other = halves(last_low)
    branch = jnp.einsum("te,de->td", mixed_own, half_out, preferred_element_type=f32)
    branch = branch + jnp.einsum("te,de->td", mixed_other, other_out, preferred_element_type=f32)
    output = (hidden_full + branch).astype(bf16)
    dug = du * gain_in[None, :]
    inward = jnp.mean(dug * hidden_full, axis=1, keepdims=True)
    input_grad = grad_out.astype(f32) + scale * dug - hidden_full * scale**3 * inward
    small_grad = jnp.concatenate(
        [
            jnp.sum(du * hidden_full * scale, axis=0),
            conv_vec[:K].reshape(-1),
            conv_vec[K],
            jnp.sum(grad_raw, axis=0),
            -rate[0] * jnp.sum(steps * grad_logs, axis=0),
            jnp.sum(vec_a[1].reshape(H, P_SIZE), axis=1),
            vec_a[0],
        ]
    )

    output, input_grad = tie((output, input_grad), work_x, work_z)

    block_out, block_z, block_x = out.result(), work_z.result(), work_x.result()
    block_in = jnp.concatenate([block_z, block_x], axis=1)
    big_square = jnp.sum(block_in**2) + jnp.sum(block_out**2)
    packed = jnp.concatenate([small_grad, jnp.full((64,), big_square)]).reshape(-1, 128)
    packed = sum_all(packed, devices).reshape(-1)
    small_total, square_total = packed[: small_grad.shape[0]], packed[small_grad.shape[0]]
    owned_in = owned_rows(block_in, count, lead, slot)
    owned_out = owned_rows(block_out, count, lead, slot)
    norm = jnp.sqrt(square_total + jnp.sum(small_total * small_total))
    clip = 1.0 / jnp.maximum(norm, 1.0)
    correction = jnp.float32(bias_fix)
    w_in_new, m_in_new, v_in_new = adamw(w_in, m_in, v_in, owned_in * clip, rate_matrix, correction)
    w_out_new, m_out_new, v_out_new = adamw(
        w_out, m_out, v_out, owned_out * clip, rate_matrix, correction
    )
    small_new, small_m_new, small_v_new = adamw(
        small_params, small_m, small_v, small_total * clip, rate_vector, correction
    )
    return (
        output,
        input_grad,
        w_in_new,
        m_in_new,
        v_in_new,
        w_out_new,
        m_out_new,
        v_out_new,
        small_new,
        small_m_new,
        small_v_new,
        owned_in,
        owned_out,
        small_total,
        norm.reshape(1),
    )


def solution(mesh):
    tokens, row, whole_array = P(OWNERS, None), P("dp", None), P()
    in_specs = (tokens, tokens, row, row, P("dp"), whole_array) + (tokens,) * 6 + (whole_array,) * 3
    out_specs = (tokens,) * 8 + (whole_array,) * 3 + (tokens,) * 2 + (whole_array,) * 2
    return jax.shard_map(local, mesh=mesh, in_specs=in_specs, out_specs=out_specs, check_vma=False)
```

time: 3350 us -> 1010 us (0.30)
  waiting for transfers between devices: 1930 us -> 360 us
  local copies, waits for them, and re-layouts: 549 us -> 79.1 us
  other arithmetic: 330 us -> 125 us
  Pallas kernels: 0 us -> 130 us
  matrix products: 318 us -> 193 us
  blocking collectives: 48.4 us -> 0 us
  starting transfers between devices: 124 us -> 86.1 us
    all_to_all x4 -> x0, waiting for transfers between devices: 1610 us -> none  [the longest x1 918 us: local(): lax.all_to_all(part_in.reshape(seq_count, data_count * slot, width_in), '...]
    ppermute x2 -> x76, waiting for transfers between devices: 0.01 us -> 307 us  [the longest x64 305 us: exchange(): lax.ppermute(value, OWNERS, [(i, i ^ 1 << bit) for i in range(devices)])]
    all_gather x4 -> x2, waiting for transfers between devices: 246 us -> 53.6 us  [the longest x1 32.8 us: local(): weights_z = lax.all_gather(even_in[:, :E], OWNERS, axis=0, tiled=True)]
    gather x4 -> x0, local copies, waits for them, and re-layouts: 171 us -> none  [the longest x1 112 us: natural_order(): jnp.take(gathered[0], place, axis=0)]
    reshape x17 -> x5, local copies, waits for them, and re-layouts: 166 us -> 6.14 us  [the longest x2 4.98 us: local(): jnp.stack([total, steps, tail, enter], axis=2).reshape(T, PAIRS, 8)]
    pallas_call x0 -> x4, Pallas kernels: none -> 130 us  [the longest x1 57 us: local(): run(backward_kernel, PAIRS, [turns(T), turns(T), lanes(1), lanes(T), lane...]
    reduce_sum x26 -> x10, other arithmetic: 139 us -> 9.78 us  [the longest x1 3.29 us: local(): jnp.sum(grad_other * gain_other * gated_other, axis=1, keepdims=True)]
    dot_general x42 -> x34, matrix products: 318 us -> 193 us  [the longest x18 66.1 us: product(): lax.dot_general(features, piece, (((0,), (0,)), ((), ())), preferred_elem...]
  transfers between devices with their start and end apart: 11 -> 78, of which waited for: 7 -> 32; matrix products, arithmetic and copies ran while one was open for 24% -> 31% of each run, Pallas kernels for 0% -> 13%
where the time goes in v1:
time: 1010 us; the launch traced here: 996 us
  waiting for transfers between devices  360 us (36%)
  matrix products  193 us (19%)
  Pallas kernels  130 us (13%)
  other arithmetic  125 us (12%)
  starting transfers between devices  86.1 us (9%)
  local copies, waits for them, and re-layouts  79.1 us (8%)
  between operations  22.4 us (2%)
    ppermute x64, waiting for transfers between devices, exchange(): lax.ppermute(value, OWNERS, [(i, i ^ 1 << bit) for i in range(devices)])  305 us
    dot_general x18, matrix products, product(): lax.dot_general(features, piece, (((0,), (0,)), ((), ())), preferred_elem...  66.1 us
    ppermute x64, starting transfers between devices, exchange(): lax.ppermute(value, OWNERS, [(i, i ^ 1 << bit) for i in range(devices)])  63.6 us
    pallas_call x1, Pallas kernels, local(): run(backward_kernel, PAIRS, [turns(T), turns(T), lanes(1), lanes(T), lane...  57 us
    pallas_call x1, Pallas kernels, local(): run(inner_kernel, PAIRS, [lanes(T), lanes(T), planes(T, 8), whole(T, N),...  36.7 us
    pallas_call x1, Pallas kernels, local(): run(forward_kernel, PAIRS, [lanes(T), lanes(T), planes(T, 8), planes(4, T...  34.7 us
    all_gather x1, waiting for transfers between devices, local(): weights_z = lax.all_gather(even_in[:, :E], OWNERS, axis=0, tiled=True)  32.8 us
    all_gather x1, waiting for transfers between devices, local(): weights_x = lax.all_gather(even_in[:, E:], OWNERS, axis=0, tiled=True)  20.8 us
  transfers between devices with their start and end apart: 78, of which 32 were waited for; matrix products, arithmetic and copies ran while one was open for 31% of the time, Pallas kernels for 13%

profile of v1, /device:TPU:0, one launch (start us, length us, event | category | flops | bytes accessed | tf_op | source)
XLA Modules:
  0.0 995.9 jit_solution(12630885607871387753)
XLA Ops:
  21.4 6.3 collective-permute-start.1
  32.6 7.6 fusion.38
  50.3 3.2 collective-permute-start.10
  53.5 25.2 %collective-permute-done.6 = bf16[128,896]{1,0:T(8,128)(2,1)S(1)} collective-permute-done((bf16[128,896]{1,0:T(8,128)(2,1)S(1)}, bf16[128,896]{1,0:T(8,128)(2,1)S(1)}, u32[]{:S(2)}, u32[]{:S(2)}) %collective-permute-start.6) | collective-permute-done | bytes 229408 | tf_op jit(solution)/shard_map/ppermute | solution.py:78
  79.4 11.1 %collective-permute-done.3 = bf16[128,896]{1,0:T(8,128)(2,1)S(1)} collective-permute-done((bf16[128,896]{1,0:T(8,128)(2,1)S(1)}, bf16[128,896]{1,0:T(8,128)(2,1)S(1)}, u32[]{:S(2)}, u32[]{:S(2)}) %collective-permute-start.3) | collective-permute-done | bytes 229408 | tf_op jit(solution)/shard_map/ppermute | solution.py:78
  92.2 11.7 %collective-permute-done.7 = bf16[2,128,896]{2,1,0:T(8,128)(2,1)S(1)} collective-permute-done((bf16[2,128,896]{2,1,0:T(8,128)(2,1)S(1)}, bf16[2,128,896]{2,1,0:T(8,128)(2,1)S(1)}, u32[]{:S(2)}, u32[]{:S(2)}) %collective-permute-start.7) | collective-permute-done | bytes 458784 | tf_op jit(solution)/shard_map/ppermute | solution.py:78
  106.7 25.6 %collective-permute-done.4 = bf16[2,128,896]{2,1,0:T(8,128)(2,1)S(1)} collective-permute-done((bf16[2,128,896]{2,1,0:T(8,128)(2,1)S(1)}, bf16[2,128,896]{2,1,0:T(8,128)(2,1)S(1)}, u32[]{:S(2)}, u32[]{:S(2)}) %collective-permute-start.4) | collective-permute-done | bytes 458784 | tf_op jit(solution)/shard_map/ppermute | solution.py:78
  132.7 5.7 collective-permute-done.11
  138.4 8.3 collective-permute-done.8
  148.4 10.0 %collective-permute-done.5 = bf16[2,2,128,896]{3,2,1,0:T(8,128)(2,1)S(1)} collective-permute-done((bf16[2,2,128,896]{3,2,1,0:T(8,128)(2,1)S(1)}, bf16[2,2,128,896]{3,2,1,0:T(8,128)(2,1)S(1)}, u32[]{:S(2)}, u32[]{:S(2)}) %collective-permute-start.5) | collective-permute-done | bytes 917536 | tf_op jit(solution)/shard_map/ppermute | solution.py:78
  160.0 20.8 %all-gather.5.cloned.1.call-done = bf16[2048,4416]{1,0:T(8,128)(2,1)} async-done(((bf16[64,4416]{1,0:T(8,128)(2,1)}), bf16[2048,4416]{1,0:T(8,128)(2,1)}) %all-gather.5.cloned.1.call-update) | async-done | bytes 18087952 | tf_op jit(solution)/shard_map/all_gather | solution.py:415
  180.9 14.5 %convolution_convert_fusion.in_ref = bf16[512,4416]{1,0:T(8,128)(2,1)S(1)} fusion(bf16[2048,4416]{1,0:T(8,128)(2,1)} %all-gather.5.cloned.1.call-done, bf16[512,2048]{1,0:T(8,128)(2,1)} %param.15, f32[2048]{0:T(1024)S(1)} %slice.204, f32[512]{0:T(512)S(1)} %get-tuple-element.237), kind=kOutput, calls=%fused_computation.24 | convolution fusion | flops 9267478528 | bytes 24717312 | tf_op jit(solution)/shard_map/dot_general | solution.py:427
  203.9 4.6 slice.261
  209.1 4.8 copy.141
  220.1 7.0 multiply_convert_fusion.x_ref
  227.1 6.4 add_convert_fusion.12
  247.5 30.3 %collective-permute-done.13 = bf16[2,2,2,128,896]{4,3,0,1,2:T(8,128)(2,1)} collective-permute-done((bf16[2,2,2,128,896]{4,3,0,1,2:T(8,128)(2,1)}, bf16[2,2,2,128,896]{4,3,0,1,2:T(8,128)(2,1)}, u32[]{:S(2)}, u32[]{:S(2)}) %collective-permute-start.13) | collective-permute-done | bytes 1835040 | tf_op jit(solution)/shard_map/ppermute | solution.py:78
  287.0 32.8 %all-gather.3.cloned.1.call-done = bf16[2048,4096]{1,0:T(8,128)(2,1)} async-done(((bf16[64,4096]{1,0:T(8,128)(2,1)}), bf16[2048,4096]{1,0:T(8,128)(2,1)}) %all-gather.3.cloned.1.call-update) | async-done | bytes 16777232 | tf_op jit(solution)/shard_map/all_gather | solution.py:416
  323.5 13.9 %convolution_convert_fusion.1.z_ref = bf16[512,4096]{1,0:T(8,128)(2,1)} fusion(bf16[2048,4096]{1,0:T(8,128)(2,1)} %all-gather.3.cloned.1.call-done, bf16[512,2048]{1,0:T(8,128)(2,1)S(1)} %copy-done.25, f32[2048]{0:T(1024)S(1)} %slice.204, f32[512]{0:T(512)S(1)} %copy-done.105), kind=kOutput, calls=%fused_computation.31 | convolution fusion | flops 8596226048 | bytes 23078912 | tf_op jit(solution)/shard_map/dot_general | solution.py:469
  340.2 4.0 pad_maximum_fusion
  346.2 34.7 %shard_map.262 = (f32[512,4096]{1,0:T(8,128)}, f32[512,4096]{1,0:T(8,128)}, f32[512,128]{1,0:T(8,128)S(1)}) custom-call(bf16[512,4352]{1,0:T(8,128)(2,1)} %multiply_convert_fusion.x_ref, bf16[512,4096]{1,0:T(8,128)(2,1)} %convolution_convert_fusion.1.z_ref, f32[32,512,8]{2,1,0:T(8,128)} %bitcast.300, f32[32,4,512]{2,1,0:T(4,128)S(1)} %reshape.442.rows_ref, ...), custom_call_target="tpu_custom_call" | custom-call | tf_op jit(solution)/shard_map/pallas_call | solution.py:470
  381.1 4.9 multiply_convert_fusion.1
  385.9 3.8 convolution_convert_fusion.6
  390.0 3.8 convolution_convert_fusion.7
  396.6 6.2 fusion.33
  404.3 8.3 convolution_bitcast_fusion.1.do_ref
  412.6 3.6 add_convert_fusion.8
  416.2 4.7 add_convert_fusion.4
  421.0 5.4 add_convert_fusion.5
  426.4 11.2 %convolution_bitcast_fusion.other_ref = f32[512,2048]{1,0:T(8,128)} fusion(bf16[512,2048]{1,0:T(8,128)(2,1)S(1)} %copy-done.73, bf16[2048,2048]{1,0:T(8,128)(2,1)} %collective-permute-done.15), kind=kOutput, calls=%fused_computation.76 | convolution fusion | flops 4294967296 | bytes 14680064 | tf_op jit(solution)/shard_map/dot_general | solution.py:487
  442.1 6.7 collective-permute-start.23
  448.8 3.3 multiply_reduce_fusion
  457.7 57.0 %shard_map.263 = (bf16[512,4096]{1,0:T(8,128)(2,1)}, f32[512,4096]{1,0:T(8,128)}, f32[128,4096]{1,0:T(8,128)S(1)}, f32[512,512]{1,0:T(8,128)S(1)}, f32[512,128]{...) custom-call(f32[512,2048]{1,0:T(8,128)} %copy-done.28, f32[512,2048]{1,0:T(8,128)} %convolution_bitcast_fusion.other_ref, ...), custom_call_target="tpu_custom_call" | custom-call | tf_op jit(solution)/shard_map/pallas_call | solution.py:497
  530.8 15.0 %fusion.211 = f32[512,2048]{1,0:T(8,128)} fusion(bf16[512,4096]{1,0:T(8,128)(2,1)} %get-tuple-element.109, bf16[2048,4096]{1,0:T(8,128)(2,1)} %all-gather.3.cloned.1.call-done), kind=kOutput, calls=%fused_computation.454 | convolution fusion | flops 8589934592 | bytes 25165824 | tf_op jit(solution)/shard_map/tc,dc->td/dot_general | solution.py:515
  545.8 3.7 convolution_convert_fusion.4
  556.3 19.0 %collective-permute-done.31 = bf16[2,2,64,768]{3,2,0,1:T(8,128)(2,1)S(1)} collective-permute-done((bf16[2,2,64,768]{3,2,0,1:T(8,128)(2,1)S(1)}, bf16[2,2,64,768]{3,2,0,1:T(8,128)(2,1)S(1)}, u32[]{:S(2)}, u32[]{:S(2)}) %collective-permute-start.31) | collective-permute-done | bytes 393248 | tf_op jit(solution)/shard_map/ppermute | solution.py:78
  578.5 17.5 %collective-permute-done.30 = bf16[2,2,64,1664]{3,2,0,1:T(8,128)(2,1)S(1)} collective-permute-done((bf16[2,2,64,1664]{3,2,0,1:T(8,128)(2,1)S(1)}, bf16[2,2,64,1664]{3,2,0,1:T(8,128)(2,1)S(1)}, u32[]{:S(2)}, u32[]{:S(2)}) %collective-permute-start.30) | collective-permute-done | bytes 852000 | tf_op jit(solution)/shard_map/ppermute | solution.py:78
  616.5 36.7 %shard_map.264 = (bf16[512,4096]{1,0:T(8,128)(2,1)}, f32[8,4096]{1,0:T(8,128)S(1)}, f32[16,4096]{1,0:T(8,128)S(1)}, f32[512,128]{1,0:T(8,128)S(1)}, f32[512,128]{1,0:T(8,128)S(1)}) custom-call(f32[512,4096]{1,0:T(8,128)} %get-tuple-element.114.dx_ref, bf16[512,4352]{1,0:T(8,128)(2,1)} %multiply_convert_fusion.x_ref, f32[32,512,8]{2,1,0:T(8,128)} %bitcast.302, ...), custom_call_target="tpu_custom_call" | custom-call | tf_op jit(solution)/shard_map/pallas_call | solution.py:523
  661.6 8.4 collective-permute-done.35
  697.6 5.0 collective-permute-done.44
  704.8 7.0 collective-permute-done.43
  724.4 5.5 convolution_convert_fusion.2
  729.9 16.7 %fusion.212 = f32[512,2048]{1,0:T(8,128)} fusion(bf16[512,4416]{1,0:T(8,128)(2,1)} %fusion.165, bf16[2048,4416]{1,0:T(8,128)(2,1)} %all-gather.5.cloned.1.call-done), kind=kOutput, calls=%fused_computation.455 | convolution fusion | flops 9261023232 | bytes 26804224 | tf_op jit(solution)/shard_map/tc,dc->td/dot_general | solution.py:564
  752.0 5.8 convolution_convert_fusion.3
  771.8 7.5 collective-permute-done.51
  780.3 3.5 add_convert_fusion.6
  783.8 3.5 copy.161
  787.3 5.2 add_convert_fusion
  792.5 7.9 add_convert_fusion.1
  814.4 7.9 fusion.48
  822.3 11.0 %fusion.14 = bf16[512,2048]{1,0:T(8,128)(2,1)} fusion(bf16[512,2048]{1,0:T(8,128)(2,1)S(1)} %copy-done.27, f32[512,2048]{1,0:T(8,128)} %fusion.48, bf16[2048,2048]{1,0:T(8,128)(2,1)} %collective-permute-done.15, bf16[512,4096]{1,0:T(8,128)(2,1)} %copy-done.50, s32[]{:T(128)S(6)} %select_n.416), kind=kOutput, calls=%fused_computation.38 | convolution fusion | flops 4299161600 | bytes 18874372 | tf_op jit(solution)/shard_map/te,de->td/dot_general | solution.py:570
  833.4 4.9 fusion.16
  842.5 10.2 %collective-permute-done.55 = bf16[2,2,2,64,1792]{4,3,0,1,2:T(8,128)(2,1)} collective-permute-done((bf16[2,2,2,64,1792]{4,3,0,1,2:T(8,128)(2,1)}, bf16[2,2,2,64,1792]{4,3,0,1,2:T(8,128)(2,1)}, u32[]{:S(2)}, u32[]{:S(2)}) %collective-permute-start.55) | collective-permute-done | bytes 1835040 | tf_op jit(solution)/shard_map/ppermute | solution.py:78
  854.6 24.2 %collective-permute-done.54 = bf16[2,2,2,64,1792]{4,3,0,1,2:T(8,128)(2,1)S(1)} collective-permute-done((bf16[2,2,2,64,1792]{4,3,0,1,2:T(8,128)(2,1)S(1)}, bf16[2,2,2,64,1792]{4,3,0,1,2:T(8,128)(2,1)S(1)}, u32[]{:S(2)}, u32[]{:S(2)}) %collective-permute-start.54) | collective-permute-done | bytes 1835040 | tf_op jit(solution)/shard_map/ppermute | solution.py:78
  882.2 17.8 %collective-permute-done.66 = bf16[2,2,64,832]{3,2,1,0:T(8,128)(2,1)S(1)} collective-permute-done((bf16[2,2,64,832]{3,2,1,0:T(8,128)(2,1)S(1)}, bf16[2,2,64,832]{3,2,1,0:T(8,128)(2,1)S(1)}, u32[]{:S(2)}, u32[]{:S(2)}) %collective-permute-start.66) | collective-permute-done | bytes 426016 | tf_op jit(solution)/shard_map/ppermute | solution.py:78
  900.7 5.9 collective-permute-done.67
  909.8 13.5 %collective-permute-done.61 = bf16[2,64,1792]{2,1,0:T(8,128)(2,1)S(1)} collective-permute-done((bf16[2,64,1792]{2,1,0:T(8,128)(2,1)S(1)}, bf16[2,64,1792]{2,1,0:T(8,128)(2,1)S(1)}, u32[]{:S(2)}, u32[]{:S(2)}) %collective-permute-start.61) | collective-permute-done | bytes 458784 | tf_op jit(solution)/shard_map/ppermute | solution.py:78
  923.7 7.7 collective-permute-done.64
  932.0 8.3 collective-permute-done.62
  940.4 3.6 collective-permute-done.65
  949.8 4.7 collective-permute-done.71
  959.5 4.8 collective-permute-done.73
  974.4 5.6 multiply_subtract_fusion.1
  980.9 6.8 multiply_subtract_fusion
  (637 shorter events, 261.5 us)
Async XLA Ops:
  7.2 173.7 %all-gather.5.cloned.1.call-start = ((), (), s32[]{:S(2)}) async-start(), calls=%async_computation.1 | async-start | bytes 18923520 | tf_op jit(solution)/shard_map/all_gather | solution.py:415
  18.7 301.0 %all-gather.3.cloned.1.call-start = ((), (), s32[]{:S(2)}) async-start(), calls=%async_computation | async-start | bytes 17301504 | tf_op jit(solution)/shard_map/all_gather | solution.py:416
  21.4 18.9 %collective-permute-start.1 = (bf16[16,4096]{1,0:T(8,128)(2,1)}, bf16[16,4096]{1,0:T(8,128)(2,1)}, u32[]{:S(2)}, u32[]{:S(2)}) collective-permute-start(bf16[16,4096]{1,0:T(8,128)(2,1)} %dynamic-slice_convert_fusion.16), channel_id=1, source_target_pairs={{0,1},{1,2},{2,3},{3,4},{4,5},{5,6},{6,7},{7,8},{8,9},{9,10},{10,1... | collective-permute-start | bytes 393224 | tf_op jit(solution)/shard_map/ppermute | solution.py:63
  47.2 31.5 %collective-permute-start.6 = (bf16[128,896]{1,0:T(8,128)(2,1)S(1)}, bf16[128,896]{1,0:T(8,128)(2,1)S(1)}, u32[]{:S(2)}, u32[]{:S(2)}) collective-permute-start(bf16[128,896]{1,0:T(8,128)(2,1)S(1)} %get-tuple-element.209), channel_id=1, source_target_pairs={{0,16},{1,17},{2,18},{3,19},{4,20},{5,21},{6,22},{7,23},{8,24},{9,... | collective-permute-start | bytes 688136 | tf_op jit(solution)/shard_map/ppermute | solution.py:78
  49.9 40.7 %collective-permute-start.3 = (bf16[128,896]{1,0:T(8,128)(2,1)S(1)}, bf16[128,896]{1,0:T(8,128)(2,1)S(1)}, u32[]{:S(2)}, u32[]{:S(2)}) collective-permute-start(bf16[128,896]{1,0:T(8,128)(2,1)S(1)} %get-tuple-element.210), channel_id=1, source_target_pairs={{0,16},{1,17},{2,18},{3,19},{4,20},{5,21},{6,22},{7,23},{8,24},{9,... | collective-permute-start | bytes 688136 | tf_op jit(solution)/shard_map/ppermute | solution.py:78
  50.3 29.2 %collective-permute-start.10 = (bf16[2,128,256]{2,1,0:T(8,128)(2,1)S(1)}, bf16[2,128,256]{2,1,0:T(8,128)(2,1)S(1)}, u32[]{:S(2)}, u32[]{:S(2)}) collective-permute-start(bf16[2,128,256]{2,1,0:T(8,128)(2,1)S(1)} %pad_maximum_fusion.16), channel_id=1, source_target_pairs={{0,2},{1,3},{2,0},{3,1},{4,6},{5,7},{6,4},{7,5},{8,10},{9,11},{10,... | collective-permute-start | bytes 393224 | tf_op jit(solution)/shard_map/ppermute | solution.py:78
  78.8 25.2 %collective-permute-start.7 = (bf16[2,128,896]{2,1,0:T(8,128)(2,1)S(1)}, bf16[2,128,896]{2,1,0:T(8,128)(2,1)S(1)}, u32[]{:S(2)}, u32[]{:S(2)}) collective-permute-start(bf16[2,128,896]{2,1,0:T(8,128)(2,1)S(1)} %pad_maximum_fusion.14), channel_id=1, source_target_pairs={{0,8},{1,9},{2,10},{3,11},{4,12},{5,13},{6,14},{7,15},{8,0},{9,1},... | collective-permute-start | bytes 1376264 | tf_op jit(solution)/shard_map/ppermute | solution.py:78
  90.7 41.7 %collective-permute-start.4 = (bf16[2,128,896]{2,1,0:T(8,128)(2,1)S(1)}, bf16[2,128,896]{2,1,0:T(8,128)(2,1)S(1)}, u32[]{:S(2)}, u32[]{:S(2)}) collective-permute-start(bf16[2,128,896]{2,1,0:T(8,128)(2,1)S(1)} %pad_maximum_fusion.13), channel_id=1, source_target_pairs={{0,8},{1,9},{2,10},{3,11},{4,12},{5,13},{6,14},{7,15},{8,0},{9,1},... | collective-permute-start | bytes 1376264 | tf_op jit(solution)/shard_map/ppermute | solution.py:78
  104.2 42.6 %collective-permute-start.8 = (bf16[2,2,128,896]{3,2,0,1:T(8,128)(2,1)S(1)}, bf16[2,2,128,896]{3,2,0,1:T(8,128)(2,1)S(1)}, u32[]{:S(2)}, u32[]{:S(2)}) collective-permute-start(bf16[2,2,128,896]{3,2,0,1:T(8,128)(2,1)S(1)} %pad_maximum_fusion.9), channel_id=1, source_target_pairs={{0,2},{1,3},{2,0},{3,1},{4,6},{5,7},{6,4},{7,5},{8,10},{9,11},{10,... | collective-permute-start | bytes 2752520 | tf_op jit(solution)/shard_map/ppermute | solution.py:78
  106.5 31.8 %collective-permute-start.11 = (bf16[2,2,128,256]{3,2,0,1:T(8,128)(2,1)S(1)}, bf16[2,2,128,256]{3,2,0,1:T(8,128)(2,1)S(1)}, u32[]{:S(2)}, u32[]{:S(2)}) collective-permute-start(bf16[2,2,128,256]{3,2,0,1:T(8,128)(2,1)S(1)} %pad_maximum_fusion.15), channel_id=1, source_target_pairs={{0,16},{1,17},{2,18},{3,19},{4,20},{5,21},{6,22},{7,23},{8,24},{9,... | collective-permute-start | bytes 786440 | tf_op jit(solution)/shard_map/ppermute | solution.py:78
  132.6 25.8 %collective-permute-start.5 = (bf16[2,2,128,896]{3,2,1,0:T(8,128)(2,1)S(1)}, bf16[2,2,128,896]{3,2,1,0:T(8,128)(2,1)S(1)}, u32[]{:S(2)}, u32[]{:S(2)}) collective-permute-start(bf16[2,2,128,896]{3,2,1,0:T(8,128)(2,1)S(1)} %pad_maximum_fusion.8), channel_id=1, source_target_pairs={{0,4},{1,5},{2,6},{3,7},{4,0},{5,1},{6,2},{7,3},{8,12},{9,13},{10,... | collective-permute-start | bytes 2752520 | tf_op jit(solution)/shard_map/ppermute | solution.py:78
  200.5 16.4 %collective-permute-start.16 = (bf16[3,4352]{1,0:T(4,128)(2,1)S(1)}, bf16[3,4352]{1,0:T(4,128)(2,1)S(1)}, u32[]{:S(2)}, u32[]{:S(2)}) collective-permute-start(bf16[3,4352]{1,0:T(4,128)(2,1)S(1)} %slice.260), channel_id=1, source_target_pairs={{0,1},{1,2},{2,3},{4,5},{5,6},{6,7},{8,9},{9,10},{10,11},{12,13},{... | collective-permute-start | bytes 78344 | tf_op jit(solution)/shard_map/ppermute | solution.py:431
  214.4 27.9 %collective-permute-start.14 = (bf16[2,2,2,128,256]{4,3,1,2,0:T(8,128)(2,1)S(1)}, bf16[2,2,2,128,256]{4,3,1,2,0:T(8,128)(2,1)}, u32[]{:S(2)}, u32[]{:S(2)}) collective-permute-start(bf16[2,2,2,128,256]{4,3,1,2,0:T(8,128)(2,1)S(1)} %pad_maximum_fusion.10), channel_id=1, source_target_pairs={{0,8},{1,9},{2,10},{3,11},{4,12},{5,13},{6,14},{7,15},{8,0},{9,1},... | collective-permute-start | bytes 1572872 | tf_op jit(solution)/shard_map/ppermute | solution.py:78
  214.9 62.9 %collective-permute-start.13 = (bf16[2,2,2,128,896]{4,3,0,1,2:T(8,128)(2,1)}, bf16[2,2,2,128,896]{4,3,0,1,2:T(8,128)(2,1)}, u32[]{:S(2)}, u32[]{:S(2)}) collective-permute-start(bf16[2,2,2,128,896]{4,3,0,1,2:T(8,128)(2,1)} %pad_maximum_fusion.5), channel_id=1, source_target_pairs={{0,4},{1,5},{2,6},{3,7},{4,0},{5,1},{6,2},{7,3},{8,12},{9,13},{10,... | collective-permute-start | bytes 5505032 | tf_op jit(solution)/shard_map/ppermute | solution.py:78
  216.3 66.0 %collective-permute-start.12 = (bf16[2,2,2,128,896]{4,3,2,1,0:T(8,128)(2,1)}, bf16[2,2,2,128,896]{4,3,2,1,0:T(8,128)(2,1)}, u32[]{:S(2)}, u32[]{:S(2)}) collective-permute-start(bf16[2,2,2,128,896]{4,3,2,1,0:T(8,128)(2,1)} %pad_maximum_fusion.4), channel_id=1, source_target_pairs={{0,2},{1,3},{2,0},{3,1},{4,6},{5,7},{6,4},{7,5},{8,10},{9,11},{10,... | collective-permute-start | bytes 5505032 | tf_op jit(solution)/shard_map/ppermute | solution.py:78
  245.9 73.8 %collective-permute-start.18 = (bf16[128,4096]{1,0:T(8,128)(2,1)}, bf16[128,4096]{1,0:T(8,128)(2,1)}, u32[]{:S(2)}, u32[]{:S(2)}) collective-permute-start(bf16[128,4096]{1,0:T(8,128)(2,1)} %fusion.44), channel_id=1, source_target_pairs={{1,2},{5,6},{9,10},{13,14},{17,18},{21,22},{25,26},{29,30}} | collective-permute-start | bytes 3145736 | tf_op jit(solution)/shard_map/ppermute | solution.py:380
  322.2 22.3 %collective-permute-start.19 = (bf16[128,4096]{1,0:T(8,128)(2,1)S(1)}, bf16[128,4096]{1,0:T(8,128)(2,1)S(1)}, u32[]{:S(2)}, u32[]{:S(2)}) collective-permute-start(bf16[128,4096]{1,0:T(8,128)(2,1)S(1)} %add_convert_fusion.11), channel_id=1, source_target_pairs={{2,3},{6,7},{10,11},{14,15},{18,19},{22,23},{26,27},{30,31}} | collective-permute-start | bytes 3145736 | tf_op jit(solution)/shard_map/ppermute | solution.py:380
  344.2 82.2 %collective-permute-start.15 = (bf16[2048,2048]{1,0:T(8,128)(2,1)}, bf16[2048,2048]{1,0:T(8,128)(2,1)}, u32[]{:S(2)}, u32[]{:S(2)}) collective-permute-start(bf16[2048,2048]{1,0:T(8,128)(2,1)} %pad_maximum_fusion), channel_id=1, source_target_pairs={{0,1},{1,0},{2,3},{3,2},{4,5},{5,4},{6,7},{7,6},{8,9},{9,8},{10,11... | collective-permute-start | bytes 25165832 | tf_op jit(solution)/shard_map/ppermute | solution.py:78
  389.8 26.5 %collective-permute-start.21 = (bf16[1024,1664]{1,0:T(8,128)(2,1)}, bf16[1024,1664]{1,0:T(8,128)(2,1)}, u32[]{:S(2)}, u32[]{:S(2)}) collective-permute-start(bf16[1024,1664]{1,0:T(8,128)(2,1)} %convolution_convert_fusion.6), channel_id=1, source_target_pairs={{0,1},{1,0},{2,3},{3,2},{4,5},{5,4},{6,7},{7,6},{8,9},{9,8},{10,11... | collective-permute-start | bytes 10223624 | tf_op jit(solution)/shard_map/ppermute | solution.py:78
  393.9 27.1 %collective-permute-start.20 = (bf16[1024,1664]{1,0:T(8,128)(2,1)}, bf16[1024,1664]{1,0:T(8,128)(2,1)}, u32[]{:S(2)}, u32[]{:S(2)}) collective-permute-start(bf16[1024,1664]{1,0:T(8,128)(2,1)} %convolution_convert_fusion.7), channel_id=1, source_target_pairs={{0,1},{1,0},{2,3},{3,2},{4,5},{5,4},{6,7},{7,6},{8,9},{9,8},{10,11... | collective-permute-start | bytes 10223624 | tf_op jit(solution)/shard_map/ppermute | solution.py:78
  396.4 16.3 %collective-permute-start.22 = (bf16[1024,768]{1,0:T(8,128)(2,1)}, bf16[1024,768]{1,0:T(8,128)(2,1)}, u32[]{:S(2)}, u32[]{:S(2)}) collective-permute-start(bf16[1024,768]{1,0:T(8,128)(2,1)} %convolution_convert_fusion.10), channel_id=1, source_target_pairs={{0,1},{1,0},{2,3},{3,2},{4,5},{5,4},{6,7},{7,6},{8,9},{9,8},{10,11... | collective-permute-start | bytes 4718600 | tf_op jit(solution)/shard_map/ppermute | solution.py:78
  438.5 85.5 %collective-permute-start.25 = (bf16[2,2,2,64,768]{4,3,1,2,0:T(8,128)(2,1)}, bf16[2,2,2,64,768]{4,3,1,2,0:T(8,128)(2,1)}, u32[]{:S(2)}, u32[]{:S(2)}) collective-permute-start(bf16[2,2,2,64,768]{4,3,1,2,0:T(8,128)(2,1)} %copy_bitcast_fusion.7), channel_id=1, source_target_pairs={{0,8},{1,9},{2,10},{3,11},{4,12},{5,13},{6,14},{7,15},{8,0},{9,1},... | collective-permute-start | bytes 2359304 | tf_op jit(solution)/shard_map/ppermute | solution.py:78
  440.2 85.2 %collective-permute-start.24 = (bf16[2,2,2,64,1664]{4,3,0,1,2:T(8,128)(2,1)}, bf16[2,2,2,64,1664]{4,3,0,1,2:T(8,128)(2,1)}, u32[]{:S(2)}, u32[]{:S(2)}) collective-permute-start(bf16[2,2,2,64,1664]{4,3,0,1,2:T(8,128)(2,1)} %copy_bitcast_fusion.4), channel_id=1, source_target_pairs={{0,4},{1,5},{2,6},{3,7},{4,0},{5,1},{6,2},{7,3},{8,12},{9,13},{10,... | collective-permute-start | bytes 5111816 | tf_op jit(solution)/shard_map/ppermute | solution.py:78
  442.1 85.4 %collective-permute-start.23 = (bf16[2,2,2,64,1664]{4,3,0,1,2:T(8,128)(2,1)}, bf16[2,2,2,64,1664]{4,3,0,1,2:T(8,128)(2,1)}, u32[]{:S(2)}, u32[]{:S(2)}) collective-permute-start(bf16[2,2,2,64,1664]{4,3,0,1,2:T(8,128)(2,1)} %copy_bitcast_fusion.5), channel_id=1, source_target_pairs={{0,2},{1,3},{2,0},{3,1},{4,6},{5,7},{6,4},{7,5},{8,10},{9,11},{10,... | collective-permute-start | bytes 5111816 | tf_op jit(solution)/shard_map/ppermute | solution.py:78
  529.9 21.7 %collective-permute-start.26 = (bf16[128,4096]{1,0:T(8,128)(2,1)S(1)}, bf16[128,4096]{1,0:T(8,128)(2,1)S(1)}, u32[]{:S(2)}, u32[]{:S(2)}) collective-permute-start(bf16[128,4096]{1,0:T(8,128)(2,1)S(1)} %add_convert_fusion.10), channel_id=1, source_target_pairs={{3,2},{7,6},{11,10},{15,14},{19,18},{23,22},{27,26},{31,30}} | collective-permute-start | bytes 3145736 | tf_op jit(solution)/shard_map/ppermute | solution.py:380
  552.0 25.5 %collective-permute-start.27 = (bf16[128,4096]{1,0:T(8,128)(2,1)S(1)}, bf16[128,4096]{1,0:T(8,128)(2,1)S(1)}, u32[]{:S(2)}, u32[]{:S(2)}) collective-permute-start(bf16[128,4096]{1,0:T(8,128)(2,1)S(1)} %fusion.46), channel_id=1, source_target_pairs={{2,1},{6,5},{10,9},{14,13},{18,17},{22,21},{26,25},{30,29}} | collective-permute-start | bytes 3145736 | tf_op jit(solution)/shard_map/ppermute | solution.py:380
  553.7 44.2 %collective-permute-start.34 = (bf16[1024,768]{1,0:T(8,128)(2,1)S(1)}, bf16[1024,768]{1,0:T(8,128)(2,1)S(1)}, u32[]{:S(2)}, u32[]{:S(2)}) collective-permute-start(bf16[1024,768]{1,0:T(8,128)(2,1)S(1)} %convolution_convert_fusion.9), channel_id=1, source_target_pairs={{0,1},{1,0},{2,3},{3,2},{4,5},{5,4},{6,7},{7,6},{8,9},{9,8},{10,11... | collective-permute-start | bytes 4718600 | tf_op jit(solution)/shard_map/ppermute | solution.py:78
  553.8 47.2 %collective-permute-start.33 = (bf16[1024,1664]{1,0:T(8,128)(2,1)S(1)}, bf16[1024,1664]{1,0:T(8,128)(2,1)S(1)}, u32[]{:S(2)}, u32[]{:S(2)}) collective-permute-start(bf16[1024,1664]{1,0:T(8,128)(2,1)S(1)} %convolution_convert_fusion.4), channel_id=1, source_target_pairs={{0,1},{1,0},{2,3},{3,2},{4,5},{5,4},{6,7},{7,6},{8,9},{9,8},{10,11... | collective-permute-start | bytes 10223624 | tf_op jit(solution)/shard_map/ppermute | solution.py:78
  554.3 48.9 %collective-permute-start.32 = (bf16[1024,1664]{1,0:T(8,128)(2,1)S(1)}, bf16[1024,1664]{1,0:T(8,128)(2,1)S(1)}, u32[]{:S(2)}, u32[]{:S(2)}) collective-permute-start(bf16[1024,1664]{1,0:T(8,128)(2,1)S(1)} %convolution_convert_fusion.5), channel_id=1, source_target_pairs={{0,1},{1,0},{2,3},{3,2},{4,5},{5,4},{6,7},{7,6},{8,9},{9,8},{10,11... | collective-permute-start | bytes 10223624 | tf_op jit(solution)/shard_map/ppermute | solution.py:78
  554.4 20.8 %collective-permute-start.31 = (bf16[2,2,64,768]{3,2,0,1:T(8,128)(2,1)S(1)}, bf16[2,2,64,768]{3,2,0,1:T(8,128)(2,1)S(1)}, u32[]{:S(2)}, u32[]{:S(2)}) collective-permute-start(bf16[2,2,64,768]{3,2,0,1:T(8,128)(2,1)S(1)} %dynamic-slice_bitcast_fusion.9), channel_id=1, source_target_pairs={{0,16},{1,17},{2,18},{3,19},{4,20},{5,21},{6,22},{7,23},{8,24},{9,... | collective-permute-start | bytes 1179656 | tf_op jit(solution)/shard_map/ppermute | solution.py:78
  575.3 20.8 %collective-permute-start.30 = (bf16[2,2,64,1664]{3,2,0,1:T(8,128)(2,1)S(1)}, bf16[2,2,64,1664]{3,2,0,1:T(8,128)(2,1)S(1)}, u32[]{:S(2)}, u32[]{:S(2)}) collective-permute-start(bf16[2,2,64,1664]{3,2,0,1:T(8,128)(2,1)S(1)} %dynamic-slice_bitcast_fusion.5), channel_id=1, source_target_pairs={{0,2},{1,3},{2,0},{3,1},{4,6},{5,7},{6,4},{7,5},{8,10},{9,11},{10,... | collective-permute-start | bytes 2555912 | tf_op jit(solution)/shard_map/ppermute | solution.py:78
  577.5 20.2 %collective-permute-start.29 = (bf16[2,2,64,1664]{3,2,0,1:T(8,128)(2,1)S(1)}, bf16[2,2,64,1664]{3,2,0,1:T(8,128)(2,1)S(1)}, u32[]{:S(2)}, u32[]{:S(2)}) collective-permute-start(bf16[2,2,64,1664]{3,2,0,1:T(8,128)(2,1)S(1)} %dynamic-slice_bitcast_fusion.6), channel_id=1, source_target_pairs={{0,4},{1,5},{2,6},{3,7},{4,0},{5,1},{6,2},{7,3},{8,12},{9,13},{10,... | collective-permute-start | bytes 2555912 | tf_op jit(solution)/shard_map/ppermute | solution.py:78
  606.5 63.5 %collective-permute-start.40 = (bf16[2,2,2,64,768]{4,3,1,2,0:T(8,128)(2,1)}, bf16[2,2,2,64,768]{4,3,1,2,0:T(8,128)(2,1)}, u32[]{:S(2)}, u32[]{:S(2)}) collective-permute-start(bf16[2,2,2,64,768]{4,3,1,2,0:T(8,128)(2,1)} %copy_bitcast_fusion.6), channel_id=1, source_target_pairs={{0,8},{1,9},{2,10},{3,11},{4,12},{5,13},{6,14},{7,15},{8,0},{9,1},... | collective-permute-start | bytes 2359304 | tf_op jit(solution)/shard_map/ppermute | solution.py:78
  608.1 63.6 %collective-permute-start.39 = (bf16[2,2,2,64,1664]{4,3,0,1,2:T(8,128)(2,1)}, bf16[2,2,2,64,1664]{4,3,0,1,2:T(8,128)(2,1)}, u32[]{:S(2)}, u32[]{:S(2)}) collective-permute-start(bf16[2,2,2,64,1664]{4,3,0,1,2:T(8,128)(2,1)} %copy_bitcast_fusion.2), channel_id=1, source_target_pairs={{0,4},{1,5},{2,6},{3,7},{4,0},{5,1},{6,2},{7,3},{8,12},{9,13},{10,... | collective-permute-start | bytes 5111816 | tf_op jit(solution)/shard_map/ppermute | solution.py:78
  609.9 63.8 %collective-permute-start.38 = (bf16[2,2,2,64,1664]{4,3,0,1,2:T(8,128)(2,1)}, bf16[2,2,2,64,1664]{4,3,0,1,2:T(8,128)(2,1)}, u32[]{:S(2)}, u32[]{:S(2)}) collective-permute-start(bf16[2,2,2,64,1664]{4,3,0,1,2:T(8,128)(2,1)} %copy_bitcast_fusion.3), channel_id=1, source_target_pairs={{0,2},{1,3},{2,0},{3,1},{4,6},{5,7},{6,4},{7,5},{8,10},{9,11},{10,... | collective-permute-start | bytes 5111816 | tf_op jit(solution)/shard_map/ppermute | solution.py:78
  610.0 48.6 %collective-permute-start.37 = (bf16[2,64,768]{2,1,0:T(8,128)(2,1)S(1)}, bf16[2,64,768]{2,1,0:T(8,128)(2,1)S(1)}, u32[]{:S(2)}, u32[]{:S(2)}) collective-permute-start(bf16[2,64,768]{2,1,0:T(8,128)(2,1)S(1)} %fusion.154), channel_id=1, source_target_pairs={{0,2},{1,3},{2,0},{3,1},{4,6},{5,7},{6,4},{7,5},{8,10},{9,11},{10,... | collective-permute-start | bytes 589832 | tf_op jit(solution)/shard_map/ppermute | solution.py:78
  612.9 47.5 %collective-permute-start.36 = (bf16[2,64,1664]{2,1,0:T(8,128)(2,1)}, bf16[2,64,1664]{2,1,0:T(8,128)(2,1)}, u32[]{:S(2)}, u32[]{:S(2)}) collective-permute-start(bf16[2,64,1664]{2,1,0:T(8,128)(2,1)} %fusion.134), channel_id=1, source_target_pairs={{0,8},{1,9},{2,10},{3,11},{4,12},{5,13},{6,14},{7,15},{8,0},{9,1},... | collective-permute-start | bytes 1277960 | tf_op jit(solution)/shard_map/ppermute | solution.py:78
  677.2 41.0 %collective-permute-start.47 = (bf16[2,2,64,768]{3,2,0,1:T(8,128)(2,1)}, bf16[2,2,64,768]{3,2,0,1:T(8,128)(2,1)}, u32[]{:S(2)}, u32[]{:S(2)}) collective-permute-start(bf16[2,2,64,768]{3,2,0,1:T(8,128)(2,1)} %dynamic-slice_bitcast_fusion.8), channel_id=1, source_target_pairs={{0,16},{1,17},{2,18},{3,19},{4,20},{5,21},{6,22},{7,23},{8,24},{9,... | collective-permute-start | bytes 1179656 | tf_op jit(solution)/shard_map/ppermute | solution.py:78
  680.2 40.2 %collective-permute-start.46 = (bf16[2,2,64,1664]{3,2,0,1:T(8,128)(2,1)}, bf16[2,2,64,1664]{3,2,0,1:T(8,128)(2,1)}, u32[]{:S(2)}, u32[]{:S(2)}) collective-permute-start(bf16[2,2,64,1664]{3,2,0,1:T(8,128)(2,1)} %dynamic-slice_bitcast_fusion.3), channel_id=1, source_target_pairs={{0,2},{1,3},{2,0},{3,1},{4,6},{5,7},{6,4},{7,5},{8,10},{9,11},{10,... | collective-permute-start | bytes 2555912 | tf_op jit(solution)/shard_map/ppermute | solution.py:78
  681.4 41.6 %collective-permute-start.45 = (bf16[2,2,64,1664]{3,2,0,1:T(8,128)(2,1)}, bf16[2,2,64,1664]{3,2,0,1:T(8,128)(2,1)}, u32[]{:S(2)}, u32[]{:S(2)}) collective-permute-start(bf16[2,2,64,1664]{3,2,0,1:T(8,128)(2,1)} %dynamic-slice_bitcast_fusion.4), channel_id=1, source_target_pairs={{0,4},{1,5},{2,6},{3,7},{4,0},{5,1},{6,2},{7,3},{8,12},{9,13},{10,... | collective-permute-start | bytes 2555912 | tf_op jit(solution)/shard_map/ppermute | solution.py:78
  683.6 19.0 %collective-permute-start.44 = (bf16[64,768]{1,0:T(8,128)(2,1)}, bf16[64,768]{1,0:T(8,128)(2,1)}, u32[]{:S(2)}, u32[]{:S(2)}) collective-permute-start(bf16[64,768]{1,0:T(8,128)(2,1)} %fusion.163), channel_id=1, source_target_pairs={{0,4},{1,5},{2,6},{3,7},{4,0},{5,1},{6,2},{7,3},{8,12},{9,13},{10,... | collective-permute-start | bytes 294920 | tf_op jit(solution)/shard_map/ppermute | solution.py:78
  695.1 16.8 %collective-permute-start.43 = (bf16[64,1664]{1,0:T(8,128)(2,1)}, bf16[64,1664]{1,0:T(8,128)(2,1)S(1)}, u32[]{:S(2)}, u32[]{:S(2)}) collective-permute-start(bf16[64,1664]{1,0:T(8,128)(2,1)} %fusion.151), channel_id=1, source_target_pairs={{0,16},{1,17},{2,18},{3,19},{4,20},{5,21},{6,22},{7,23},{8,24},{9,... | collective-permute-start | bytes 638984 | tf_op jit(solution)/shard_map/ppermute | solution.py:78
  702.6 13.8 %collective-permute-start.42 = (bf16[64,1664]{1,0:T(8,128)(2,1)}, bf16[64,1664]{1,0:T(8,128)(2,1)S(1)}, u32[]{:S(2)}, u32[]{:S(2)}) collective-permute-start(bf16[64,1664]{1,0:T(8,128)(2,1)} %fusion.150), channel_id=1, source_target_pairs={{0,16},{1,17},{2,18},{3,19},{4,20},{5,21},{6,22},{7,23},{8,24},{9,... | collective-permute-start | bytes 638984 | tf_op jit(solution)/shard_map/ppermute | solution.py:78
  746.6 40.7 %collective-permute-start.49 = (bf16[1024,1792]{1,0:T(8,128)(2,1)}, bf16[1024,1792]{1,0:T(8,128)(2,1)}, u32[]{:S(2)}, u32[]{:S(2)}) collective-permute-start(bf16[1024,1792]{1,0:T(8,128)(2,1)} %convolution_convert_fusion.2), channel_id=1, source_target_pairs={{0,1},{1,0},{2,3},{3,2},{4,5},{5,4},{6,7},{7,6},{8,9},{9,8},{10,11... | collective-permute-start | bytes 11010056 | tf_op jit(solution)/shard_map/ppermute | solution.py:78
  749.2 16.6 %collective-permute-start.53 = (bf16[2,64,768]{2,1,0:T(8,128)(2,1)S(1)}, bf16[2,64,768]{2,1,0:T(8,128)(2,1)S(1)}, u32[]{:S(2)}, u32[]{:S(2)}) collective-permute-start(bf16[2,64,768]{2,1,0:T(8,128)(2,1)S(1)} %fusion.155), channel_id=1, source_target_pairs={{0,2},{1,3},{2,0},{3,1},{4,6},{5,7},{6,4},{7,5},{8,10},{9,11},{10,... | collective-permute-start | bytes 589832 | tf_op jit(solution)/shard_map/ppermute | solution.py:78
  757.8 34.7 %collective-permute-start.48 = (bf16[1024,1792]{1,0:T(8,128)(2,1)}, bf16[1024,1792]{1,0:T(8,128)(2,1)}, u32[]{:S(2)}, u32[]{:S(2)}) collective-permute-start(bf16[1024,1792]{1,0:T(8,128)(2,1)} %convolution_convert_fusion.3), channel_id=1, source_target_pairs={{0,1},{1,0},{2,3},{3,2},{4,5},{5,4},{6,7},{7,6},{8,9},{9,8},{10,11... | collective-permute-start | bytes 11010056 | tf_op jit(solution)/shard_map/ppermute | solution.py:78
  758.1 12.8 %collective-permute-start.52 = (bf16[2,64,1664]{2,1,0:T(8,128)(2,1)S(1)}, bf16[2,64,1664]{2,1,0:T(8,128)(2,1)S(1)}, u32[]{:S(2)}, u32[]{:S(2)}) collective-permute-start(bf16[2,64,1664]{2,1,0:T(8,128)(2,1)S(1)} %fusion.136), channel_id=1, source_target_pairs={{0,8},{1,9},{2,10},{3,11},{4,12},{5,13},{6,14},{7,15},{8,0},{9,1},... | collective-permute-start | bytes 1277960 | tf_op jit(solution)/shard_map/ppermute | solution.py:78
  760.7 19.6 %collective-permute-start.50 = (bf16[1024,832]{0,1:T(8,128)(2,1)S(1)}, bf16[1024,832]{0,1:T(8,128)(2,1)S(1)}, u32[]{:S(2)}, u32[]{:S(2)}) collective-permute-start(bf16[1024,832]{0,1:T(8,128)(2,1)S(1)} %convolution_convert_fusion.8), channel_id=1, source_target_pairs={{0,1},{1,0},{2,3},{3,2},{4,5},{5,4},{6,7},{7,6},{8,9},{9,8},{10,11... | collective-permute-start | bytes 5111816 | tf_op jit(solution)/shard_map/ppermute | solution.py:78
  765.8 13.5 %collective-permute-start.51 = (bf16[2,64,1664]{2,1,0:T(8,128)(2,1)S(1)}, bf16[2,64,1664]{2,1,0:T(8,128)(2,1)S(1)}, u32[]{:S(2)}, u32[]{:S(2)}) collective-permute-start(bf16[2,64,1664]{2,1,0:T(8,128)(2,1)S(1)} %fusion.135), channel_id=1, source_target_pairs={{0,8},{1,9},{2,10},{3,11},{4,12},{5,13},{6,14},{7,15},{8,0},{9,1},... | collective-permute-start | bytes 1277960 | tf_op jit(solution)/shard_map/ppermute | solution.py:78
  801.4 37.1 %collective-permute-start.59 = (bf16[64,768]{1,0:T(8,128)(2,1)S(1)}, bf16[64,768]{1,0:T(8,128)(2,1)S(1)}, u32[]{:S(2)}, u32[]{:S(2)}) collective-permute-start(bf16[64,768]{1,0:T(8,128)(2,1)S(1)} %fusion.164), channel_id=1, source_target_pairs={{0,4},{1,5},{2,6},{3,7},{4,0},{5,1},{6,2},{7,3},{8,12},{9,13},{10,... | collective-permute-start | bytes 294920 | tf_op jit(solution)/shard_map/ppermute | solution.py:78
  804.8 34.5 %collective-permute-start.58 = (bf16[64,1664]{1,0:T(8,128)(2,1)}, bf16[64,1664]{1,0:T(8,128)(2,1)}, u32[]{:S(2)}, u32[]{:S(2)}) collective-permute-start(bf16[64,1664]{1,0:T(8,128)(2,1)} %fusion.153), channel_id=1, source_target_pairs={{0,16},{1,17},{2,18},{3,19},{4,20},{5,21},{6,22},{7,23},{8,24},{9,... | collective-permute-start | bytes 638984 | tf_op jit(solution)/shard_map/ppermute | solution.py:78
  806.6 34.4 %collective-permute-start.57 = (bf16[64,1664]{1,0:T(8,128)(2,1)}, bf16[64,1664]{1,0:T(8,128)(2,1)S(1)}, u32[]{:S(2)}, u32[]{:S(2)}) collective-permute-start(bf16[64,1664]{1,0:T(8,128)(2,1)} %fusion.152), channel_id=1, source_target_pairs={{0,16},{1,17},{2,18},{3,19},{4,20},{5,21},{6,22},{7,23},{8,24},{9,... | collective-permute-start | bytes 638984 | tf_op jit(solution)/shard_map/ppermute | solution.py:78
  810.5 30.6 %collective-permute-start.56 = (bf16[2,2,2,64,832]{4,3,2,1,0:T(8,128)(2,1)}, bf16[2,2,2,64,832]{4,3,2,1,0:T(8,128)(2,1)}, u32[]{:S(2)}, u32[]{:S(2)}) collective-permute-start(bf16[2,2,2,64,832]{4,3,2,1,0:T(8,128)(2,1)} %dynamic-slice_bitcast_fusion.2), channel_id=1, source_target_pairs={{0,8},{1,9},{2,10},{3,11},{4,12},{5,13},{6,14},{7,15},{8,0},{9,1},... | collective-permute-start | bytes 2555912 | tf_op jit(solution)/shard_map/ppermute | solution.py:78
  812.1 40.6 %collective-permute-start.55 = (bf16[2,2,2,64,1792]{4,3,0,1,2:T(8,128)(2,1)}, bf16[2,2,2,64,1792]{4,3,0,1,2:T(8,128)(2,1)}, u32[]{:S(2)}, u32[]{:S(2)}) collective-permute-start(bf16[2,2,2,64,1792]{4,3,0,1,2:T(8,128)(2,1)} %copy_bitcast_fusion), channel_id=1, source_target_pairs={{0,4},{1,5},{2,6},{3,7},{4,0},{5,1},{6,2},{7,3},{8,12},{9,13},{10,... | collective-permute-start | bytes 5505032 | tf_op jit(solution)/shard_map/ppermute | solution.py:78
  838.5 40.3 %collective-permute-start.54 = (bf16[2,2,2,64,1792]{4,3,0,1,2:T(8,128)(2,1)S(1)}, bf16[2,2,2,64,1792]{4,3,0,1,2:T(8,128)(2,1)S(1)}, u32[]{:S(2)}, u32[]{:S(2)}) collective-permute-start(bf16[2,2,2,64,1792]{4,3,0,1,2:T(8,128)(2,1)S(1)} %copy_bitcast_fusion.1), channel_id=1, source_target_pairs={{0,2},{1,3},{2,0},{3,1},{4,6},{5,7},{6,4},{7,5},{8,10},{9,11},{10,... | collective-permute-start | bytes 5505032 | tf_op jit(solution)/shard_map/ppermute | solution.py:78
  879.3 20.7 %collective-permute-start.66 = (bf16[2,2,64,832]{3,2,1,0:T(8,128)(2,1)S(1)}, bf16[2,2,64,832]{3,2,1,0:T(8,128)(2,1)S(1)}, u32[]{:S(2)}, u32[]{:S(2)}) collective-permute-start(bf16[2,2,64,832]{3,2,1,0:T(8,128)(2,1)S(1)} %dynamic-slice_bitcast_fusion.7), channel_id=1, source_target_pairs={{0,16},{1,17},{2,18},{3,19},{4,20},{5,21},{6,22},{7,23},{8,24},{9,... | collective-permute-start | bytes 1277960 | tf_op jit(solution)/shard_map/ppermute | solution.py:78
  881.0 26.5 %collective-permute-start.63 = (bf16[2,2,64,1792]{3,2,0,1:T(8,128)(2,1)S(1)}, bf16[2,2,64,1792]{3,2,0,1:T(8,128)(2,1)S(1)}, u32[]{:S(2)}, u32[]{:S(2)}) collective-permute-start(bf16[2,2,64,1792]{3,2,0,1:T(8,128)(2,1)S(1)} %dynamic-slice_bitcast_fusion), channel_id=1, source_target_pairs={{0,2},{1,3},{2,0},{3,1},{4,6},{5,7},{6,4},{7,5},{8,10},{9,11},{10,... | collective-permute-start | bytes 2752520 | tf_op jit(solution)/shard_map/ppermute | solution.py:78
  881.4 25.7 %collective-permute-start.60 = (bf16[2,2,64,1792]{3,2,0,1:T(8,128)(2,1)S(1)}, bf16[2,2,64,1792]{3,2,0,1:T(8,128)(2,1)S(1)}, u32[]{:S(2)}, u32[]{:S(2)}) collective-permute-start(bf16[2,2,64,1792]{3,2,0,1:T(8,128)(2,1)S(1)} %dynamic-slice_bitcast_fusion.1), channel_id=1, source_target_pairs={{0,4},{1,5},{2,6},{3,7},{4,0},{5,1},{6,2},{7,3},{8,12},{9,13},{10,... | collective-permute-start | bytes 2752520 | tf_op jit(solution)/shard_map/ppermute | solution.py:78
  906.6 37.4 %collective-permute-start.68 = (bf16[64,832]{1,0:T(8,128)(2,1)S(1)}, bf16[64,832]{1,0:T(8,128)(2,1)S(1)}, u32[]{:S(2)}, u32[]{:S(2)}) collective-permute-start(bf16[64,832]{1,0:T(8,128)(2,1)S(1)} %fusion.162), channel_id=1, source_target_pairs={{0,4},{1,5},{2,6},{3,7},{4,0},{5,1},{6,2},{7,3},{8,12},{9,13},{10,... | collective-permute-start | bytes 319496 | tf_op jit(solution)/shard_map/ppermute | solution.py:78
  907.4 15.9 %collective-permute-start.61 = (bf16[2,64,1792]{2,1,0:T(8,128)(2,1)S(1)}, bf16[2,64,1792]{2,1,0:T(8,128)(2,1)S(1)}, u32[]{:S(2)}, u32[]{:S(2)}) collective-permute-start(bf16[2,64,1792]{2,1,0:T(8,128)(2,1)S(1)} %fusion.117), channel_id=1, source_target_pairs={{0,8},{1,9},{2,10},{3,11},{4,12},{5,13},{6,14},{7,15},{8,0},{9,1},... | collective-permute-start | bytes 1376264 | tf_op jit(solution)/shard_map/ppermute | solution.py:78
  907.7 23.6 %collective-permute-start.64 = (bf16[2,64,1792]{2,1,0:T(8,128)(2,1)S(1)}, bf16[2,64,1792]{2,1,0:T(8,128)(2,1)S(1)}, u32[]{:S(2)}, u32[]{:S(2)}) collective-permute-start(bf16[2,64,1792]{2,1,0:T(8,128)(2,1)S(1)} %fusion.118), channel_id=1, source_target_pairs={{0,8},{1,9},{2,10},{3,11},{4,12},{5,13},{6,14},{7,15},{8,0},{9,1},... | collective-permute-start | bytes 1376264 | tf_op jit(solution)/shard_map/ppermute | solution.py:78
  923.4 16.9 %collective-permute-start.62 = (bf16[64,1792]{1,0:T(8,128)(2,1)S(1)}, bf16[64,1792]{1,0:T(8,128)(2,1)S(1)}, u32[]{:S(2)}, u32[]{:S(2)}) collective-permute-start(bf16[64,1792]{1,0:T(8,128)(2,1)S(1)} %fusion.143), channel_id=1, source_target_pairs={{0,16},{1,17},{2,18},{3,19},{4,20},{5,21},{6,22},{7,23},{8,24},{9,... | collective-permute-start | bytes 688136 | tf_op jit(solution)/shard_map/ppermute | solution.py:78
  931.5 12.5 %collective-permute-start.65 = (bf16[64,1792]{1,0:T(8,128)(2,1)S(1)}, bf16[64,1792]{1,0:T(8,128)(2,1)S(1)}, u32[]{:S(2)}, u32[]{:S(2)}) collective-permute-start(bf16[64,1792]{1,0:T(8,128)(2,1)S(1)} %fusion.144), channel_id=1, source_target_pairs={{0,16},{1,17},{2,18},{3,19},{4,20},{5,21},{6,22},{7,23},{8,24},{9,... | collective-permute-start | bytes 688136 | tf_op jit(solution)/shard_map/ppermute | solution.py:78
  967.3 13.5 %collective-permute-start.69 = (f32[16,8512]{1,0:T(8,128)}, f32[16,8512]{1,0:T(8,128)}, u32[]{:S(2)}, u32[]{:S(2)}) collective-permute-start(f32[16,8512]{1,0:T(8,128)} %slice.283), channel_id=1, source_target_pairs={{1,0},{2,1},{3,2},{4,3},{5,4},{6,5},{7,6},{8,7},{9,8},{10,9},{11,1... | collective-permute-start | bytes 1634312 | tf_op jit(solution)/shard_map/ppermute | solution.py:71
  (149 other events, 2800.9 us)
Sparse Core Ops, SparseCore 0:
  18.8 161.9 all-gather.4
  184.3 135.3 all-gather.2

commit v2 on v1

--- a/solution.py
+++ b/solution.py
@@ -1,3 +1,5 @@
+from functools import partial
+
 import jax
 import jax.numpy as jnp
 from jax import lax
@@ -93,17 +95,16 @@
     return jnp.dot(left, pick, preferred_element_type=f32).astype(bf16)
 
 
-def orders_of(devices, gather):
+def orders_of(devices, pieces):
     rest = list(range(3, devices.bit_length() - 1))
-    orders = [[1, 2] + rest, [2, 1] + rest, rest[:2] + [1, 2] + rest[2:]]
-    return [order[::-1] for order in orders] if gather else orders
+    return [[1, 2] + rest, [2, 1] + rest, rest[:2] + [1, 2] + rest[2:]][:pieces]
 
 
 class Reduce:
     def __init__(self, left, right, mine, base, devices, cuts):
         bits = devices.bit_length() - 1
         self.mine, self.devices, self.step = mine, devices, 0
-        self.orders = orders_of(devices, False)
+        self.orders = orders_of(devices, len(cuts) + 1)
         self.axes = [list(range(bits - 1, 0, -1)) for _ in self.orders]
         pieces = [right[:, begin:end] for begin, end in zip((0,) + cuts, cuts + (right.shape[1],))]
 
@@ -133,39 +134,6 @@
         while self.step < len(self.orders[0]):
             self.advance()
         return jnp.concatenate(self.values, axis=1)
-
-
-class Gather:
-    def __init__(self, block, mine, devices, cuts):
-        base, columns = block.shape
-        half = columns // 2
-        low = mine % 2
-        other = lax.dynamic_slice_in_dim(block, (1 - low) * half, half, 1)
-        own = lax.dynamic_slice_in_dim(block, low * half, half, 1)
-        got = exchange(other, 0, devices)
-        both = jnp.concatenate([jnp.where(low == 0, own, got), jnp.where(low == 0, got, own)], axis=0)
-        self.mine, self.devices, self.step = mine, devices, 0
-        self.orders = orders_of(devices, True)
-        self.bits = [[] for _ in self.orders]
-        self.values = [both[:, begin:end] for begin, end in zip((0,) + cuts, cuts + (half,))]
-
-    def advance(self):
-        for piece, (order, bits) in enumerate(zip(self.orders, self.bits)):
-            bit, value = order[self.step], self.values[piece]
-            own = (self.mine >> bit) & 1
-            got = exchange(value, bit, self.devices)
-            bits.append(bit)
-            bits.sort(reverse=True)
-            axis = bits.index(bit)
-            self.values[piece] = jnp.stack(
-                [jnp.where(own == 0, value, got), jnp.where(own == 0, got, value)], axis=axis
-            )
-        self.step += 1
-
-    def result(self):
-        while self.step < len(self.orders[0]):
-            self.advance()
-        return jnp.concatenate([value.reshape(D, value.shape[-1]) for value in self.values], axis=1)
 
 
 def tie(value, *works):
@@ -235,8 +203,8 @@
 
 
 def backward_kernel(
-    do_ref, other_ref, own_ref, y_ref, z_ref, x_ref, cols_ref, rows_ref, gt_ref, qt_ref, state_ref, tok_ref, mask_ref, skip_ref,
-    gain_ref, dz_ref, dx_ref, ds_ref, dgt_ref, dq_ref, heads_ref, vec_ref,
+    do_ref, y_ref, z_ref, x_ref, cols_ref, rows_ref, gt_ref, state_ref, tok_ref, mask_ref, skip_ref,
+    gain_ref, dx_ref, dgt_ref, dq_ref, heads_ref, vec_ref,
 ):
     length = x_ref.shape[0]
     step = min(256, length)
@@ -250,17 +218,15 @@
     sig = sigmoid(z)
     gate = z * sig * mask
     gy = y * gate
-    do = jnp.where(own_ref[...] > 0.5, do_ref[...], other_ref[...])
+    do = do_ref[...]
     dgy = r * do * gain - gy * pull
     dy = dgy * gate
-    dz_ref[...] = (dgy * y * mask * sig * (1.0 + z * (1.0 - sig))).astype(bf16)
     vec_ref[0:1, :] = jnp.sum(do * gy * r, axis=0, keepdims=True)
     vec_ref[1:2, :] = jnp.sum(dy * x, axis=0, keepdims=True)
     vec_ref[2:8, :] = jnp.zeros((6, 128), f32)
     dyb = dy.astype(bf16)
     entering = (dy * spread(cols, 3, left)).astype(bf16)
     stateb = state_ref[...].astype(bf16)
-    ds_ref[...] = dot(qt_ref[...], entering)
 
     @pl.when(pl.program_id(0) == 0)
     def _():
@@ -315,7 +281,7 @@
 
 
 def inner_kernel(
-    dx_ref, x_ref, cols_ref, k_ref, later_ref, mask_ref, in_ref, rim_ref, taps_ref, out_ref, vec_ref, edge_ref,
+    first, dx_ref, x_ref, cols_ref, k_ref, later_ref, mask_ref, in_ref, rim_ref, taps_ref, out_ref, vec_ref, edge_ref,
     heads_ref, dk_ref, pad_ref, dc_ref,
 ):
     left = first_head(x_ref.shape)
@@ -332,7 +298,7 @@
         dk_ref[...] = jnp.zeros_like(dk_ref)
         heads_ref[...] = jnp.zeros_like(heads_ref)
 
-    note_heads(heads_ref, xu, 0, left)
+    note_heads(heads_ref, xu, first, left)
 
     dk_ref[...] += dot_t((x * tail * steps).astype(bf16), later)
     dact = (dx_ref[...] + steps * u) * mask
@@ -347,16 +313,12 @@
     return pl.BlockSpec((rows, 128), lambda i: (0, i + shift))
 
 
-def turns(rows):
-    return pl.BlockSpec((rows, 128), lambda i: (0, i % (PAIRS // 2)))
-
-
 def whole(rows, width):
     return pl.BlockSpec((rows, width), lambda i: (0, 0))
 
 
-def planes(rows, width):
-    return pl.BlockSpec((1, rows, width), lambda i: (i, 0, 0))
+def planes(rows, width, shift=0):
+    return pl.BlockSpec((1, rows, width), lambda i: (i + shift, 0, 0))
 
 
 def run(kernel, steps, ins, outs, shapes, scratch=()):
@@ -414,12 +376,8 @@
     even_out = even_rows(w_out, count, lead, base)
     weights_x = lax.all_gather(even_in[:, E:], OWNERS, axis=0, tiled=True)
     weights_z = lax.all_gather(even_in[:, :E], OWNERS, axis=0, tiled=True)
-    gather = Gather(even_out, mine, devices, (896, 1792))
-    gather.advance()
-    gather.advance()
-    gather.advance()
-    weights_x = tie(weights_x, gather)
-    gather.advance()
+    tokens_out = split_rows(grad_out, mine, base)
+    weights_x, tokens_out = lax.optimization_barrier((weights_x, tokens_out))
 
     hidden_full = hidden.astype(f32)
     scale = lax.rsqrt(jnp.mean(hidden_full * hidden_full, axis=1, keepdims=True) + norm_eps)
@@ -462,10 +420,12 @@
     weight = jnp.dot((tail * steps).astype(bf16), heads_of, preferred_element_type=f32)
     handed = (act[:, :E].astype(f32) * mask_row * weight).astype(bf16)
     fresh = jnp.dot(keys.T, handed, preferred_element_type=f32)
+    entry = jnp.dot(enter.astype(bf16), heads_of, preferred_element_type=f32).astype(bf16)
+    even_out, weights_z, fresh, cols, rows, scores, entry = lax.optimization_barrier(
+        (even_out, weights_z, fresh, cols, rows, scores, entry)
+    )
+    weights_out = lax.all_gather(even_out, OWNERS, axis=0, tiled=True)
     entered = hand_on(fresh, carry, False)
-    weights_z = tie(weights_z, gather)
-    half_out = gather.result()
-    other_out = exchange(half_out, 0, devices)
     gate_raw = jnp.dot(normed, weights_z, preferred_element_type=f32).astype(bf16)
     y, gated, squares = run(
         forward_kernel,
@@ -476,61 +436,76 @@
     )(act, gate_raw, cols, rows, scores, queries, entered, mask_row, skip_row)
     root = lax.rsqrt(jnp.sum(squares, axis=1, keepdims=True) / active + norm_eps)
     mixed_low = (gated * root * gain_row).astype(bf16)
-    half = E // 2
-    own_at, other_at = (mine % 2) * half, (1 - mine % 2) * half
-
-    def halves(array):
-        return [lax.dynamic_slice_in_dim(array, at, half, 1) for at in (own_at, other_at)]
-
-    out = Reduce(split_rows(grad_out, mine, base), mixed_low, mine, base, devices, (1664, 3328))
-    grad_own = jnp.dot(grad_out, half_out, preferred_element_type=f32)
-    grad_other = jnp.dot(grad_out, other_out, preferred_element_type=f32)
-    grad_own, grad_other = tie((grad_own, grad_other), out)
+    out = Reduce(tokens_out, mixed_low, mine, base, devices, (2048,))
+    weights_out = tie(weights_out, out)
     out.advance()
-    gain_own, gain_other = halves(gain_row)
-    gated_own, gated_other = halves(gated)
-    along_own = jnp.sum(grad_own * gain_own * gated_own, axis=1, keepdims=True)
-    along_other = jnp.sum(grad_other * gain_other * gated_other, axis=1, keepdims=True)
-    pull = root**3 * (along_own + along_other) / active
-    own_row = (jnp.arange(E)[None, :] // half == mine % 2).astype(f32)
+    mixed_grad = jnp.dot(grad_out, weights_out, preferred_element_type=f32)
+    pull = root**3 * jnp.sum(mixed_grad * gain_row * gated, axis=1, keepdims=True) / active
+    gate_full = gate_raw.astype(f32)
+    open_part = sigmoid(gate_full)
+    grad_gated = root * mixed_grad * gain_row - gated * pull
+    grad_gate = grad_gated * y * mask_row * open_part * (1.0 + gate_full * (1.0 - open_part))
+    grad_gate = grad_gate.astype(bf16)
+    entering = (grad_gated * (gate_full * open_part) * mask_row * entry).astype(bf16)
+    grad_entered = jnp.dot(queries.T, entering, preferred_element_type=f32)
+    features = split_rows(normed, mine, base)
+    work_z = Reduce(features, grad_gate, mine, base, devices, (2048,))
+    mixed_grad = tie(mixed_grad, out, work_z)
+    out.advance()
+    work_z.advance()
     tok = jnp.concatenate([root, pull, jnp.zeros((T, 6), f32)], axis=1)
-    grad_gate, grad_x, grad_entered, grad_scores, grad_queries, heads_a, vec_a = run(
+    grad_x, grad_scores, grad_queries, heads_a, vec_a = run(
         backward_kernel,
         PAIRS,
         [
-            turns(T), turns(T), lanes(1), lanes(T), lanes(T), lanes(T), planes(T, 8), planes(4, T), whole(T, T),
-            whole(N, T), lanes(N),
-            whole(T, 8), lanes(1), lanes(1), lanes(1),
+            lanes(T), lanes(T), lanes(T), lanes(T), planes(T, 8), planes(4, T), whole(T, T), lanes(N), whole(T, 8),
+            lanes(1), lanes(1), lanes(1),
         ],
-        [lanes(T), lanes(T), lanes(N), whole(T, T), whole(T, N), whole(T, 128), lanes(8)],
-        [
-            ((T, E), bf16), ((T, E), f32), ((N, E), f32), ((T, T), f32), ((T, N), f32), ((T, 128), f32),
-            ((8, E), f32),
-        ],
-    )(grad_own, grad_other, own_row, y, gate_raw, act, cols, rows, scores.T, queries.T, entered, tok, mask_row, skip_row, gain_row)
-    grad_gate, grad_entered = tie((grad_gate, grad_entered), out)
-    features = split_rows(normed, mine, base)
-    work_z = Reduce(features, grad_gate, mine, base, devices, (1664, 3328))
+        [lanes(T), whole(T, T), whole(T, N), whole(T, 128), lanes(8)],
+        [((T, E), f32), ((T, T), f32), ((T, N), f32), ((T, 128), f32), ((8, E), f32)],
+    )(mixed_grad, y, gate_raw, act, cols, rows, scores.T, entered, tok, mask_row, skip_row, gain_row)
+    later = hand_on(grad_entered, carry, True)
+    grad_x, grad_gate = tie((grad_x, grad_gate), out, work_z)
     out.advance()
+    work_z.advance()
     du = jnp.einsum("tc,dc->td", grad_gate, weights_z, preferred_element_type=f32)
-    later = hand_on(grad_entered, carry, True)
     later, du = tie((later, du), out, work_z)
     out.advance()
     work_z.advance()
     rim8 = jnp.concatenate([jnp.zeros((8 - (K - 1), CW), bf16), rim], axis=0)
     taps = jnp.concatenate([conv_weight, conv_bias[None, :], jnp.zeros((3, CW), f32)], axis=0)
     scratch = (pltpu.VMEM((T + 16, 128), f32), pltpu.VMEM((T + 16, 128), f32))
-    inner, vec_b, edge_b, heads_b, grad_keys = run(
-        inner_kernel,
-        PAIRS,
-        [lanes(T), lanes(T), planes(T, 8), whole(T, N), lanes(N), lanes(1), lanes(T), lanes(8), lanes(8)],
-        [lanes(T), lanes(8), lanes(16), whole(T, 128), whole(T, N)],
-        [((T, E), bf16), ((8, E), f32), ((16, E), f32), ((T, 128), f32), ((T, N), f32)],
-        scratch,
-    )(grad_x, act, cols, keys, later, mask_row, proj_x, rim8, taps)
-    inner, grad_keys = tie((inner, grad_keys), out, work_z)
-    out.advance()
+    part = PAIRS // 2
+
+    def inner_half(shift, later):
+        return run(
+            partial(inner_kernel, 2 * shift),
+            part,
+            [
+                lanes(T, shift), lanes(T, shift), planes(T, 8, shift), whole(T, N), lanes(N, shift), lanes(1, shift),
+                lanes(T, shift), lanes(8, shift), lanes(8, shift),
+            ],
+            [lanes(T), lanes(8), lanes(16), whole(T, 128), whole(T, N)],
+            [((T, E // 2), bf16), ((8, E // 2), f32), ((16, E // 2), f32), ((T, 128), f32), ((T, N), f32)],
+            scratch,
+        )(grad_x, act, cols, keys, later, mask_row, proj_x, rim8, taps)
+
+    def ends_of(edges):
+        route = [(i + 1, i) for i in range(seq_count - 1)]
+        pushed = lax.ppermute(edges[8 - (K - 1) : 8], "seq", route)
+        kept = jnp.zeros((8 - (K - 1), edges.shape[1]), f32)
+        return (edges[8:] + jnp.concatenate([kept, pushed], axis=0)).astype(bf16)
+
+    inner_a, vec_a2, edge_a, heads_b, keys_a = inner_half(0, later)
+    grad_proj_a = lax.dynamic_update_slice(inner_a, ends_of(edge_a), (T - 8, 0))
+    work_a = Reduce(features, grad_proj_a, mine, base, devices, (1024,))
+    later_b = tie(later, out, work_z, work_a)
+    work_a.advance()
+    inner_b, vec_b, edge_b, heads_c, grad_keys = inner_half(part, later_b)
+    inner_b, grad_keys = tie((inner_b, grad_keys), work_a)
     work_z.advance()
+    work_a.advance()
+    grad_keys = grad_keys + keys_a
     pairs_t = jnp.where(allowed.T, grad_scores, 0.0).astype(bf16)
     grad_keys = grad_keys + jnp.dot(pairs_t, queries, preferred_element_type=f32)
     grad_queries = grad_queries + jnp.einsum("st,sn->tn", pairs_t, keys, preferred_element_type=f32)
@@ -542,11 +517,9 @@
         [((T, 2 * N), bf16), ((8, 2 * N), f32), ((16, 2 * N), f32)],
         scratch,
     )(jnp.concatenate([grad_keys, grad_queries], axis=1), proj_x, rim8, taps)
-    edges = jnp.concatenate([edge_b, edge_c], axis=1)
-    pushed = lax.ppermute(edges[8 - (K - 1) : 8], "seq", [(i + 1, i) for i in range(seq_count - 1)])
-    ends = (edges[8:] + jnp.concatenate([jnp.zeros((8 - (K - 1), CW), f32), pushed], axis=0)).astype(bf16)
-
-    along = heads_a[:, H:] + heads_b[:, :H]
+    ends = ends_of(jnp.concatenate([edge_b, edge_c], axis=1))
+
+    along = heads_a[:, H:] + heads_b[:, :H] + heads_c[:, :H]
     leaving = carry * entered + fresh
     crossing = jnp.sum((later * leaving).reshape(N, H, P_SIZE), axis=(0, 2))
     upper = (order[:, None] <= order[None, :]).astype(f32)
@@ -554,20 +527,19 @@
         upper, heads_a[:, :H] - steps * along, precision=lax.Precision.HIGHEST
     )
     grad_raw = (along - rate * grad_logs) * jax.nn.sigmoid(raw)
-    conv_vec = jnp.concatenate([vec_b, vec_c], axis=1)
-    grad_proj = jnp.concatenate([inner, outer, grad_raw.astype(bf16)], axis=1)
+    conv_vec = jnp.concatenate([vec_a2, vec_b, vec_c], axis=1)
+    grad_proj = jnp.concatenate([inner_b, outer, grad_raw.astype(bf16)], axis=1)
     grad_proj = lax.dynamic_update_slice(grad_proj, ends, (T - 8, 0))
-    grad_proj = tie(grad_proj, out, work_z)
-    work_x = Reduce(features, grad_proj, mine, base, devices, (1792, 3584))
-    work_z.advance()
-
-    du = du + jnp.einsum("tc,dc->td", grad_proj, weights_x, preferred_element_type=f32)
-    du, last_low = tie((du, mixed_low), work_x, work_z)
+    grad_proj = tie(grad_proj, work_a, work_z)
+    work_a.advance()
+    work_x = Reduce(features, grad_proj, mine, base, devices, (1024, 2048))
+
+    grad_last, last_low = tie((grad_proj, mixed_low), work_x, work_a)
     work_x.advance()
-    work_z.advance()
-    mixed_own, mixed_other = halves(last_low)
-    branch = jnp.einsum("te,de->td", mixed_own, half_out, preferred_element_type=f32)
-    branch = branch + jnp.einsum("te,de->td", mixed_other, other_out, preferred_element_type=f32)
+    work_a.advance()
+    du = du + jnp.einsum("tc,dc->td", grad_proj_a, weights_x[:, : E // 2], preferred_element_type=f32)
+    du = du + jnp.einsum("tc,dc->td", grad_last, weights_x[:, E // 2 :], preferred_element_type=f32)
+    branch = jnp.einsum("te,de->td", last_low, weights_out, preferred_element_type=f32)
     output = (hidden_full + branch).astype(bf16)
     dug = du * gain_in[None, :]
     inward = jnp.mean(dug * hidden_full, axis=1, keepdims=True)
@@ -584,9 +556,10 @@
         ]
     )
 
-    output, input_grad = tie((output, input_grad), work_x, work_z)
-
-    block_out, block_z, block_x = out.result(), work_z.result(), work_x.result()
+    output, input_grad = tie((output, input_grad), work_x, work_a)
+
+    block_out, block_z = out.result(), work_z.result()
+    block_x = jnp.concatenate([work_a.result(), work_x.result()], axis=1)
     block_in = jnp.concatenate([block_z, block_x], axis=1)
     big_square = jnp.sum(block_in**2) + jnp.sum(block_out**2)
     packed = jnp.concatenate([small_grad, jnp.full((64,), big_square)]).reshape(-1, 128)

time: 1010 us -> 950 us (0.941)
  waiting for transfers between devices: 360 us -> 312 us
  other arithmetic: 125 us -> 104 us
  starting transfers between devices: 86.1 us -> 105 us
  matrix products: 193 us -> 208 us
  local copies, waits for them, and re-layouts: 79.1 us -> 64.9 us
    ppermute x64 -> x50, waiting for transfers between devices: 305 us -> 138 us  [exchange(): lax.ppermute(value, OWNERS, [(i, i ^ 1 << bit) for i in range(devices)])]
    all_gather x1, waiting for transfers between devices: 20.8 us -> 105 us  [local(): weights_x = lax.all_gather(even_in[:, E:], OWNERS, axis=0, tiled=True)]
    all_gather x1, waiting for transfers between devices: 32.8 us -> 66.7 us  [local(): weights_z = lax.all_gather(even_in[:, :E], OWNERS, axis=0, tiled=True)]
    another operation x25 -> x1, other arithmetic: 15.7 us -> 0.18 us  [the longest x24 15.5 us: advance(): jnp.stack([jnp.where(own == 0, value, got), jnp.where(own == 0, got, valu...]
    ppermute x64 -> x50, starting transfers between devices: 63.6 us -> 77.8 us  [exchange(): lax.ppermute(value, OWNERS, [(i, i ^ 1 << bit) for i in range(devices)])]
    dot_general x5 -> x6, matrix products: 55.2 us -> 69.2 us  [the longest x1 18.8 us: local(): mixed_grad = jnp.dot(grad_out, weights_out, preferred_element_type=f32)]
    pallas_call x2 -> x3, Pallas kernels: 93.7 us -> 84.1 us  [the longest x1 47 us: local(): run(backward_kernel, PAIRS, [lanes(T), lanes(T), lanes(T), lanes(T), plan...]
  transfers between devices with their start and end apart: 78 -> 66, of which waited for: 32 -> 33; matrix products, arithmetic and copies ran while one was open for 31% -> 27% of each run, Pallas kernels for 13% -> 11%
where the time goes in v2:
time: 950 us; the launch traced here: 936 us
  waiting for transfers between devices  312 us (33%)
  matrix products  208 us (22%)
  Pallas kernels  120 us (13%)
  starting transfers between devices  105 us (11%)
  other arithmetic  104 us (11%)
  local copies, waits for them, and re-layouts  64.9 us (7%)
  between operations  22.1 us (2%)
    ppermute x50, waiting for transfers between devices, exchange(): lax.ppermute(value, OWNERS, [(i, i ^ 1 << bit) for i in range(devices)])  138 us
    all_gather x1, waiting for transfers between devices, local(): weights_x = lax.all_gather(even_in[:, E:], OWNERS, axis=0, tiled=True)  105 us
    ppermute x50, starting transfers between devices, exchange(): lax.ppermute(value, OWNERS, [(i, i ^ 1 << bit) for i in range(devices)])  77.8 us
    dot_general x18, matrix products, product(): lax.dot_general(features, piece, (((0,), (0,)), ((), ())), preferred_elem...  70.4 us
    all_gather x1, waiting for transfers between devices, local(): weights_z = lax.all_gather(even_in[:, :E], OWNERS, axis=0, tiled=True)  66.7 us
    pallas_call x1, Pallas kernels, local(): run(backward_kernel, PAIRS, [lanes(T), lanes(T), lanes(T), lanes(T), plan...  47 us
    pallas_call x2, Pallas kernels, inner_half(): run(partial(inner_kernel, 2 * shift), part, [lanes(T, shift), lanes(T, sh...  37.1 us
    pallas_call x1, Pallas kernels, local(): run(forward_kernel, PAIRS, [lanes(T), lanes(T), planes(T, 8), planes(4, T...  34.3 us
  transfers between devices with their start and end apart: 66, of which 33 were waited for; matrix products, arithmetic and copies ran while one was open for 27% of the time, Pallas kernels for 11%

profile of v2, /device:TPU:0, one launch (start us, length us, event | category | flops | bytes accessed | tf_op | source)
XLA Modules:
  0.0 935.9 jit_solution(10364912772567929545)
XLA Ops:
  21.4 6.3 collective-permute-start
  31.0 7.4 fusion.52
  41.9 104.5 %all-gather.6.cloned.1.call-done = bf16[2048,4416]{1,0:T(8,128)(2,1)} async-done(((bf16[64,4416]{1,0:T(8,128)(2,1)}), bf16[2048,4416]{1,0:T(8,128)(2,1)}) %all-gather.6.cloned.1.call-update) | async-done | bytes 18087952 | tf_op jit(solution)/shard_map/all_gather | solution.py:377
  146.4 13.9 %convolution_convert_fusion.in_ref = bf16[512,4416]{1,0:T(8,128)(2,1)S(1)} fusion(bf16[2048,4416]{1,0:T(8,128)(2,1)} %all-gather.6.cloned.1.call-done, bf16[512,2048]{1,0:T(8,128)(2,1)S(1)} %copy-done.34, f32[2048]{0:T(1024)S(1)} %slice.205, f32[512]{0:T(512)} %get-tuple-element.215), kind=kOutput, calls=%fused_computation.46 | convolution fusion | flops 9267478528 | bytes 24717312 | tf_op jit(solution)/shard_map/dot_general | solution.py:385
  167.8 3.2 convolution_convert_fusion.2
  174.1 4.7 copy.124
  179.3 3.2 maximum_convert_fusion
  182.6 5.7 multiply_convert_fusion.x_ref
  190.9 4.8 fusion.24
  195.7 66.7 %all-gather.4.cloned.1.call-done = bf16[2048,4096]{1,0:T(8,128)(2,1)} async-done(((bf16[64,4096]{1,0:T(8,128)(2,1)}), bf16[2048,4096]{1,0:T(8,128)(2,1)}) %all-gather.4.cloned.1.call-update) | async-done | bytes 16777232 | tf_op jit(solution)/shard_map/all_gather | solution.py:378
  272.1 3.2 add_convert_fusion.10
  277.1 13.9 %convolution_convert_fusion.1.z_ref = bf16[512,4096]{1,0:T(8,128)(2,1)} fusion(bf16[2048,4096]{1,0:T(8,128)(2,1)} %all-gather.4.cloned.1.call-done, bf16[512,2048]{1,0:T(8,128)(2,1)S(1)} %copy-done.35, f32[2048]{0:T(1024)S(1)} %slice.205, f32[512]{0:T(512)S(1)} %copy-done.108), kind=kOutput, calls=%fused_computation.48 | convolution fusion | flops 8596226048 | bytes 23078912 | tf_op jit(solution)/shard_map/dot_general | solution.py:429
  294.0 2.7 convert_add_fusion.16.state_ref
  296.8 34.3 %shard_map.262 = (f32[512,4096]{1,0:T(8,128)}, f32[512,4096]{1,0:T(8,128)}, f32[512,128]{1,0:T(8,128)S(1)}) custom-call(bf16[512,4352]{1,0:T(8,128)(2,1)} %copy-done.22, bf16[512,4096]{1,0:T(8,128)(2,1)} %convolution_convert_fusion.1.z_ref, f32[32,512,8]{2,1,0:T(8,128)} %bitcast.237, f32[32,4,512]{2,1,0:T(4,128)S(1)} %reshape.362.rows_ref, ...), custom_call_target="tpu_custom_call" | custom-call | tf_op jit(solution)/shard_map/pallas_call | solution.py:430
  332.9 4.9 multiply_convert_fusion.1
  337.9 4.4 convolution_convert_fusion.6
  342.2 15.5 %collective-permute-start.6 = (bf16[1024,2048]{1,0:T(8,128)(2,1)}, bf16[1024,2048]{1,0:T(8,128)(2,1)}, u32[]{:S(2)}, u32[]{:S(2)}) collective-permute-start(bf16[1024,2048]{1,0:T(8,128)(2,1)} %convolution_convert_fusion.6), channel_id=1, source_target_pairs={{0,1},{1,0},{2,3},{3,2},{4,5},{5,4},{6,7},{7,6},{8,9},{9,8},{10,11... | collective-permute-start | bytes 12582920 | tf_op jit(solution)/shard_map/ppermute | solution.py:80
  357.8 4.3 convolution_convert_fusion.5
  364.0 7.9 fusion.47
  371.9 6.8 add_convert_fusion.3
  378.7 6.5 add_convert_fusion.2
  385.3 18.8 %multiply_reduce_fusion = (f32[512]{0:T(512)S(1)}, f32[512,4096]{1,0:T(8,128)}) fusion(f32[512,4096]{1,0:T(8,128)} %get-tuple-element.103, f32[4096]{0:T(1024)S(1)} %slice.229, bf16[512,2048]{1,0:T(8,128)(2,1)} %param.16, bf16[2048,4096]{1,0:T(8,128)(2,1)} %all-gather.8.cloned.1.call-done), kind=kOutput, calls=%fused_computation.39 | convolution fusion | flops 8596226048 | bytes 35670016 | tf_op jit(solution)/shard_map/dot_general | solution.py:442
  404.1 12.0 %add_convert_fusion.9 = (bf16[128,4096]{1,0:T(8,128)(2,1)}, f32[128,4096]{1,0:T(8,128)}) fusion(f32[4096]{0:T(1024)S(1)} %copy-done.97, bf16[512,4096]{1,0:T(8,128)(2,1)S(1)} %copy-done.23, bf16[512,4096]{1,0:T(8,128)(2,1)} %convolution_convert_fusion.2, f32[4096]{0:T(1024)S(1)} %copy-done.95, f32[512,4096]{1,0:T(8,128)} %get-tuple-element.103, ...), kind=kOutput, calls=%fused_computation.127 | convolution fusion | flops 567279616 | bytes 28495872 | tf_op jit(solution)/shard_map/dot_general | solution.py:450
  418.4 3.9 collective-permute-start.8
  425.5 10.6 %fusion.13 = bf16[512,4096]{1,0:T(8,128)(2,1)} fusion(bf16[512,4096]{1,0:T(8,128)(2,1)S(1)} %copy-done.23, f32[512,4096]{1,0:T(8,128)S(1)} %bitcast.242, f32[4096]{0:T(1024)S(1)} %copy-done.95, f32[512,4096]{1,0:T(8,128)} %get-tuple-element.103, f32[512]{0:T(512)S(1)} %fusion.195, f32[4096]{0:T(1024)S(1)} %slice.229, ...), kind=kLoop, calls=%fused_computation.28 | loop fusion | flops 33554432 | bytes 33591296 | tf_op jit(solution)/shard_map/convert_element_type | solution.py:448
  436.0 6.4 convolution_convert_fusion.4
  443.1 4.4 convolution_convert_fusion.3
  460.0 8.7 collective-permute-done.8
  472.6 3.2 fusion.37
  475.8 5.3 add_convert_fusion.1
  481.1 6.1 add_convert_fusion
  491.4 14.0 %collective-permute-start.14 = (bf16[2,2,2,64,2048]{4,3,0,1,2:T(8,128)(2,1)}, bf16[2,2,2,64,2048]{4,3,0,1,2:T(8,128)(2,1)}, u32[]{:S(2)}, u32[]{:S(2)}) collective-permute-start(bf16[2,2,2,64,2048]{4,3,0,1,2:T(8,128)(2,1)} %copy_bitcast_fusion.1), channel_id=1, source_target_pairs={{0,2},{1,3},{2,0},{3,1},{4,6},{5,7},{6,4},{7,5},{8,10},{9,11},{10,... | collective-permute-start | bytes 6291464 | tf_op jit(solution)/shard_map/ppermute | solution.py:80
  505.4 3.0 convert_add_fusion.15.later_ref
  511.4 47.0 %shard_map.263 = (f32[512,4096]{1,0:T(8,128)}, f32[512,512]{1,0:T(8,128)S(1)}, f32[512,128]{1,0:T(8,128)S(1)}, f32[512,128]{1,0:T(8,128)S(1)}, f32[8,4096]{1,0:T(8,128)S(1)}) custom-call(f32[512,4096]{1,0:T(8,128)} %get-tuple-element.109.do_ref, f32[512,4096]{1,0:T(8,128)} %get-tuple-element.108.y_ref, bf16[512,4096]{1,0:T(8,128)(2,1)} %convolution_convert_fusion.1.z_ref, ...), custom_call_target="tpu_custom_call" | custom-call | tf_op jit(solution)/shard_map/pallas_call | solution.py:457
  569.1 4.9 collective-permute-done.13
  580.8 15.0 %fusion.226 = f32[512,2048]{1,0:T(8,128)} fusion(bf16[512,4096]{1,0:T(8,128)(2,1)} %fusion.13, bf16[2048,4096]{1,0:T(8,128)(2,1)} %all-gather.4.cloned.1.call-done), kind=kOutput, calls=%fused_computation.424 | convolution fusion | flops 8589934592 | bytes 25165824 | tf_op jit(solution)/shard_map/tc,dc->td/dot_general | solution.py:471
  601.3 9.4 %collective-permute-done.19 = bf16[2,64,2048]{2,1,0:T(8,128)(2,1)S(1)} collective-permute-done((bf16[2,64,2048]{2,1,0:T(8,128)(2,1)S(1)}, bf16[2,64,2048]{2,1,0:T(8,128)(2,1)S(1)}, u32[]{:S(2)}, u32[]{:S(2)}) %collective-permute-start.19) | collective-permute-done | bytes 524320 | tf_op jit(solution)/shard_map/ppermute | solution.py:80
  610.9 10.6 %collective-permute-done.20 = bf16[2,64,2048]{2,1,0:T(8,128)(2,1)S(1)} collective-permute-done((bf16[2,64,2048]{2,1,0:T(8,128)(2,1)S(1)}, bf16[2,64,2048]{2,1,0:T(8,128)(2,1)S(1)}, u32[]{:S(2)}, u32[]{:S(2)}) %collective-permute-start.20) | collective-permute-done | bytes 524320 | tf_op jit(solution)/shard_map/ppermute | solution.py:80
  635.9 18.5 %shard_map.264 = (bf16[512,2048]{1,0:T(8,128)(2,1)S(1)}, f32[8,2048]{1,0:T(8,128)S(1)}, f32[16,2048]{1,0:T(8,128)S(1)}, f32[512,128]{1,0:T(8,128)S(1)}, f32[512,128]{1,0:T(8,128)S(1)}) custom-call(f32[512,4096]{1,0:T(8,128)} %get-tuple-element.115.dx_ref, bf16[512,4352]{1,0:T(8,128)(2,1)} %copy-done.22, f32[32,512,8]{2,1,0:T(8,128)} %bitcast.239, ...), custom_call_target="tpu_custom_call" | custom-call | tf_op jit(solution)/shard_map/pallas_call | solution.py:481
  659.5 9.6 %fusion.20 = f32[512,2048]{1,0:T(8,128)} fusion(bf16[512,2048]{1,0:T(8,128)(2,1)S(1)} %fusion.178, bf16[2048,4416]{1,0:T(8,128)(2,1)} %all-gather.6.cloned.1.call-done), kind=kOutput, calls=%fused_computation.34 | convolution fusion | flops 4294967296 | bytes 14680064 | tf_op jit(solution)/shard_map/tc,dc->td/dot_general | solution.py:540
  680.9 18.6 %shard_map.265 = (bf16[512,2048]{1,0:T(8,128)(2,1)S(1)}, f32[8,2048]{1,0:T(8,128)S(1)}, f32[16,2048]{1,0:T(8,128)S(1)}, f32[512,128]{1,0:T(8,128)S(1)}, f32[512,128]{1,0:T(8,128)S(1)}) custom-call(f32[512,4096]{1,0:T(8,128)} %get-tuple-element.115.dx_ref, bf16[512,4352]{1,0:T(8,128)(2,1)} %copy-done.22, f32[32,512,8]{2,1,0:T(8,128)} %bitcast.240, ...), custom_call_target="tpu_custom_call" | custom-call | tf_op jit(solution)/shard_map/pallas_call | solution.py:481
  709.5 14.4 %collective-permute-done.35 = bf16[64,2048]{1,0:T(8,128)(2,1)S(1)} collective-permute-done((bf16[64,2048]{1,0:T(8,128)(2,1)S(1)}, bf16[64,2048]{1,0:T(8,128)(2,1)S(1)}, u32[]{:S(2)}, u32[]{:S(2)}) %collective-permute-start.35) | collective-permute-done | bytes 262176 | tf_op jit(solution)/shard_map/ppermute | solution.py:80
  724.7 3.9 collective-permute-done.36
  742.6 8.0 collective-permute-done.33
  753.7 4.0 convolution_convert_fusion.8
  763.8 7.0 collective-permute-done.40
  771.6 4.3 collective-permute-done.41
  780.4 5.0 add_convert_fusion.5
  785.4 4.7 add_convert_fusion.4
  790.1 13.4 %fusion.28 = bf16[512,2048]{1,0:T(8,128)(2,1)} fusion(bf16[512,2048]{1,0:T(8,128)(2,1)S(1)} %copy-done.36, bf16[512,4096]{1,0:T(8,128)(2,1)S(1)} %copy-done.55, bf16[2048,4096]{1,0:T(8,128)(2,1)} %all-gather.8.cloned.1.call-done), kind=kOutput, calls=%fused_computation.55 | convolution fusion | flops 8593080320 | bytes 25165824 | tf_op jit(solution)/shard_map/te,de->td/dot_general | solution.py:542
  803.5 12.1 %fusion.33 = (f32[2048]{0:T(1024)S(1)}, f32[512]{0:T(512)S(1)}, f32[512,2048]{1,0:T(8,128)S(1)}) fusion(bf16[512,2048]{1,0:T(8,128)(2,1)S(1)} %copy-done.36, f32[512]{0:T(512)S(1)} %copy-done.109, f32[2048]{0:T(1024)S(1)} %copy-done.102, f32[512,2048]{1,0:T(8,128)} %fusion.226, f32[512,2048]{1,0:T(8,128)} %fusion.20, bf16[512,2368]{1,0:T(8,128)(2,1)} %fusion.177, ...), kind=kOutput, calls=%fused_computation.60 | convolution fusion | flops 4975490560 | bytes 27152384 | tf_op jit(solution)/shard_map/tc,dc->td/dot_general | solution.py:541
  823.2 3.3 fusion.30
  826.6 5.7 collective-permute-done.45
  835.7 6.2 collective-permute-done.42
  846.8 8.1 collective-permute-done.53
  855.9 4.5 collective-permute-done.54
  864.3 8.3 collective-permute-done.48
  872.8 3.0 collective-permute-done.51
  876.1 6.9 collective-permute-done.49
  890.8 4.2 collective-permute-done.58
  896.3 3.6 collective-permute-done.59
  900.0 4.8 collective-permute-done.60
  914.9 8.3 multiply_subtract_fusion.1
  924.0 4.1 multiply_subtract_fusion.2
  (588 shorter events, 211.3 us)
Async XLA Ops:
  7.2 139.3 %all-gather.6.cloned.1.call-start = ((), (), s32[]{:S(2)}) async-start(), calls=%async_computation.1 | async-start | bytes 18923520 | tf_op jit(solution)/shard_map/all_gather | solution.py:377
  10.2 4.5 collective-permute-start.1
  18.7 243.7 %all-gather.4.cloned.1.call-start = ((), (), s32[]{:S(2)}) async-start(), calls=%async_computation | async-start | bytes 17301504 | tf_op jit(solution)/shard_map/all_gather | solution.py:378
  20.7 364.6 %all-gather.8.cloned.1.call-start = ((), (), s32[]{:S(2)}) async-start(), calls=%async_computation.2 | async-start | bytes 17301504 | tf_op jit(solution)/shard_map/all_gather | solution.py:427
  21.4 19.6 %collective-permute-start = (bf16[16,4096]{1,0:T(8,128)(2,1)}, bf16[16,4096]{1,0:T(8,128)(2,1)}, u32[]{:S(2)}, u32[]{:S(2)}) collective-permute-start(bf16[16,4096]{1,0:T(8,128)(2,1)} %dynamic-slice_convert_fusion.17), channel_id=1, source_target_pairs={{0,1},{1,2},{2,3},{3,4},{4,5},{5,6},{6,7},{7,8},{8,9},{9,10},{10,1... | collective-permute-start | bytes 393224 | tf_op jit(solution)/shard_map/ppermute | solution.py:65
  164.1 15.3 %collective-permute-start.2 = (bf16[3,4352]{1,0:T(4,128)(2,1)S(1)}, bf16[3,4352]{1,0:T(4,128)(2,1)S(1)}, u32[]{:S(2)}, u32[]{:S(2)}) collective-permute-start(bf16[3,4352]{1,0:T(4,128)(2,1)S(1)} %slice.263), channel_id=1, source_target_pairs={{0,1},{1,2},{2,3},{4,5},{5,6},{6,7},{8,9},{9,10},{10,11},{12,13},{... | collective-permute-start | bytes 78344 | tf_op jit(solution)/shard_map/ppermute | solution.py:389
  264.2 4.6 collective-permute-start.3
  275.3 18.7 %collective-permute-start.5 = (bf16[128,4096]{1,0:T(8,128)(2,1)}, bf16[128,4096]{1,0:T(8,128)(2,1)}, u32[]{:S(2)}, u32[]{:S(2)}) collective-permute-start(bf16[128,4096]{1,0:T(8,128)(2,1)} %add_convert_fusion.10), channel_id=1, source_target_pairs={{2,3},{6,7},{10,11},{14,15},{18,19},{22,23},{26,27},{30,31}} | collective-permute-start | bytes 3145736 | tf_op jit(solution)/shard_map/ppermute | solution.py:342
  342.2 29.7 %collective-permute-start.6 = (bf16[1024,2048]{1,0:T(8,128)(2,1)}, bf16[1024,2048]{1,0:T(8,128)(2,1)}, u32[]{:S(2)}, u32[]{:S(2)}) collective-permute-start(bf16[1024,2048]{1,0:T(8,128)(2,1)} %convolution_convert_fusion.6), channel_id=1, source_target_pairs={{0,1},{1,0},{2,3},{3,2},{4,5},{5,4},{6,7},{7,6},{8,9},{9,8},{10,11... | collective-permute-start | bytes 12582920 | tf_op jit(solution)/shard_map/ppermute | solution.py:80
  362.1 16.6 %collective-permute-start.7 = (bf16[1024,2048]{1,0:T(8,128)(2,1)}, bf16[1024,2048]{1,0:T(8,128)(2,1)}, u32[]{:S(2)}, u32[]{:S(2)}) collective-permute-start(bf16[1024,2048]{1,0:T(8,128)(2,1)} %convolution_convert_fusion.5), channel_id=1, source_target_pairs={{0,1},{1,0},{2,3},{3,2},{4,5},{5,4},{6,7},{7,6},{8,9},{9,8},{10,11... | collective-permute-start | bytes 12582920 | tf_op jit(solution)/shard_map/ppermute | solution.py:80
  416.1 31.4 %collective-permute-start.16 = (bf16[128,4096]{1,0:T(8,128)(2,1)}, bf16[128,4096]{1,0:T(8,128)(2,1)S(1)}, u32[]{:S(2)}, u32[]{:S(2)}) collective-permute-start(bf16[128,4096]{1,0:T(8,128)(2,1)} %get-tuple-element.218), channel_id=1, source_target_pairs={{3,2},{7,6},{11,10},{15,14},{19,18},{23,22},{27,26},{31,30}} | collective-permute-start | bytes 3145736 | tf_op jit(solution)/shard_map/ppermute | solution.py:342
  418.4 50.2 %collective-permute-start.8 = (bf16[2,2,2,64,2048]{4,3,0,1,2:T(8,128)(2,1)}, bf16[2,2,2,64,2048]{4,3,0,1,2:T(8,128)(2,1)}, u32[]{:S(2)}, u32[]{:S(2)}) collective-permute-start(bf16[2,2,2,64,2048]{4,3,0,1,2:T(8,128)(2,1)} %copy_bitcast_fusion.3), channel_id=1, source_target_pairs={{0,2},{1,3},{2,0},{3,1},{4,6},{5,7},{6,4},{7,5},{8,10},{9,11},{10,... | collective-permute-start | bytes 6291464 | tf_op jit(solution)/shard_map/ppermute | solution.py:80
  423.8 48.8 %collective-permute-start.9 = (bf16[2,2,2,64,2048]{4,3,0,1,2:T(8,128)(2,1)}, bf16[2,2,2,64,2048]{4,3,0,1,2:T(8,128)(2,1)}, u32[]{:S(2)}, u32[]{:S(2)}) collective-permute-start(bf16[2,2,2,64,2048]{4,3,0,1,2:T(8,128)(2,1)} %copy_bitcast_fusion.2), channel_id=1, source_target_pairs={{0,4},{1,5},{2,6},{3,7},{4,0},{5,1},{6,2},{7,3},{8,12},{9,13},{10,... | collective-permute-start | bytes 6291464 | tf_op jit(solution)/shard_map/ppermute | solution.py:80
  442.4 33.3 %collective-permute-start.10 = (bf16[1024,2048]{1,0:T(8,128)(2,1)}, bf16[1024,2048]{1,0:T(8,128)(2,1)}, u32[]{:S(2)}, u32[]{:S(2)}) collective-permute-start(bf16[1024,2048]{1,0:T(8,128)(2,1)} %convolution_convert_fusion.4), channel_id=1, source_target_pairs={{0,1},{1,0},{2,3},{3,2},{4,5},{5,4},{6,7},{7,6},{8,9},{9,8},{10,11... | collective-permute-start | bytes 12582920 | tf_op jit(solution)/shard_map/ppermute | solution.py:80
  447.5 33.7 %collective-permute-start.11 = (bf16[1024,2048]{1,0:T(8,128)(2,1)}, bf16[1024,2048]{1,0:T(8,128)(2,1)}, u32[]{:S(2)}, u32[]{:S(2)}) collective-permute-start(bf16[1024,2048]{1,0:T(8,128)(2,1)} %convolution_convert_fusion.3), channel_id=1, source_target_pairs={{0,1},{1,0},{2,3},{3,2},{4,5},{5,4},{6,7},{7,6},{8,9},{9,8},{10,11... | collective-permute-start | bytes 12582920 | tf_op jit(solution)/shard_map/ppermute | solution.py:80
  448.8 6.7 collective-permute-start.17
  458.3 47.1 %collective-permute-start.18 = (bf16[128,4096]{1,0:T(8,128)(2,1)S(1)}, bf16[128,4096]{1,0:T(8,128)(2,1)S(1)}, u32[]{:S(2)}, u32[]{:S(2)}) collective-permute-start(bf16[128,4096]{1,0:T(8,128)(2,1)S(1)} %add_convert_fusion.8), channel_id=1, source_target_pairs={{1,0},{5,4},{9,8},{13,12},{17,16},{21,20},{25,24},{29,28}} | collective-permute-start | bytes 3145736 | tf_op jit(solution)/shard_map/ppermute | solution.py:342
  488.3 79.2 %collective-permute-start.12 = (bf16[2,2,64,2048]{3,2,0,1:T(8,128)(2,1)}, bf16[2,2,64,2048]{3,2,0,1:T(8,128)(2,1)}, u32[]{:S(2)}, u32[]{:S(2)}) collective-permute-start(bf16[2,2,64,2048]{3,2,0,1:T(8,128)(2,1)} %dynamic-slice_bitcast_fusion.3), channel_id=1, source_target_pairs={{0,4},{1,5},{2,6},{3,7},{4,0},{5,1},{6,2},{7,3},{8,12},{9,13},{10,... | collective-permute-start | bytes 3145736 | tf_op jit(solution)/shard_map/ppermute | solution.py:80
  491.4 84.2 %collective-permute-start.14 = (bf16[2,2,2,64,2048]{4,3,0,1,2:T(8,128)(2,1)}, bf16[2,2,2,64,2048]{4,3,0,1,2:T(8,128)(2,1)}, u32[]{:S(2)}, u32[]{:S(2)}) collective-permute-start(bf16[2,2,2,64,2048]{4,3,0,1,2:T(8,128)(2,1)} %copy_bitcast_fusion.1), channel_id=1, source_target_pairs={{0,2},{1,3},{2,0},{3,1},{4,6},{5,7},{6,4},{7,5},{8,10},{9,11},{10,... | collective-permute-start | bytes 6291464 | tf_op jit(solution)/shard_map/ppermute | solution.py:80
  509.4 64.7 %collective-permute-start.13 = (bf16[2,2,64,2048]{3,2,0,1:T(8,128)(2,1)}, bf16[2,2,64,2048]{3,2,0,1:T(8,128)(2,1)}, u32[]{:S(2)}, u32[]{:S(2)}) collective-permute-start(bf16[2,2,64,2048]{3,2,0,1:T(8,128)(2,1)} %dynamic-slice_bitcast_fusion.2), channel_id=1, source_target_pairs={{0,2},{1,3},{2,0},{3,1},{4,6},{5,7},{6,4},{7,5},{8,10},{9,11},{10,... | collective-permute-start | bytes 3145736 | tf_op jit(solution)/shard_map/ppermute | solution.py:80
  510.9 67.3 %collective-permute-start.15 = (bf16[2,2,2,64,2048]{4,3,0,1,2:T(8,128)(2,1)}, bf16[2,2,2,64,2048]{4,3,0,1,2:T(8,128)(2,1)}, u32[]{:S(2)}, u32[]{:S(2)}) collective-permute-start(bf16[2,2,2,64,2048]{4,3,0,1,2:T(8,128)(2,1)} %copy_bitcast_fusion), channel_id=1, source_target_pairs={{0,4},{1,5},{2,6},{3,7},{4,0},{5,1},{6,2},{7,3},{8,12},{9,13},{10,... | collective-permute-start | bytes 6291464 | tf_op jit(solution)/shard_map/ppermute | solution.py:80
  595.9 14.9 %collective-permute-start.19 = (bf16[2,64,2048]{2,1,0:T(8,128)(2,1)S(1)}, bf16[2,64,2048]{2,1,0:T(8,128)(2,1)S(1)}, u32[]{:S(2)}, u32[]{:S(2)}) collective-permute-start(bf16[2,64,2048]{2,1,0:T(8,128)(2,1)S(1)} %fusion.120), channel_id=1, source_target_pairs={{0,8},{1,9},{2,10},{3,11},{4,12},{5,13},{6,14},{7,15},{8,0},{9,1},... | collective-permute-start | bytes 1572872 | tf_op jit(solution)/shard_map/ppermute | solution.py:80
  596.1 25.3 %collective-permute-start.20 = (bf16[2,64,2048]{2,1,0:T(8,128)(2,1)S(1)}, bf16[2,64,2048]{2,1,0:T(8,128)(2,1)S(1)}, u32[]{:S(2)}, u32[]{:S(2)}) collective-permute-start(bf16[2,64,2048]{2,1,0:T(8,128)(2,1)S(1)} %fusion.121), channel_id=1, source_target_pairs={{0,8},{1,9},{2,10},{3,11},{4,12},{5,13},{6,14},{7,15},{8,0},{9,1},... | collective-permute-start | bytes 1572872 | tf_op jit(solution)/shard_map/ppermute | solution.py:80
  598.2 25.0 %collective-permute-start.21 = (bf16[2,2,64,2048]{3,2,0,1:T(8,128)(2,1)S(1)}, bf16[2,2,64,2048]{3,2,0,1:T(8,128)(2,1)S(1)}, u32[]{:S(2)}, u32[]{:S(2)}) collective-permute-start(bf16[2,2,64,2048]{3,2,0,1:T(8,128)(2,1)S(1)} %dynamic-slice_bitcast_fusion.1), channel_id=1, source_target_pairs={{0,4},{1,5},{2,6},{3,7},{4,0},{5,1},{6,2},{7,3},{8,12},{9,13},{10,... | collective-permute-start | bytes 3145736 | tf_op jit(solution)/shard_map/ppermute | solution.py:80
  598.7 26.1 %collective-permute-start.22 = (bf16[2,2,64,2048]{3,2,0,1:T(8,128)(2,1)S(1)}, bf16[2,2,64,2048]{3,2,0,1:T(8,128)(2,1)S(1)}, u32[]{:S(2)}, u32[]{:S(2)}) collective-permute-start(bf16[2,2,64,2048]{3,2,0,1:T(8,128)(2,1)S(1)} %dynamic-slice_bitcast_fusion), channel_id=1, source_target_pairs={{0,2},{1,3},{2,0},{3,1},{4,6},{5,7},{6,4},{7,5},{8,10},{9,11},{10,... | collective-permute-start | bytes 3145736 | tf_op jit(solution)/shard_map/ppermute | solution.py:80
  630.1 42.7 %collective-permute-start.23 = (bf16[64,2048]{1,0:T(8,128)(2,1)S(1)}, bf16[64,2048]{1,0:T(8,128)(2,1)S(1)}, u32[]{:S(2)}, u32[]{:S(2)}) collective-permute-start(bf16[64,2048]{1,0:T(8,128)(2,1)S(1)} %fusion.146), channel_id=1, source_target_pairs={{0,16},{1,17},{2,18},{3,19},{4,20},{5,21},{6,22},{7,23},{8,24},{9,... | collective-permute-start | bytes 786440 | tf_op jit(solution)/shard_map/ppermute | solution.py:80
  632.7 40.2 %collective-permute-start.24 = (bf16[64,2048]{1,0:T(8,128)(2,1)S(1)}, bf16[64,2048]{1,0:T(8,128)(2,1)S(1)}, u32[]{:S(2)}, u32[]{:S(2)}) collective-permute-start(bf16[64,2048]{1,0:T(8,128)(2,1)S(1)} %fusion.147), channel_id=1, source_target_pairs={{0,16},{1,17},{2,18},{3,19},{4,20},{5,21},{6,22},{7,23},{8,24},{9,... | collective-permute-start | bytes 786440 | tf_op jit(solution)/shard_map/ppermute | solution.py:80
  635.5 37.5 %collective-permute-start.25 = (bf16[2,64,2048]{2,1,0:T(8,128)(2,1)S(1)}, bf16[2,64,2048]{2,1,0:T(8,128)(2,1)S(1)}, u32[]{:S(2)}, u32[]{:S(2)}) collective-permute-start(bf16[2,64,2048]{2,1,0:T(8,128)(2,1)S(1)} %fusion.122), channel_id=1, source_target_pairs={{0,8},{1,9},{2,10},{3,11},{4,12},{5,13},{6,14},{7,15},{8,0},{9,1},... | collective-permute-start | bytes 1572872 | tf_op jit(solution)/shard_map/ppermute | solution.py:80
  654.5 3.7 collective-permute-start.27
  656.3 18.1 %collective-permute-start.26 = (bf16[2,64,2048]{2,1,0:T(8,128)(2,1)S(1)}, bf16[2,64,2048]{2,1,0:T(8,128)(2,1)S(1)}, u32[]{:S(2)}, u32[]{:S(2)}) collective-permute-start(bf16[2,64,2048]{2,1,0:T(8,128)(2,1)S(1)} %fusion.123), channel_id=1, source_target_pairs={{0,8},{1,9},{2,10},{3,11},{4,12},{5,13},{6,14},{7,15},{8,0},{9,1},... | collective-permute-start | bytes 1572872 | tf_op jit(solution)/shard_map/ppermute | solution.py:80
  669.1 6.1 collective-permute-start.28
  672.8 5.5 collective-permute-start.29
  701.0 28.5 %collective-permute-start.30 = (bf16[2,2,2,64,1024]{4,3,0,1,2:T(8,128)(2,1)S(1)}, bf16[2,2,2,64,1024]{4,3,0,1,2:T(8,128)(2,1)S(1)}, u32[]{:S(2)}, u32[]{:S(2)}) collective-permute-start(bf16[2,2,2,64,1024]{4,3,0,1,2:T(8,128)(2,1)S(1)} %copy_bitcast_fusion.7), channel_id=1, source_target_pairs={{0,2},{1,3},{2,0},{3,1},{4,6},{5,7},{6,4},{7,5},{8,10},{9,11},{10,... | collective-permute-start | bytes 3145736 | tf_op jit(solution)/shard_map/ppermute | solution.py:80
  701.9 28.0 %collective-permute-start.31 = (bf16[2,2,2,64,1024]{4,3,0,1,2:T(8,128)(2,1)S(1)}, bf16[2,2,2,64,1024]{4,3,0,1,2:T(8,128)(2,1)S(1)}, u32[]{:S(2)}, u32[]{:S(2)}) collective-permute-start(bf16[2,2,2,64,1024]{4,3,0,1,2:T(8,128)(2,1)S(1)} %copy_bitcast_fusion.6), channel_id=1, source_target_pairs={{0,4},{1,5},{2,6},{3,7},{4,0},{5,1},{6,2},{7,3},{8,12},{9,13},{10,... | collective-permute-start | bytes 3145736 | tf_op jit(solution)/shard_map/ppermute | solution.py:80
  702.5 21.3 %collective-permute-start.35 = (bf16[64,2048]{1,0:T(8,128)(2,1)S(1)}, bf16[64,2048]{1,0:T(8,128)(2,1)S(1)}, u32[]{:S(2)}, u32[]{:S(2)}) collective-permute-start(bf16[64,2048]{1,0:T(8,128)(2,1)S(1)} %fusion.148), channel_id=1, source_target_pairs={{0,16},{1,17},{2,18},{3,19},{4,20},{5,21},{6,22},{7,23},{8,24},{9,... | collective-permute-start | bytes 786440 | tf_op jit(solution)/shard_map/ppermute | solution.py:80
  704.1 24.5 %collective-permute-start.36 = (bf16[64,2048]{1,0:T(8,128)(2,1)S(1)}, bf16[64,2048]{1,0:T(8,128)(2,1)S(1)}, u32[]{:S(2)}, u32[]{:S(2)}) collective-permute-start(bf16[64,2048]{1,0:T(8,128)(2,1)S(1)} %fusion.149), channel_id=1, source_target_pairs={{0,16},{1,17},{2,18},{3,19},{4,20},{5,21},{6,22},{7,23},{8,24},{9,... | collective-permute-start | bytes 786440 | tf_op jit(solution)/shard_map/ppermute | solution.py:80
  733.3 8.7 collective-permute-start.32
  735.6 15.0 %collective-permute-start.33 = (bf16[2,2,64,1024]{3,2,0,1:T(8,128)(2,1)}, bf16[2,2,64,1024]{3,2,0,1:T(8,128)(2,1)}, u32[]{:S(2)}, u32[]{:S(2)}) collective-permute-start(bf16[2,2,64,1024]{3,2,0,1:T(8,128)(2,1)} %dynamic-slice_bitcast_fusion.7), channel_id=1, source_target_pairs={{0,4},{1,5},{2,6},{3,7},{4,0},{5,1},{6,2},{7,3},{8,12},{9,13},{10,... | collective-permute-start | bytes 1572872 | tf_op jit(solution)/shard_map/ppermute | solution.py:80
  737.5 14.9 %collective-permute-start.34 = (bf16[2,2,64,1024]{3,2,0,1:T(8,128)(2,1)}, bf16[2,2,64,1024]{3,2,0,1:T(8,128)(2,1)S(1)}, u32[]{:S(2)}, u32[]{:S(2)}) collective-permute-start(bf16[2,2,64,1024]{3,2,0,1:T(8,128)(2,1)} %dynamic-slice_bitcast_fusion.6), channel_id=1, source_target_pairs={{0,2},{1,3},{2,0},{3,1},{4,6},{5,7},{6,4},{7,5},{8,10},{9,11},{10,... | collective-permute-start | bytes 1572872 | tf_op jit(solution)/shard_map/ppermute | solution.py:80
  757.7 22.7 %collective-permute-start.37 = (bf16[1024,1024]{1,0:T(8,128)(2,1)}, bf16[1024,1024]{1,0:T(8,128)(2,1)}, u32[]{:S(2)}, u32[]{:S(2)}) collective-permute-start(bf16[1024,1024]{1,0:T(8,128)(2,1)} %convolution_convert_fusion.8), channel_id=1, source_target_pairs={{0,1},{1,0},{2,3},{3,2},{4,5},{5,4},{6,7},{7,6},{8,9},{9,8},{10,11... | collective-permute-start | bytes 6291464 | tf_op jit(solution)/shard_map/ppermute | solution.py:80
  760.3 25.1 %collective-permute-start.38 = (bf16[1024,1024]{1,0:T(8,128)(2,1)}, bf16[1024,1024]{1,0:T(8,128)(2,1)}, u32[]{:S(2)}, u32[]{:S(2)}) collective-permute-start(bf16[1024,1024]{1,0:T(8,128)(2,1)} %convolution_convert_fusion.7), channel_id=1, source_target_pairs={{0,1},{1,0},{2,3},{3,2},{4,5},{5,4},{6,7},{7,6},{8,9},{9,8},{10,11... | collective-permute-start | bytes 6291464 | tf_op jit(solution)/shard_map/ppermute | solution.py:80
  761.3 15.4 %collective-permute-start.39 = (bf16[1024,320]{0,1:T(8,128)(2,1)S(1)}, bf16[1024,320]{0,1:T(8,128)(2,1)S(1)}, u32[]{:S(2)}, u32[]{:S(2)}) collective-permute-start(bf16[1024,320]{0,1:T(8,128)(2,1)S(1)} %convolution_convert_fusion.11), channel_id=1, source_target_pairs={{0,1},{1,0},{2,3},{3,2},{4,5},{5,4},{6,7},{7,6},{8,9},{9,8},{10,11... | collective-permute-start | bytes 1966088 | tf_op jit(solution)/shard_map/ppermute | solution.py:80
  761.5 9.2 collective-permute-start.40
  761.6 14.3 %collective-permute-start.41 = (bf16[2,64,1024]{2,1,0:T(8,128)(2,1)S(1)}, bf16[2,64,1024]{2,1,0:T(8,128)(2,1)S(1)}, u32[]{:S(2)}, u32[]{:S(2)}) collective-permute-start(bf16[2,64,1024]{2,1,0:T(8,128)(2,1)S(1)} %fusion.151), channel_id=1, source_target_pairs={{0,8},{1,9},{2,10},{3,11},{4,12},{5,13},{6,14},{7,15},{8,0},{9,1},... | collective-permute-start | bytes 786440 | tf_op jit(solution)/shard_map/ppermute | solution.py:80
  817.1 24.7 %collective-permute-start.42 = (bf16[2,2,2,64,1024]{4,3,0,1,2:T(8,128)(2,1)S(1)}, bf16[2,2,2,64,1024]{4,3,0,1,2:T(8,128)(2,1)S(1)}, u32[]{:S(2)}, u32[]{:S(2)}) collective-permute-start(bf16[2,2,2,64,1024]{4,3,0,1,2:T(8,128)(2,1)S(1)} %copy_bitcast_fusion.5), channel_id=1, source_target_pairs={{0,2},{1,3},{2,0},{3,1},{4,6},{5,7},{6,4},{7,5},{8,10},{9,11},{10,... | collective-permute-start | bytes 3145736 | tf_op jit(solution)/shard_map/ppermute | solution.py:80
  818.7 24.5 %collective-permute-start.43 = (bf16[2,2,2,64,1024]{4,3,0,1,2:T(8,128)(2,1)S(1)}, bf16[2,2,2,64,1024]{4,3,0,1,2:T(8,128)(2,1)S(1)}, u32[]{:S(2)}, u32[]{:S(2)}) collective-permute-start(bf16[2,2,2,64,1024]{4,3,0,1,2:T(8,128)(2,1)S(1)} %copy_bitcast_fusion.4), channel_id=1, source_target_pairs={{0,4},{1,5},{2,6},{3,7},{4,0},{5,1},{6,2},{7,3},{8,12},{9,13},{10,... | collective-permute-start | bytes 3145736 | tf_op jit(solution)/shard_map/ppermute | solution.py:80
  819.8 15.8 %collective-permute-start.44 = (bf16[2,2,2,64,320]{4,3,2,1,0:T(8,128)(2,1)S(1)}, bf16[2,2,2,64,320]{4,3,2,1,0:T(8,128)(2,1)S(1)}, u32[]{:S(2)}, u32[]{:S(2)}) collective-permute-start(bf16[2,2,2,64,320]{4,3,2,1,0:T(8,128)(2,1)S(1)} %dynamic-slice_bitcast_fusion.8), channel_id=1, source_target_pairs={{0,8},{1,9},{2,10},{3,11},{4,12},{5,13},{6,14},{7,15},{8,0},{9,1},... | collective-permute-start | bytes 983048 | tf_op jit(solution)/shard_map/ppermute | solution.py:80
  820.1 12.1 %collective-permute-start.45 = (bf16[64,1024]{1,0:T(8,128)(2,1)S(1)}, bf16[64,1024]{1,0:T(8,128)(2,1)S(1)}, u32[]{:S(2)}, u32[]{:S(2)}) collective-permute-start(bf16[64,1024]{1,0:T(8,128)(2,1)S(1)} %fusion.163), channel_id=1, source_target_pairs={{0,16},{1,17},{2,18},{3,19},{4,20},{5,21},{6,22},{7,23},{8,24},{9,... | collective-permute-start | bytes 393224 | tf_op jit(solution)/shard_map/ppermute | solution.py:80
  822.8 10.9 %collective-permute-start.46 = (bf16[64,1024]{1,0:T(8,128)(2,1)S(1)}, bf16[64,1024]{1,0:T(8,128)(2,1)S(1)}, u32[]{:S(2)}, u32[]{:S(2)}) collective-permute-start(bf16[64,1024]{1,0:T(8,128)(2,1)S(1)} %fusion.164), channel_id=1, source_target_pairs={{0,16},{1,17},{2,18},{3,19},{4,20},{5,21},{6,22},{7,23},{8,24},{9,... | collective-permute-start | bytes 393224 | tf_op jit(solution)/shard_map/ppermute | solution.py:80
  843.7 18.1 %collective-permute-start.47 = (bf16[2,2,64,1024]{3,2,0,1:T(8,128)(2,1)S(1)}, bf16[2,2,64,1024]{3,2,0,1:T(8,128)(2,1)S(1)}, u32[]{:S(2)}, u32[]{:S(2)}) collective-permute-start(bf16[2,2,64,1024]{3,2,0,1:T(8,128)(2,1)S(1)} %dynamic-slice_bitcast_fusion.5), channel_id=1, source_target_pairs={{0,4},{1,5},{2,6},{3,7},{4,0},{5,1},{6,2},{7,3},{8,12},{9,13},{10,... | collective-permute-start | bytes 1572872 | tf_op jit(solution)/shard_map/ppermute | solution.py:80
  844.7 10.2 %collective-permute-start.53 = (bf16[2,2,64,320]{3,2,1,0:T(8,128)(2,1)S(1)}, bf16[2,2,64,320]{3,2,1,0:T(8,128)(2,1)S(1)}, u32[]{:S(2)}, u32[]{:S(2)}) collective-permute-start(bf16[2,2,64,320]{3,2,1,0:T(8,128)(2,1)S(1)} %dynamic-slice_bitcast_fusion.9), channel_id=1, source_target_pairs={{0,16},{1,17},{2,18},{3,19},{4,20},{5,21},{6,22},{7,23},{8,24},{9,... | collective-permute-start | bytes 491528 | tf_op jit(solution)/shard_map/ppermute | solution.py:80
  846.2 17.0 %collective-permute-start.50 = (bf16[2,2,64,1024]{3,2,0,1:T(8,128)(2,1)S(1)}, bf16[2,2,64,1024]{3,2,0,1:T(8,128)(2,1)S(1)}, u32[]{:S(2)}, u32[]{:S(2)}) collective-permute-start(bf16[2,2,64,1024]{3,2,0,1:T(8,128)(2,1)S(1)} %dynamic-slice_bitcast_fusion.4), channel_id=1, source_target_pairs={{0,2},{1,3},{2,0},{3,1},{4,6},{5,7},{6,4},{7,5},{8,10},{9,11},{10,... | collective-permute-start | bytes 1572872 | tf_op jit(solution)/shard_map/ppermute | solution.py:80
  855.0 5.4 collective-permute-start.54
  860.4 24.0 %collective-permute-start.55 = (bf16[64,320]{1,0:T(8,128)(2,1)S(1)}, bf16[64,320]{1,0:T(8,128)(2,1)S(1)}, u32[]{:S(2)}, u32[]{:S(2)}) collective-permute-start(bf16[64,320]{1,0:T(8,128)(2,1)S(1)} %fusion.176), channel_id=1, source_target_pairs={{0,4},{1,5},{2,6},{3,7},{4,0},{5,1},{6,2},{7,3},{8,12},{9,13},{10,... | collective-permute-start | bytes 122888 | tf_op jit(solution)/shard_map/ppermute | solution.py:80
  861.9 10.6 %collective-permute-start.48 = (bf16[2,64,1024]{2,1,0:T(8,128)(2,1)S(1)}, bf16[2,64,1024]{2,1,0:T(8,128)(2,1)S(1)}, u32[]{:S(2)}, u32[]{:S(2)}) collective-permute-start(bf16[2,64,1024]{2,1,0:T(8,128)(2,1)S(1)} %fusion.152), channel_id=1, source_target_pairs={{0,8},{1,9},{2,10},{3,11},{4,12},{5,13},{6,14},{7,15},{8,0},{9,1},... | collective-permute-start | bytes 786440 | tf_op jit(solution)/shard_map/ppermute | solution.py:80
  863.4 12.3 %collective-permute-start.51 = (bf16[2,64,1024]{2,1,0:T(8,128)(2,1)S(1)}, bf16[2,64,1024]{2,1,0:T(8,128)(2,1)S(1)}, u32[]{:S(2)}, u32[]{:S(2)}) collective-permute-start(bf16[2,64,1024]{2,1,0:T(8,128)(2,1)S(1)} %fusion.153), channel_id=1, source_target_pairs={{0,8},{1,9},{2,10},{3,11},{4,12},{5,13},{6,14},{7,15},{8,0},{9,1},... | collective-permute-start | bytes 786440 | tf_op jit(solution)/shard_map/ppermute | solution.py:80
  872.7 10.3 %collective-permute-start.49 = (bf16[64,1024]{1,0:T(8,128)(2,1)S(1)}, bf16[64,1024]{1,0:T(8,128)(2,1)S(1)}, u32[]{:S(2)}, u32[]{:S(2)}) collective-permute-start(bf16[64,1024]{1,0:T(8,128)(2,1)S(1)} %fusion.165), channel_id=1, source_target_pairs={{0,16},{1,17},{2,18},{3,19},{4,20},{5,21},{6,22},{7,23},{8,24},{9,... | collective-permute-start | bytes 393224 | tf_op jit(solution)/shard_map/ppermute | solution.py:80
  875.8 8.6 collective-permute-start.52
  889.7 5.3 collective-permute-start.58
  895.0 4.9 collective-permute-start.59
  899.9 4.9 collective-permute-start.60
  904.8 6.5 collective-permute-start.61
  906.3 17.6 %collective-permute-start.62 = (f32[16,4096]{1,0:T(8,128)}, f32[16,4096]{1,0:T(8,128)}, u32[]{:S(2)}, u32[]{:S(2)}) collective-permute-start(f32[16,4096]{1,0:T(8,128)} %slice.293), channel_id=1, source_target_pairs={{1,0},{2,1},{3,2},{4,3},{5,4},{6,5},{7,6},{8,7},{9,8},{10,9},{11,1... | collective-permute-start | bytes 786440 | tf_op jit(solution)/shard_map/ppermute | solution.py:73
  908.4 6.4 collective-permute-start.56
  (140 other events, 1851.2 us)
Sparse Core Ops, SparseCore 0:
  18.8 127.5 all-gather.5
  149.9 112.5 all-gather.3
  265.9 113.7 all-gather.7

commit v3 on v2

--- a/solution.py
+++ b/solution.py
@@ -321,7 +321,7 @@
     return pl.BlockSpec((1, rows, width), lambda i: (i + shift, 0, 0))
 
 
-def run(kernel, steps, ins, outs, shapes, scratch=()):
+def run(kernel, steps, ins, outs, shapes, scratch=(), micros=2):
     return pl.pallas_call(
         kernel,
         grid=(steps,),
@@ -330,6 +330,7 @@
         out_shape=[jax.ShapeDtypeStruct(*shape) for shape in shapes],
         scratch_shapes=list(scratch),
         compiler_params=pltpu.CompilerParams(vmem_limit_bytes=48 * 1024 * 1024),
+        cost_estimate=pl.CostEstimate(flops=micros * 10**9, transcendentals=0, bytes_accessed=micros * 3 * 10**6),
     )
 
 
@@ -376,12 +377,11 @@
     even_out = even_rows(w_out, count, lead, base)
     weights_x = lax.all_gather(even_in[:, E:], OWNERS, axis=0, tiled=True)
     weights_z = lax.all_gather(even_in[:, :E], OWNERS, axis=0, tiled=True)
-    tokens_out = split_rows(grad_out, mine, base)
-    weights_x, tokens_out = lax.optimization_barrier((weights_x, tokens_out))
-
     hidden_full = hidden.astype(f32)
     scale = lax.rsqrt(jnp.mean(hidden_full * hidden_full, axis=1, keepdims=True) + norm_eps)
     normed = (hidden_full * scale * gain_in[None, :]).astype(bf16)
+    tokens_out, features = split_rows(grad_out, mine, base), split_rows(normed, mine, base)
+    weights_x, tokens_out, features = lax.optimization_barrier((weights_x, tokens_out, features))
     proj_x = jnp.dot(normed, weights_x, preferred_element_type=f32).astype(bf16)
     conv_in = proj_x[:, :CW]
     raw = proj_x[:, CW:].astype(f32) + dt_bias[None, :]
@@ -433,6 +433,7 @@
         [lanes(T), lanes(T), planes(T, 8), planes(4, T), whole(T, T), whole(T, N), lanes(N), lanes(1), lanes(1)],
         [lanes(T), lanes(T), whole(T, 128)],
         [((T, E), f32), ((T, E), f32), ((T, 128), f32)],
+        micros=34,
     )(act, gate_raw, cols, rows, scores, queries, entered, mask_row, skip_row)
     root = lax.rsqrt(jnp.sum(squares, axis=1, keepdims=True) / active + norm_eps)
     mixed_low = (gated * root * gain_row).astype(bf16)
@@ -448,7 +449,6 @@
     grad_gate = grad_gate.astype(bf16)
     entering = (grad_gated * (gate_full * open_part) * mask_row * entry).astype(bf16)
     grad_entered = jnp.dot(queries.T, entering, preferred_element_type=f32)
-    features = split_rows(normed, mine, base)
     work_z = Reduce(features, grad_gate, mine, base, devices, (2048,))
     mixed_grad = tie(mixed_grad, out, work_z)
     out.advance()
@@ -463,6 +463,7 @@
         ],
         [lanes(T), whole(T, T), whole(T, N), whole(T, 128), lanes(8)],
         [((T, E), f32), ((T, T), f32), ((T, N), f32), ((T, 128), f32), ((8, E), f32)],
+        micros=45,
     )(mixed_grad, y, gate_raw, act, cols, rows, scores.T, entered, tok, mask_row, skip_row, gain_row)
     later = hand_on(grad_entered, carry, True)
     grad_x, grad_gate = tie((grad_x, grad_gate), out, work_z)
@@ -488,6 +489,7 @@
             [lanes(T), lanes(8), lanes(16), whole(T, 128), whole(T, N)],
             [((T, E // 2), bf16), ((8, E // 2), f32), ((16, E // 2), f32), ((T, 128), f32), ((T, N), f32)],
             scratch,
+            micros=18,
         )(grad_x, act, cols, keys, later, mask_row, proj_x, rim8, taps)
 
     def ends_of(edges):

time: 950 us -> 945 us (level)
  waiting for transfers between devices: 312 us -> 334 us
  starting transfers between devices: 105 us -> 92.5 us
    ppermute x50, waiting for transfers between devices: 138 us -> 152 us  [exchange(): lax.ppermute(value, OWNERS, [(i, i ^ 1 << bit) for i in range(devices)])]
    ppermute x50, starting transfers between devices: 77.8 us -> 66 us  [exchange(): lax.ppermute(value, OWNERS, [(i, i ^ 1 << bit) for i in range(devices)])]
    ppermute x6, waiting for transfers between devices: 2.22 us -> 13.3 us  [hand_on(): entered = entered + lax.ppermute(leaving, 'seq', route).astype(f32)]
  transfers between devices with their start and end apart: 66 -> 66, of which waited for: 33 -> 36; matrix products, arithmetic and copies ran while one was open for 27% -> 26% of each run, Pallas kernels for 11% -> 11%
where the time goes in v3:
time: 945 us; the launch traced here: 930 us
  waiting for transfers between devices  334 us (35%)
  matrix products  203 us (21%)
  Pallas kernels  118 us (12%)
  other arithmetic  103 us (11%)
  starting transfers between devices  92.5 us (10%)
  local copies, waits for them, and re-layouts  57.9 us (6%)
  between operations  21.8 us (2%)
    ppermute x50, waiting for transfers between devices, exchange(): lax.ppermute(value, OWNERS, [(i, i ^ 1 << bit) for i in range(devices)])  152 us
    all_gather x1, waiting for transfers between devices, local(): weights_x = lax.all_gather(even_in[:, E:], OWNERS, axis=0, tiled=True)  102 us
    dot_general x18, matrix products, product(): lax.dot_general(features, piece, (((0,), (0,)), ((), ())), preferred_elem...  68.4 us
    ppermute x50, starting transfers between devices, exchange(): lax.ppermute(value, OWNERS, [(i, i ^ 1 << bit) for i in range(devices)])  66 us
    all_gather x1, waiting for transfers between devices, local(): weights_z = lax.all_gather(even_in[:, :E], OWNERS, axis=0, tiled=True)  65.3 us
    pallas_call x1, Pallas kernels, local(): run(backward_kernel, PAIRS, [lanes(T), lanes(T), lanes(T), lanes(T), plan...  45.2 us
    pallas_call x2, Pallas kernels, inner_half(): run(partial(inner_kernel, 2 * shift), part, [lanes(T, shift), lanes(T, sh...  37.1 us
    pallas_call x1, Pallas kernels, local(): run(forward_kernel, PAIRS, [lanes(T), lanes(T), planes(T, 8), planes(4, T...  34.3 us
  transfers between devices with their start and end apart: 66, of which 36 were waited for; matrix products, arithmetic and copies ran while one was open for 26% of the time, Pallas kernels for 11%

profile of v3, /device:TPU:0, one launch (start us, length us, event | category | flops | bytes accessed | tf_op | source)
XLA Modules:
  0.0 929.8 jit_solution(6349241129366260795)
XLA Ops:
  21.4 6.3 collective-permute-start
  30.9 6.0 fusion.47
  36.9 5.7 fusion.52
  44.4 102.1 %all-gather.6.cloned.1.call-done = bf16[2048,4416]{1,0:T(8,128)(2,1)} async-done(((bf16[64,4416]{1,0:T(8,128)(2,1)}), bf16[2048,4416]{1,0:T(8,128)(2,1)}) %all-gather.6.cloned.1.call-update) | async-done | bytes 18087952 | tf_op jit(solution)/shard_map/all_gather | solution.py:378
  146.5 13.9 %convolution_convert_fusion.in_ref = bf16[512,4416]{1,0:T(8,128)(2,1)S(1)} fusion(bf16[2048,4416]{1,0:T(8,128)(2,1)} %all-gather.6.cloned.1.call-done, bf16[512,2048]{1,0:T(8,128)(2,1)S(1)} %copy-done.27, f32[2048]{0:T(1024)S(1)} %slice.205, f32[512]{0:T(512)S(1)} %get-tuple-element.217), kind=kOutput, calls=%fused_computation.46 | convolution fusion | flops 9267478528 | bytes 24717312 | tf_op jit(solution)/shard_map/dot_general | solution.py:385
  167.9 3.2 convolution_convert_fusion.2
  174.1 4.7 copy.124
  179.3 3.2 maximum_convert_fusion
  182.6 5.7 multiply_convert_fusion.x_ref
  190.8 6.4 fusion.24
  197.3 65.3 %all-gather.4.cloned.1.call-done = bf16[2048,4096]{1,0:T(8,128)(2,1)} async-done(((bf16[64,4096]{1,0:T(8,128)(2,1)}), bf16[2048,4096]{1,0:T(8,128)(2,1)}) %all-gather.4.cloned.1.call-update) | async-done | bytes 16777232 | tf_op jit(solution)/shard_map/all_gather | solution.py:379
  273.4 3.4 add_convert_fusion.10
  278.7 13.9 %convolution_convert_fusion.1.z_ref = bf16[512,4096]{1,0:T(8,128)(2,1)} fusion(bf16[2048,4096]{1,0:T(8,128)(2,1)} %all-gather.4.cloned.1.call-done, bf16[512,2048]{1,0:T(8,128)(2,1)S(1)} %copy-done.28, f32[2048]{0:T(1024)} %copy-done.96, f32[512]{0:T(512)} %copy-done.99), kind=kOutput, calls=%fused_computation.48 | convolution fusion | flops 8596226048 | bytes 23078912 | tf_op jit(solution)/shard_map/dot_general | solution.py:429
  297.1 34.3 %shard_map.262 = (f32[512,4096]{1,0:T(8,128)}, f32[512,4096]{1,0:T(8,128)}, f32[512,128]{1,0:T(8,128)S(1)}) custom-call(bf16[512,4352]{1,0:T(8,128)(2,1)} %copy-done.34, bf16[512,4096]{1,0:T(8,128)(2,1)} %convolution_convert_fusion.1.z_ref, f32[32,512,8]{2,1,0:T(8,128)} %bitcast.239, f32[32,4,512]{2,1,0:T(4,128)S(1)} %reshape.362.rows_ref, ...), custom_call_target="tpu_custom_call" | custom-call | flops 33999998976 | bytes 102000000 | tf_op jit(solution)/shard_map/pallas_call | solution.py:430
  331.6 4.9 multiply_convert_fusion.1
  336.5 4.4 convolution_convert_fusion.6
  340.9 14.9 %collective-permute-start.6 = (bf16[1024,2048]{1,0:T(8,128)(2,1)}, bf16[1024,2048]{1,0:T(8,128)(2,1)}, u32[]{:S(2)}, u32[]{:S(2)}) collective-permute-start(bf16[1024,2048]{1,0:T(8,128)(2,1)} %convolution_convert_fusion.6), channel_id=1, source_target_pairs={{0,1},{1,0},{2,3},{3,2},{4,5},{5,4},{6,7},{7,6},{8,9},{9,8},{10,11... | collective-permute-start | bytes 12582920 | tf_op jit(solution)/shard_map/ppermute | solution.py:80
  355.8 4.3 convolution_convert_fusion.5
  363.9 7.5 add_convert_fusion.3
  372.5 6.5 add_convert_fusion.2
  379.8 19.2 %multiply_reduce_fusion = (f32[512]{0:T(512)S(1)}, f32[512,4096]{1,0:T(8,128)}) fusion(f32[512,4096]{1,0:T(8,128)} %get-tuple-element.104, f32[4096]{0:T(1024)S(1)} %slice.229, bf16[512,2048]{1,0:T(8,128)(2,1)} %param.16, bf16[2048,4096]{1,0:T(8,128)(2,1)} %all-gather.8.cloned.1.call-done), kind=kOutput, calls=%fused_computation.39 | convolution fusion | flops 8596226048 | bytes 35670016 | tf_op jit(solution)/shard_map/dot_general | solution.py:443
  399.0 10.9 %add_convert_fusion.9 = (bf16[128,4096]{1,0:T(8,128)(2,1)S(1)}, f32[128,4096]{1,0:T(8,128)S(1)}) fusion(f32[4096]{0:T(1024)S(1)} %copy-done.94, bf16[512,4096]{1,0:T(8,128)(2,1)} %convolution_convert_fusion.1.z_ref, bf16[512,4096]{1,0:T(8,128)(2,1)} %convolution_convert_fusion.2, f32[4096]{0:T(1024)S(1)} %copy-done.92, ...), kind=kOutput, calls=%fused_computation.127 | convolution fusion | flops 567279616 | bytes 28495872 | tf_op jit(solution)/shard_map/dot_general | solution.py:451
  412.4 4.4 collective-permute-start.8
  419.6 11.3 %fusion.13 = bf16[512,4096]{1,0:T(8,128)(2,1)} fusion(bf16[512,4096]{1,0:T(8,128)(2,1)} %convolution_convert_fusion.1.z_ref, f32[512,4096]{1,0:T(8,128)} %get-tuple-element.110.y_ref, f32[4096]{0:T(1024)S(1)} %copy-done.92, f32[512,4096]{1,0:T(8,128)S(1)} %bitcast.238, f32[512]{0:T(512)S(1)} %fusion.195, f32[4096]{0:T(1024)S(1)} %slice.229, ...), kind=kLoop, calls=%fused_computation.28 | loop fusion | flops 33554432 | bytes 33591296 | tf_op jit(solution)/shard_map/convert_element_type | solution.py:449
  434.2 4.4 convolution_convert_fusion.4
  439.0 4.4 convolution_convert_fusion.3
  448.4 14.6 %collective-permute-done.8 = bf16[2,2,2,64,2048]{4,3,0,1,2:T(8,128)(2,1)} collective-permute-done((bf16[2,2,2,64,2048]{4,3,0,1,2:T(8,128)(2,1)}, bf16[2,2,2,64,2048]{4,3,0,1,2:T(8,128)(2,1)}, u32[]{:S(2)}, u32[]{:S(2)}) %collective-permute-start.8) | collective-permute-done | bytes 2097184 | tf_op jit(solution)/shard_map/ppermute | solution.py:80
  469.5 11.1 %collective-permute-done.18 = bf16[128,4096]{1,0:T(8,128)(2,1)S(1)} collective-permute-done((bf16[128,4096]{1,0:T(8,128)(2,1)S(1)}, bf16[128,4096]{1,0:T(8,128)(2,1)S(1)}, u32[]{:S(2)}, u32[]{:S(2)}) %collective-permute-start.18) | collective-permute-done | bytes 1048608 | tf_op jit(solution)/shard_map/ppermute | solution.py:343
  480.6 3.0 convert_add_fusion.15.later_ref
  483.6 4.6 add_convert_fusion.1
  488.2 6.1 add_convert_fusion
  497.9 3.7 collective-permute-start.13
  505.3 45.2 %shard_map.263 = (f32[512,4096]{1,0:T(8,128)}, f32[512,512]{1,0:T(8,128)S(1)}, f32[512,128]{1,0:T(8,128)S(1)}, f32[512,128]{1,0:T(8,128)S(1)}, f32[8,4096]{1,0:T(8,128)S(1)}) custom-call(f32[512,4096]{1,0:T(8,128)} %get-tuple-element.111.do_ref, f32[512,4096]{1,0:T(8,128)} %get-tuple-element.110.y_ref, bf16[512,4096]{1,0:T(8,128)(2,1)} %convolution_convert_fusion.1.z_ref, ...), custom_call_target="tpu_custom_call" | custom-call | flops 44999999488 | bytes 135000000 | tf_op jit(solution)/shard_map/pallas_call | solution.py:457
  560.9 9.2 collective-permute-done.14
  574.9 15.0 %fusion.226 = f32[512,2048]{1,0:T(8,128)} fusion(bf16[512,4096]{1,0:T(8,128)(2,1)} %fusion.13, bf16[2048,4096]{1,0:T(8,128)(2,1)} %all-gather.4.cloned.1.call-done), kind=kOutput, calls=%fused_computation.424 | convolution fusion | flops 8589934592 | bytes 25165824 | tf_op jit(solution)/shard_map/tc,dc->td/dot_general | solution.py:472
  595.6 9.1 collective-permute-done.19
  604.9 10.7 %collective-permute-done.20 = bf16[2,64,2048]{2,1,0:T(8,128)(2,1)S(1)} collective-permute-done((bf16[2,64,2048]{2,1,0:T(8,128)(2,1)S(1)}, bf16[2,64,2048]{2,1,0:T(8,128)(2,1)S(1)}, u32[]{:S(2)}, u32[]{:S(2)}) %collective-permute-start.20) | collective-permute-done | bytes 524320 | tf_op jit(solution)/shard_map/ppermute | solution.py:80
  630.5 18.5 %shard_map.264 = (bf16[512,2048]{1,0:T(8,128)(2,1)S(1)}, f32[8,2048]{1,0:T(8,128)S(1)}, f32[16,2048]{1,0:T(8,128)S(1)}, f32[512,128]{1,0:T(8,128)S(1)}, f32[512,128]{1,0:T(8,128)S(1)}) custom-call(f32[512,4096]{1,0:T(8,128)} %get-tuple-element.117.dx_ref, bf16[512,4352]{1,0:T(8,128)(2,1)} %copy-done.34, f32[32,512,8]{2,1,0:T(8,128)} %bitcast.241, ...), custom_call_target="tpu_custom_call" | custom-call | flops 17999998976 | bytes 54000000 | tf_op jit(solution)/shard_map/pallas_call | solution.py:482
  654.0 9.5 %fusion.20 = f32[512,2048]{1,0:T(8,128)} fusion(bf16[512,2048]{1,0:T(8,128)(2,1)S(1)} %fusion.178, bf16[2048,4416]{1,0:T(8,128)(2,1)} %all-gather.6.cloned.1.call-done), kind=kOutput, calls=%fused_computation.34 | convolution fusion | flops 4294967296 | bytes 14680064 | tf_op jit(solution)/shard_map/tc,dc->td/dot_general | solution.py:542
  674.6 18.5 %shard_map.265 = (bf16[512,2048]{1,0:T(8,128)(2,1)S(1)}, f32[8,2048]{1,0:T(8,128)S(1)}, f32[16,2048]{1,0:T(8,128)S(1)}, f32[512,128]{1,0:T(8,128)S(1)}, f32[512,128]{1,0:T(8,128)S(1)}) custom-call(f32[512,4096]{1,0:T(8,128)} %get-tuple-element.117.dx_ref, bf16[512,4352]{1,0:T(8,128)(2,1)} %copy-done.34, f32[32,512,8]{2,1,0:T(8,128)} %bitcast.242, ...), custom_call_target="tpu_custom_call" | custom-call | flops 17999998976 | bytes 54000000 | tf_op jit(solution)/shard_map/pallas_call | solution.py:482
  703.7 14.1 %collective-permute-done.35 = bf16[64,2048]{1,0:T(8,128)(2,1)S(1)} collective-permute-done((bf16[64,2048]{1,0:T(8,128)(2,1)S(1)}, bf16[64,2048]{1,0:T(8,128)(2,1)S(1)}, u32[]{:S(2)}, u32[]{:S(2)}) %collective-permute-start.35) | collective-permute-done | bytes 262176 | tf_op jit(solution)/shard_map/ppermute | solution.py:80
  718.7 3.9 collective-permute-done.36
  737.2 7.6 collective-permute-done.33
  748.0 4.0 convolution_convert_fusion.8
  758.1 7.0 collective-permute-done.40
  765.9 4.3 collective-permute-done.41
  774.7 5.0 add_convert_fusion.5
  779.7 4.7 add_convert_fusion.4
  784.4 13.4 %fusion.28 = bf16[512,2048]{1,0:T(8,128)(2,1)} fusion(bf16[512,2048]{1,0:T(8,128)(2,1)S(1)} %copy-done.29, bf16[512,4096]{1,0:T(8,128)(2,1)S(1)} %copy-done.50, bf16[2048,4096]{1,0:T(8,128)(2,1)} %all-gather.8.cloned.1.call-done), kind=kOutput, calls=%fused_computation.55 | convolution fusion | flops 8593080320 | bytes 25165824 | tf_op jit(solution)/shard_map/te,de->td/dot_general | solution.py:544
  797.9 12.1 %fusion.33 = (f32[2048]{0:T(1024)S(1)}, f32[512]{0:T(512)S(1)}, f32[512,2048]{1,0:T(8,128)S(1)}) fusion(bf16[512,2048]{1,0:T(8,128)(2,1)S(1)} %copy-done.29, f32[512]{0:T(512)S(1)} %copy-done.100, f32[2048]{0:T(1024)S(1)} %copy-done.97, f32[512,2048]{1,0:T(8,128)} %fusion.226, f32[512,2048]{1,0:T(8,128)} %fusion.20, bf16[512,2368]{1,0:T(8,128)(2,1)} %fusion.177, ...), kind=kOutput, calls=%fused_computation.60 | convolution fusion | flops 4975490560 | bytes 27152384 | tf_op jit(solution)/shard_map/tc,dc->td/dot_general | solution.py:543
  814.4 3.0 collective-permute-start.45
  817.5 3.3 fusion.30
  820.8 5.7 collective-permute-done.45
  829.9 6.3 collective-permute-done.42
  841.5 7.6 collective-permute-done.53
  850.1 4.9 collective-permute-done.54
  858.5 8.3 collective-permute-done.48
  866.9 3.1 collective-permute-done.51
  870.8 6.8 collective-permute-done.49
  884.4 4.4 collective-permute-done.58
  889.3 4.4 collective-permute-done.59
  893.8 4.8 collective-permute-done.60
  908.7 8.3 multiply_subtract_fusion.1
  917.8 4.1 multiply_subtract_fusion.2
  (558 shorter events, 206.6 us)
Async XLA Ops:
  7.2 139.3 %all-gather.6.cloned.1.call-start = ((), (), s32[]{:S(2)}) async-start(), calls=%async_computation.1 | async-start | bytes 18923520 | tf_op jit(solution)/shard_map/all_gather | solution.py:378
  10.2 4.5 collective-permute-start.1
  18.7 243.8 %all-gather.4.cloned.1.call-start = ((), (), s32[]{:S(2)}) async-start(), calls=%async_computation | async-start | bytes 17301504 | tf_op jit(solution)/shard_map/all_gather | solution.py:379
  20.7 359.1 %all-gather.8.cloned.1.call-start = ((), (), s32[]{:S(2)}) async-start(), calls=%async_computation.2 | async-start | bytes 17301504 | tf_op jit(solution)/shard_map/all_gather | solution.py:427
  21.4 22.0 %collective-permute-start = (bf16[16,4096]{1,0:T(8,128)(2,1)}, bf16[16,4096]{1,0:T(8,128)(2,1)}, u32[]{:S(2)}, u32[]{:S(2)}) collective-permute-start(bf16[16,4096]{1,0:T(8,128)(2,1)} %dynamic-slice_convert_fusion.17), channel_id=1, source_target_pairs={{0,1},{1,2},{2,3},{3,4},{4,5},{5,6},{6,7},{7,8},{8,9},{9,10},{10,1... | collective-permute-start | bytes 393224 | tf_op jit(solution)/shard_map/ppermute | solution.py:65
  164.1 15.2 %collective-permute-start.2 = (bf16[3,4352]{1,0:T(4,128)(2,1)S(1)}, bf16[3,4352]{1,0:T(4,128)(2,1)S(1)}, u32[]{:S(2)}, u32[]{:S(2)}) collective-permute-start(bf16[3,4352]{1,0:T(4,128)(2,1)S(1)} %slice.263), channel_id=1, source_target_pairs={{0,1},{1,2},{2,3},{4,5},{5,6},{6,7},{8,9},{9,10},{10,11},{12,13},{... | collective-permute-start | bytes 78344 | tf_op jit(solution)/shard_map/ppermute | solution.py:389
  264.7 4.6 collective-permute-start.3
  276.8 18.1 %collective-permute-start.5 = (bf16[128,4096]{1,0:T(8,128)(2,1)}, bf16[128,4096]{1,0:T(8,128)(2,1)}, u32[]{:S(2)}, u32[]{:S(2)}) collective-permute-start(bf16[128,4096]{1,0:T(8,128)(2,1)} %add_convert_fusion.10), channel_id=1, source_target_pairs={{2,3},{6,7},{10,11},{14,15},{18,19},{22,23},{26,27},{30,31}} | collective-permute-start | bytes 3145736 | tf_op jit(solution)/shard_map/ppermute | solution.py:343
  340.9 23.0 %collective-permute-start.6 = (bf16[1024,2048]{1,0:T(8,128)(2,1)}, bf16[1024,2048]{1,0:T(8,128)(2,1)}, u32[]{:S(2)}, u32[]{:S(2)}) collective-permute-start(bf16[1024,2048]{1,0:T(8,128)(2,1)} %convolution_convert_fusion.6), channel_id=1, source_target_pairs={{0,1},{1,0},{2,3},{3,2},{4,5},{5,4},{6,7},{7,6},{8,9},{9,8},{10,11... | collective-permute-start | bytes 12582920 | tf_op jit(solution)/shard_map/ppermute | solution.py:80
  360.1 12.3 %collective-permute-start.7 = (bf16[1024,2048]{1,0:T(8,128)(2,1)}, bf16[1024,2048]{1,0:T(8,128)(2,1)}, u32[]{:S(2)}, u32[]{:S(2)}) collective-permute-start(bf16[1024,2048]{1,0:T(8,128)(2,1)} %convolution_convert_fusion.5), channel_id=1, source_target_pairs={{0,1},{1,0},{2,3},{3,2},{4,5},{5,4},{6,7},{7,6},{8,9},{9,8},{10,11... | collective-permute-start | bytes 12582920 | tf_op jit(solution)/shard_map/ppermute | solution.py:80
  410.0 20.9 %collective-permute-start.16 = (bf16[128,4096]{1,0:T(8,128)(2,1)S(1)}, bf16[128,4096]{1,0:T(8,128)(2,1)S(1)}, u32[]{:S(2)}, u32[]{:S(2)}) collective-permute-start(bf16[128,4096]{1,0:T(8,128)(2,1)S(1)} %get-tuple-element.220), channel_id=1, source_target_pairs={{3,2},{7,6},{11,10},{15,14},{19,18},{23,22},{27,26},{31,30}} | collective-permute-start | bytes 3145736 | tf_op jit(solution)/shard_map/ppermute | solution.py:343
  412.4 50.6 %collective-permute-start.8 = (bf16[2,2,2,64,2048]{4,3,0,1,2:T(8,128)(2,1)}, bf16[2,2,2,64,2048]{4,3,0,1,2:T(8,128)(2,1)}, u32[]{:S(2)}, u32[]{:S(2)}) collective-permute-start(bf16[2,2,2,64,2048]{4,3,0,1,2:T(8,128)(2,1)} %copy_bitcast_fusion.3), channel_id=1, source_target_pairs={{0,2},{1,3},{2,0},{3,1},{4,6},{5,7},{6,4},{7,5},{8,10},{9,11},{10,... | collective-permute-start | bytes 6291464 | tf_op jit(solution)/shard_map/ppermute | solution.py:80
  418.3 48.7 %collective-permute-start.9 = (bf16[2,2,2,64,2048]{4,3,0,1,2:T(8,128)(2,1)}, bf16[2,2,2,64,2048]{4,3,0,1,2:T(8,128)(2,1)}, u32[]{:S(2)}, u32[]{:S(2)}) collective-permute-start(bf16[2,2,2,64,2048]{4,3,0,1,2:T(8,128)(2,1)} %copy_bitcast_fusion.2), channel_id=1, source_target_pairs={{0,4},{1,5},{2,6},{3,7},{4,0},{5,1},{6,2},{7,3},{8,12},{9,13},{10,... | collective-permute-start | bytes 6291464 | tf_op jit(solution)/shard_map/ppermute | solution.py:80
  432.2 12.2 %collective-permute-start.17 = (bf16[128,4096]{1,0:T(8,128)(2,1)}, bf16[128,4096]{1,0:T(8,128)(2,1)}, u32[]{:S(2)}, u32[]{:S(2)}) collective-permute-start(bf16[128,4096]{1,0:T(8,128)(2,1)} %fusion.60), channel_id=1, source_target_pairs={{2,1},{6,5},{10,9},{14,13},{18,17},{22,21},{26,25},{30,29}} | collective-permute-start | bytes 3145736 | tf_op jit(solution)/shard_map/ppermute | solution.py:343
  438.6 45.0 %collective-permute-start.10 = (bf16[1024,2048]{1,0:T(8,128)(2,1)}, bf16[1024,2048]{1,0:T(8,128)(2,1)}, u32[]{:S(2)}, u32[]{:S(2)}) collective-permute-start(bf16[1024,2048]{1,0:T(8,128)(2,1)} %convolution_convert_fusion.4), channel_id=1, source_target_pairs={{0,1},{1,0},{2,3},{3,2},{4,5},{5,4},{6,7},{7,6},{8,9},{9,8},{10,11... | collective-permute-start | bytes 12582920 | tf_op jit(solution)/shard_map/ppermute | solution.py:80
  443.3 44.9 %collective-permute-start.11 = (bf16[1024,2048]{1,0:T(8,128)(2,1)}, bf16[1024,2048]{1,0:T(8,128)(2,1)}, u32[]{:S(2)}, u32[]{:S(2)}) collective-permute-start(bf16[1024,2048]{1,0:T(8,128)(2,1)} %convolution_convert_fusion.3), channel_id=1, source_target_pairs={{0,1},{1,0},{2,3},{3,2},{4,5},{5,4},{6,7},{7,6},{8,9},{9,8},{10,11... | collective-permute-start | bytes 12582920 | tf_op jit(solution)/shard_map/ppermute | solution.py:80
  446.8 33.8 %collective-permute-start.18 = (bf16[128,4096]{1,0:T(8,128)(2,1)S(1)}, bf16[128,4096]{1,0:T(8,128)(2,1)S(1)}, u32[]{:S(2)}, u32[]{:S(2)}) collective-permute-start(bf16[128,4096]{1,0:T(8,128)(2,1)S(1)} %add_convert_fusion.8), channel_id=1, source_target_pairs={{1,0},{5,4},{9,8},{13,12},{17,16},{21,20},{25,24},{29,28}} | collective-permute-start | bytes 3145736 | tf_op jit(solution)/shard_map/ppermute | solution.py:343
  495.5 62.0 %collective-permute-start.12 = (bf16[2,2,64,2048]{3,2,0,1:T(8,128)(2,1)}, bf16[2,2,64,2048]{3,2,0,1:T(8,128)(2,1)}, u32[]{:S(2)}, u32[]{:S(2)}) collective-permute-start(bf16[2,2,64,2048]{3,2,0,1:T(8,128)(2,1)} %dynamic-slice_bitcast_fusion.3), channel_id=1, source_target_pairs={{0,4},{1,5},{2,6},{3,7},{4,0},{5,1},{6,2},{7,3},{8,12},{9,13},{10,... | collective-permute-start | bytes 3145736 | tf_op jit(solution)/shard_map/ppermute | solution.py:80
  497.9 61.2 %collective-permute-start.13 = (bf16[2,2,64,2048]{3,2,0,1:T(8,128)(2,1)}, bf16[2,2,64,2048]{3,2,0,1:T(8,128)(2,1)}, u32[]{:S(2)}, u32[]{:S(2)}) collective-permute-start(bf16[2,2,64,2048]{3,2,0,1:T(8,128)(2,1)} %dynamic-slice_bitcast_fusion.2), channel_id=1, source_target_pairs={{0,2},{1,3},{2,0},{3,1},{4,6},{5,7},{6,4},{7,5},{8,10},{9,11},{10,... | collective-permute-start | bytes 3145736 | tf_op jit(solution)/shard_map/ppermute | solution.py:80
  503.1 67.0 %collective-permute-start.14 = (bf16[2,2,2,64,2048]{4,3,0,1,2:T(8,128)(2,1)}, bf16[2,2,2,64,2048]{4,3,0,1,2:T(8,128)(2,1)}, u32[]{:S(2)}, u32[]{:S(2)}) collective-permute-start(bf16[2,2,2,64,2048]{4,3,0,1,2:T(8,128)(2,1)} %copy_bitcast_fusion.1), channel_id=1, source_target_pairs={{0,2},{1,3},{2,0},{3,1},{4,6},{5,7},{6,4},{7,5},{8,10},{9,11},{10,... | collective-permute-start | bytes 6291464 | tf_op jit(solution)/shard_map/ppermute | solution.py:80
  504.6 67.9 %collective-permute-start.15 = (bf16[2,2,2,64,2048]{4,3,0,1,2:T(8,128)(2,1)}, bf16[2,2,2,64,2048]{4,3,0,1,2:T(8,128)(2,1)}, u32[]{:S(2)}, u32[]{:S(2)}) collective-permute-start(bf16[2,2,2,64,2048]{4,3,0,1,2:T(8,128)(2,1)} %copy_bitcast_fusion), channel_id=1, source_target_pairs={{0,4},{1,5},{2,6},{3,7},{4,0},{5,1},{6,2},{7,3},{8,12},{9,13},{10,... | collective-permute-start | bytes 6291464 | tf_op jit(solution)/shard_map/ppermute | solution.py:80
  589.9 14.9 %collective-permute-start.19 = (bf16[2,64,2048]{2,1,0:T(8,128)(2,1)S(1)}, bf16[2,64,2048]{2,1,0:T(8,128)(2,1)S(1)}, u32[]{:S(2)}, u32[]{:S(2)}) collective-permute-start(bf16[2,64,2048]{2,1,0:T(8,128)(2,1)S(1)} %fusion.120), channel_id=1, source_target_pairs={{0,8},{1,9},{2,10},{3,11},{4,12},{5,13},{6,14},{7,15},{8,0},{9,1},... | collective-permute-start | bytes 1572872 | tf_op jit(solution)/shard_map/ppermute | solution.py:80
  590.6 24.9 %collective-permute-start.20 = (bf16[2,64,2048]{2,1,0:T(8,128)(2,1)S(1)}, bf16[2,64,2048]{2,1,0:T(8,128)(2,1)S(1)}, u32[]{:S(2)}, u32[]{:S(2)}) collective-permute-start(bf16[2,64,2048]{2,1,0:T(8,128)(2,1)S(1)} %fusion.121), channel_id=1, source_target_pairs={{0,8},{1,9},{2,10},{3,11},{4,12},{5,13},{6,14},{7,15},{8,0},{9,1},... | collective-permute-start | bytes 1572872 | tf_op jit(solution)/shard_map/ppermute | solution.py:80
  592.2 25.1 %collective-permute-start.21 = (bf16[2,2,64,2048]{3,2,0,1:T(8,128)(2,1)S(1)}, bf16[2,2,64,2048]{3,2,0,1:T(8,128)(2,1)S(1)}, u32[]{:S(2)}, u32[]{:S(2)}) collective-permute-start(bf16[2,2,64,2048]{3,2,0,1:T(8,128)(2,1)S(1)} %dynamic-slice_bitcast_fusion.1), channel_id=1, source_target_pairs={{0,4},{1,5},{2,6},{3,7},{4,0},{5,1},{6,2},{7,3},{8,12},{9,13},{10,... | collective-permute-start | bytes 3145736 | tf_op jit(solution)/shard_map/ppermute | solution.py:80
  593.1 25.9 %collective-permute-start.22 = (bf16[2,2,64,2048]{3,2,0,1:T(8,128)(2,1)S(1)}, bf16[2,2,64,2048]{3,2,0,1:T(8,128)(2,1)S(1)}, u32[]{:S(2)}, u32[]{:S(2)}) collective-permute-start(bf16[2,2,64,2048]{3,2,0,1:T(8,128)(2,1)S(1)} %dynamic-slice_bitcast_fusion), channel_id=1, source_target_pairs={{0,2},{1,3},{2,0},{3,1},{4,6},{5,7},{6,4},{7,5},{8,10},{9,11},{10,... | collective-permute-start | bytes 3145736 | tf_op jit(solution)/shard_map/ppermute | solution.py:80
  622.8 43.7 %collective-permute-start.23 = (bf16[64,2048]{1,0:T(8,128)(2,1)S(1)}, bf16[64,2048]{1,0:T(8,128)(2,1)S(1)}, u32[]{:S(2)}, u32[]{:S(2)}) collective-permute-start(bf16[64,2048]{1,0:T(8,128)(2,1)S(1)} %fusion.146), channel_id=1, source_target_pairs={{0,16},{1,17},{2,18},{3,19},{4,20},{5,21},{6,22},{7,23},{8,24},{9,... | collective-permute-start | bytes 786440 | tf_op jit(solution)/shard_map/ppermute | solution.py:80
  625.5 41.1 %collective-permute-start.24 = (bf16[64,2048]{1,0:T(8,128)(2,1)S(1)}, bf16[64,2048]{1,0:T(8,128)(2,1)S(1)}, u32[]{:S(2)}, u32[]{:S(2)}) collective-permute-start(bf16[64,2048]{1,0:T(8,128)(2,1)S(1)} %fusion.147), channel_id=1, source_target_pairs={{0,16},{1,17},{2,18},{3,19},{4,20},{5,21},{6,22},{7,23},{8,24},{9,... | collective-permute-start | bytes 786440 | tf_op jit(solution)/shard_map/ppermute | solution.py:80
  628.2 39.3 %collective-permute-start.25 = (bf16[2,64,2048]{2,1,0:T(8,128)(2,1)S(1)}, bf16[2,64,2048]{2,1,0:T(8,128)(2,1)S(1)}, u32[]{:S(2)}, u32[]{:S(2)}) collective-permute-start(bf16[2,64,2048]{2,1,0:T(8,128)(2,1)S(1)} %fusion.122), channel_id=1, source_target_pairs={{0,8},{1,9},{2,10},{3,11},{4,12},{5,13},{6,14},{7,15},{8,0},{9,1},... | collective-permute-start | bytes 1572872 | tf_op jit(solution)/shard_map/ppermute | solution.py:80
  649.1 3.6 collective-permute-start.27
  651.2 17.2 %collective-permute-start.26 = (bf16[2,64,2048]{2,1,0:T(8,128)(2,1)S(1)}, bf16[2,64,2048]{2,1,0:T(8,128)(2,1)S(1)}, u32[]{:S(2)}, u32[]{:S(2)}) collective-permute-start(bf16[2,64,2048]{2,1,0:T(8,128)(2,1)S(1)} %fusion.123), channel_id=1, source_target_pairs={{0,8},{1,9},{2,10},{3,11},{4,12},{5,13},{6,14},{7,15},{8,0},{9,1},... | collective-permute-start | bytes 1572872 | tf_op jit(solution)/shard_map/ppermute | solution.py:80
  663.5 5.5 collective-permute-start.28
  666.5 5.5 collective-permute-start.29
  694.7 28.7 %collective-permute-start.30 = (bf16[2,2,2,64,1024]{4,3,0,1,2:T(8,128)(2,1)S(1)}, bf16[2,2,2,64,1024]{4,3,0,1,2:T(8,128)(2,1)S(1)}, u32[]{:S(2)}, u32[]{:S(2)}) collective-permute-start(bf16[2,2,2,64,1024]{4,3,0,1,2:T(8,128)(2,1)S(1)} %copy_bitcast_fusion.7), channel_id=1, source_target_pairs={{0,2},{1,3},{2,0},{3,1},{4,6},{5,7},{6,4},{7,5},{8,10},{9,11},{10,... | collective-permute-start | bytes 3145736 | tf_op jit(solution)/shard_map/ppermute | solution.py:80
  696.1 27.8 %collective-permute-start.31 = (bf16[2,2,2,64,1024]{4,3,0,1,2:T(8,128)(2,1)S(1)}, bf16[2,2,2,64,1024]{4,3,0,1,2:T(8,128)(2,1)S(1)}, u32[]{:S(2)}, u32[]{:S(2)}) collective-permute-start(bf16[2,2,2,64,1024]{4,3,0,1,2:T(8,128)(2,1)S(1)} %copy_bitcast_fusion.6), channel_id=1, source_target_pairs={{0,4},{1,5},{2,6},{3,7},{4,0},{5,1},{6,2},{7,3},{8,12},{9,13},{10,... | collective-permute-start | bytes 3145736 | tf_op jit(solution)/shard_map/ppermute | solution.py:80
  696.9 20.9 %collective-permute-start.35 = (bf16[64,2048]{1,0:T(8,128)(2,1)S(1)}, bf16[64,2048]{1,0:T(8,128)(2,1)S(1)}, u32[]{:S(2)}, u32[]{:S(2)}) collective-permute-start(bf16[64,2048]{1,0:T(8,128)(2,1)S(1)} %fusion.148), channel_id=1, source_target_pairs={{0,16},{1,17},{2,18},{3,19},{4,20},{5,21},{6,22},{7,23},{8,24},{9,... | collective-permute-start | bytes 786440 | tf_op jit(solution)/shard_map/ppermute | solution.py:80
  698.9 23.7 %collective-permute-start.36 = (bf16[64,2048]{1,0:T(8,128)(2,1)S(1)}, bf16[64,2048]{1,0:T(8,128)(2,1)S(1)}, u32[]{:S(2)}, u32[]{:S(2)}) collective-permute-start(bf16[64,2048]{1,0:T(8,128)(2,1)S(1)} %fusion.149), channel_id=1, source_target_pairs={{0,16},{1,17},{2,18},{3,19},{4,20},{5,21},{6,22},{7,23},{8,24},{9,... | collective-permute-start | bytes 786440 | tf_op jit(solution)/shard_map/ppermute | solution.py:80
  727.3 8.4 collective-permute-start.32
  729.8 15.0 %collective-permute-start.33 = (bf16[2,2,64,1024]{3,2,0,1:T(8,128)(2,1)}, bf16[2,2,64,1024]{3,2,0,1:T(8,128)(2,1)}, u32[]{:S(2)}, u32[]{:S(2)}) collective-permute-start(bf16[2,2,64,1024]{3,2,0,1:T(8,128)(2,1)} %dynamic-slice_bitcast_fusion.7), channel_id=1, source_target_pairs={{0,4},{1,5},{2,6},{3,7},{4,0},{5,1},{6,2},{7,3},{8,12},{9,13},{10,... | collective-permute-start | bytes 1572872 | tf_op jit(solution)/shard_map/ppermute | solution.py:80
  731.9 14.9 %collective-permute-start.34 = (bf16[2,2,64,1024]{3,2,0,1:T(8,128)(2,1)}, bf16[2,2,64,1024]{3,2,0,1:T(8,128)(2,1)S(1)}, u32[]{:S(2)}, u32[]{:S(2)}) collective-permute-start(bf16[2,2,64,1024]{3,2,0,1:T(8,128)(2,1)} %dynamic-slice_bitcast_fusion.6), channel_id=1, source_target_pairs={{0,2},{1,3},{2,0},{3,1},{4,6},{5,7},{6,4},{7,5},{8,10},{9,11},{10,... | collective-permute-start | bytes 1572872 | tf_op jit(solution)/shard_map/ppermute | solution.py:80
  752.0 22.7 %collective-permute-start.37 = (bf16[1024,1024]{1,0:T(8,128)(2,1)}, bf16[1024,1024]{1,0:T(8,128)(2,1)}, u32[]{:S(2)}, u32[]{:S(2)}) collective-permute-start(bf16[1024,1024]{1,0:T(8,128)(2,1)} %convolution_convert_fusion.8), channel_id=1, source_target_pairs={{0,1},{1,0},{2,3},{3,2},{4,5},{5,4},{6,7},{7,6},{8,9},{9,8},{10,11... | collective-permute-start | bytes 6291464 | tf_op jit(solution)/shard_map/ppermute | solution.py:80
  754.6 25.1 %collective-permute-start.38 = (bf16[1024,1024]{1,0:T(8,128)(2,1)}, bf16[1024,1024]{1,0:T(8,128)(2,1)}, u32[]{:S(2)}, u32[]{:S(2)}) collective-permute-start(bf16[1024,1024]{1,0:T(8,128)(2,1)} %convolution_convert_fusion.7), channel_id=1, source_target_pairs={{0,1},{1,0},{2,3},{3,2},{4,5},{5,4},{6,7},{7,6},{8,9},{9,8},{10,11... | collective-permute-start | bytes 6291464 | tf_op jit(solution)/shard_map/ppermute | solution.py:80
  755.7 15.4 %collective-permute-start.39 = (bf16[1024,320]{0,1:T(8,128)(2,1)S(1)}, bf16[1024,320]{0,1:T(8,128)(2,1)S(1)}, u32[]{:S(2)}, u32[]{:S(2)}) collective-permute-start(bf16[1024,320]{0,1:T(8,128)(2,1)S(1)} %convolution_convert_fusion.11), channel_id=1, source_target_pairs={{0,1},{1,0},{2,3},{3,2},{4,5},{5,4},{6,7},{7,6},{8,9},{9,8},{10,11... | collective-permute-start | bytes 1966088 | tf_op jit(solution)/shard_map/ppermute | solution.py:80
  755.8 9.2 collective-permute-start.40
  756.0 14.3 %collective-permute-start.41 = (bf16[2,64,1024]{2,1,0:T(8,128)(2,1)S(1)}, bf16[2,64,1024]{2,1,0:T(8,128)(2,1)S(1)}, u32[]{:S(2)}, u32[]{:S(2)}) collective-permute-start(bf16[2,64,1024]{2,1,0:T(8,128)(2,1)S(1)} %fusion.151), channel_id=1, source_target_pairs={{0,8},{1,9},{2,10},{3,11},{4,12},{5,13},{6,14},{7,15},{8,0},{9,1},... | collective-permute-start | bytes 786440 | tf_op jit(solution)/shard_map/ppermute | solution.py:80
  811.5 24.7 %collective-permute-start.42 = (bf16[2,2,2,64,1024]{4,3,0,1,2:T(8,128)(2,1)S(1)}, bf16[2,2,2,64,1024]{4,3,0,1,2:T(8,128)(2,1)S(1)}, u32[]{:S(2)}, u32[]{:S(2)}) collective-permute-start(bf16[2,2,2,64,1024]{4,3,0,1,2:T(8,128)(2,1)S(1)} %copy_bitcast_fusion.5), channel_id=1, source_target_pairs={{0,2},{1,3},{2,0},{3,1},{4,6},{5,7},{6,4},{7,5},{8,10},{9,11},{10,... | collective-permute-start | bytes 3145736 | tf_op jit(solution)/shard_map/ppermute | solution.py:80
  813.0 24.5 %collective-permute-start.43 = (bf16[2,2,2,64,1024]{4,3,0,1,2:T(8,128)(2,1)S(1)}, bf16[2,2,2,64,1024]{4,3,0,1,2:T(8,128)(2,1)S(1)}, u32[]{:S(2)}, u32[]{:S(2)}) collective-permute-start(bf16[2,2,2,64,1024]{4,3,0,1,2:T(8,128)(2,1)S(1)} %copy_bitcast_fusion.4), channel_id=1, source_target_pairs={{0,4},{1,5},{2,6},{3,7},{4,0},{5,1},{6,2},{7,3},{8,12},{9,13},{10,... | collective-permute-start | bytes 3145736 | tf_op jit(solution)/shard_map/ppermute | solution.py:80
  814.0 15.8 %collective-permute-start.44 = (bf16[2,2,2,64,320]{4,3,2,1,0:T(8,128)(2,1)S(1)}, bf16[2,2,2,64,320]{4,3,2,1,0:T(8,128)(2,1)S(1)}, u32[]{:S(2)}, u32[]{:S(2)}) collective-permute-start(bf16[2,2,2,64,320]{4,3,2,1,0:T(8,128)(2,1)S(1)} %dynamic-slice_bitcast_fusion.8), channel_id=1, source_target_pairs={{0,8},{1,9},{2,10},{3,11},{4,12},{5,13},{6,14},{7,15},{8,0},{9,1},... | collective-permute-start | bytes 983048 | tf_op jit(solution)/shard_map/ppermute | solution.py:80
  814.4 12.1 %collective-permute-start.45 = (bf16[64,1024]{1,0:T(8,128)(2,1)S(1)}, bf16[64,1024]{1,0:T(8,128)(2,1)S(1)}, u32[]{:S(2)}, u32[]{:S(2)}) collective-permute-start(bf16[64,1024]{1,0:T(8,128)(2,1)S(1)} %fusion.163), channel_id=1, source_target_pairs={{0,16},{1,17},{2,18},{3,19},{4,20},{5,21},{6,22},{7,23},{8,24},{9,... | collective-permute-start | bytes 393224 | tf_op jit(solution)/shard_map/ppermute | solution.py:80
  817.4 10.5 %collective-permute-start.46 = (bf16[64,1024]{1,0:T(8,128)(2,1)S(1)}, bf16[64,1024]{1,0:T(8,128)(2,1)S(1)}, u32[]{:S(2)}, u32[]{:S(2)}) collective-permute-start(bf16[64,1024]{1,0:T(8,128)(2,1)S(1)} %fusion.164), channel_id=1, source_target_pairs={{0,16},{1,17},{2,18},{3,19},{4,20},{5,21},{6,22},{7,23},{8,24},{9,... | collective-permute-start | bytes 393224 | tf_op jit(solution)/shard_map/ppermute | solution.py:80
  838.0 17.9 %collective-permute-start.47 = (bf16[2,2,64,1024]{3,2,0,1:T(8,128)(2,1)S(1)}, bf16[2,2,64,1024]{3,2,0,1:T(8,128)(2,1)S(1)}, u32[]{:S(2)}, u32[]{:S(2)}) collective-permute-start(bf16[2,2,64,1024]{3,2,0,1:T(8,128)(2,1)S(1)} %dynamic-slice_bitcast_fusion.5), channel_id=1, source_target_pairs={{0,4},{1,5},{2,6},{3,7},{4,0},{5,1},{6,2},{7,3},{8,12},{9,13},{10,... | collective-permute-start | bytes 1572872 | tf_op jit(solution)/shard_map/ppermute | solution.py:80
  838.9 10.2 %collective-permute-start.53 = (bf16[2,2,64,320]{3,2,1,0:T(8,128)(2,1)S(1)}, bf16[2,2,64,320]{3,2,1,0:T(8,128)(2,1)S(1)}, u32[]{:S(2)}, u32[]{:S(2)}) collective-permute-start(bf16[2,2,64,320]{3,2,1,0:T(8,128)(2,1)S(1)} %dynamic-slice_bitcast_fusion.9), channel_id=1, source_target_pairs={{0,16},{1,17},{2,18},{3,19},{4,20},{5,21},{6,22},{7,23},{8,24},{9,... | collective-permute-start | bytes 491528 | tf_op jit(solution)/shard_map/ppermute | solution.py:80
  840.7 16.6 %collective-permute-start.50 = (bf16[2,2,64,1024]{3,2,0,1:T(8,128)(2,1)S(1)}, bf16[2,2,64,1024]{3,2,0,1:T(8,128)(2,1)S(1)}, u32[]{:S(2)}, u32[]{:S(2)}) collective-permute-start(bf16[2,2,64,1024]{3,2,0,1:T(8,128)(2,1)S(1)} %dynamic-slice_bitcast_fusion.4), channel_id=1, source_target_pairs={{0,2},{1,3},{2,0},{3,1},{4,6},{5,7},{6,4},{7,5},{8,10},{9,11},{10,... | collective-permute-start | bytes 1572872 | tf_op jit(solution)/shard_map/ppermute | solution.py:80
  849.2 5.8 collective-permute-start.54
  855.0 24.0 %collective-permute-start.55 = (bf16[64,320]{1,0:T(8,128)(2,1)S(1)}, bf16[64,320]{1,0:T(8,128)(2,1)S(1)}, u32[]{:S(2)}, u32[]{:S(2)}) collective-permute-start(bf16[64,320]{1,0:T(8,128)(2,1)S(1)} %fusion.176), channel_id=1, source_target_pairs={{0,4},{1,5},{2,6},{3,7},{4,0},{5,1},{6,2},{7,3},{8,12},{9,13},{10,... | collective-permute-start | bytes 122888 | tf_op jit(solution)/shard_map/ppermute | solution.py:80
  856.1 10.6 %collective-permute-start.48 = (bf16[2,64,1024]{2,1,0:T(8,128)(2,1)S(1)}, bf16[2,64,1024]{2,1,0:T(8,128)(2,1)S(1)}, u32[]{:S(2)}, u32[]{:S(2)}) collective-permute-start(bf16[2,64,1024]{2,1,0:T(8,128)(2,1)S(1)} %fusion.152), channel_id=1, source_target_pairs={{0,8},{1,9},{2,10},{3,11},{4,12},{5,13},{6,14},{7,15},{8,0},{9,1},... | collective-permute-start | bytes 786440 | tf_op jit(solution)/shard_map/ppermute | solution.py:80
  857.5 12.5 %collective-permute-start.51 = (bf16[2,64,1024]{2,1,0:T(8,128)(2,1)S(1)}, bf16[2,64,1024]{2,1,0:T(8,128)(2,1)S(1)}, u32[]{:S(2)}, u32[]{:S(2)}) collective-permute-start(bf16[2,64,1024]{2,1,0:T(8,128)(2,1)S(1)} %fusion.153), channel_id=1, source_target_pairs={{0,8},{1,9},{2,10},{3,11},{4,12},{5,13},{6,14},{7,15},{8,0},{9,1},... | collective-permute-start | bytes 786440 | tf_op jit(solution)/shard_map/ppermute | solution.py:80
  866.8 10.7 %collective-permute-start.49 = (bf16[64,1024]{1,0:T(8,128)(2,1)S(1)}, bf16[64,1024]{1,0:T(8,128)(2,1)S(1)}, u32[]{:S(2)}, u32[]{:S(2)}) collective-permute-start(bf16[64,1024]{1,0:T(8,128)(2,1)S(1)} %fusion.165), channel_id=1, source_target_pairs={{0,16},{1,17},{2,18},{3,19},{4,20},{5,21},{6,22},{7,23},{8,24},{9,... | collective-permute-start | bytes 393224 | tf_op jit(solution)/shard_map/ppermute | solution.py:80
  870.1 8.9 collective-permute-start.52
  883.6 5.3 collective-permute-start.58
  888.8 4.9 collective-permute-start.59
  893.7 4.9 collective-permute-start.60
  898.6 6.5 collective-permute-start.61
  899.7 18.1 %collective-permute-start.62 = (f32[16,4096]{1,0:T(8,128)}, f32[16,4096]{1,0:T(8,128)}, u32[]{:S(2)}, u32[]{:S(2)}) collective-permute-start(f32[16,4096]{1,0:T(8,128)} %slice.291), channel_id=1, source_target_pairs={{1,0},{2,1},{3,2},{4,3},{5,4},{6,5},{7,6},{8,7},{9,8},{10,9},{11,1... | collective-permute-start | bytes 786440 | tf_op jit(solution)/shard_map/ppermute | solution.py:73
  901.8 6.9 collective-permute-start.56
  (125 other events, 2083.6 us)
Sparse Core Ops, SparseCore 0:
  18.8 127.6 all-gather.5
  150.0 112.5 all-gather.3
  266.0 113.6 all-gather.7
